TPU v7x, 32 devices: a whole 2x2x4 slice. The times are simulated.
32 devices in a mesh: areal: 8 (over y, x, core), layer: 4 (over z).
Axes of the slice: x: 2, y: 2, z: 4, core: 2. Of those that a mesh axis runs over, the one named last changes fastest.
Arguments:
- pressure: float32 [16, 128, 128], P('layer', 'areal'), may hold values from -4 to 4
- pressure_old: float32 [16, 128, 128], P('layer', 'areal'), may hold values from -4 to 4
- saturations: float32 [2, 16, 128, 128], P(None, 'layer', 'areal'), may hold values from 0.05 to 0.45
- saturations_old: float32 [2, 16, 128, 128], P(None, 'layer', 'areal'), may hold values from 0.05 to 0.45
- pore_volume: float32 [16, 128, 128], P('layer', 'areal'), may hold values from 4 to 16
- trans: float32 [3, 16, 128, 128], P(None, 'layer', 'areal'), may hold values from 0.05 to 0.5
- upwind: int32 [3, 16, 128, 128], P(None, 'layer', 'areal'), may hold values from 0 to 1
- active: int32 [16, 128, 128], P('layer', 'areal'), may hold values 0 or 1
- fault_cell: int32 [4, 8, 8, 64], P('layer', 'areal'), may hold values from 0 to 8191, as said below
- fault_live: int32 [4, 8, 8, 64], P('layer', 'areal'), may hold values from 0 to 1, as said below
- fault_up: int32 [4, 8, 8, 64], P('layer', 'areal'), may hold values from 0 to 1, as said below
- fault_trans: float32 [4, 8, 8, 64], P('layer', 'areal'), may hold values from 0.05 to 0.5, as said below
Outputs:
- residual: float32 [3, 16, 128, 128], P(None, 'layer', 'areal')
- update: float32 [3, 16, 128, 128], P(None, 'layer', 'areal')
Inputs may be any that keep to these rules, and one draw needn't show every extreme that they name: `fault_cell`: slot (l, i, j, s) and slot (l, j, i, s) are the same fault face; entries are cell numbers of the block. fault_live[l, i, j, s] = fault_live[l, j, i, s]; zero where i = j; the live slots of a pair come first; in every layer index some pairs have all 64 slots live. fault_up[l, i, j, s] = 1 - fault_up[l, j, i, s] where i != j. fault_trans[l, i, j, s] = fault_trans[l, j, i, s].
All inputs are finite; a program needn't handle non-finite values. No bound on the sum of `active` on one device may be relied on, other than what follows from the above.
Results may differ from a plain program's by a relative error of at most 0.0003.
Values sent between devices are 32-bit elements; how exact they have to be, the bound alone decides.
No kernel may reach another device: no remote copies, remote signals or barrier semaphores. Data moves between devices by JAX's collectives and lax.ppermute only.
A program may use at most 64 MiB of HBM per device.

v0:
```python
import functools

import jax
import jax.numpy as jnp
from jax import lax
from jax.experimental import pallas as pl
from jax.experimental.pallas import tpu as pltpu
from jax.sharding import PartitionSpec as P

SWEEPS = 4

COMPRESS = (0.01, 0.02, 0.05)
DAMPING = 0.7

F32 = jnp.float32
BF16 = jnp.bfloat16


class Sizes:
    def __init__(self, areal, layer, cells, cap):
        self.areal = areal
        self.layer = layer
        self.lz, self.ry, self.nx = cells
        self.cap = cap
        self.rows = self.lz * self.ry
        self.slots = areal * cap

    def block_rows(self, y_fields, slot_fields):
        used = y_fields * self.lz + slot_fields
        return -(-used // 8) * 8


def iota(shape, dim):
    return lax.broadcasted_iota(jnp.int32, shape, dim)


def layers_of(sz, ref, *lead):
    return [ref[lead + (no,)] for no in range(sz.lz)]


def put_layers(ref, lead, parts):
    for no, part in enumerate(parts):
        ref[lead + (no,)] = part


def split_parts(value):
    high = value.astype(BF16)
    rest = value - high.astype(F32)
    middle = rest.astype(BF16)
    low = (rest - middle.astype(F32)).astype(BF16)
    return high, middle, low


def gather_slots(sz, fields, row_hot, col_hot):
    pieces = [split_parts(jnp.concatenate(field, axis=0)) for field in fields]
    lhs = jnp.concatenate([part for piece in pieces for part in piece], axis=0)
    picked = jnp.dot(lhs, col_hot, preferred_element_type=F32)
    out = []
    for no in range(len(fields)):
        base = 3 * no * sz.rows
        high = picked[base : base + sz.rows]
        middle = picked[base + sz.rows : base + 2 * sz.rows]
        low = picked[base + 2 * sz.rows : base + 3 * sz.rows]
        full = (low + middle) + high
        out.append(jnp.sum(full * row_hot, axis=0, keepdims=True))
    return jnp.concatenate(out, axis=0)


def scatter_slots(sz, values, row_hot, col_hot):
    count = values.shape[0]
    pieces = []
    for no in range(count):
        value = values[no : no + 1]
        high = value.astype(BF16).astype(F32)
        rest = value - high
        middle = rest.astype(BF16).astype(F32)
        low = (rest - middle).astype(BF16).astype(F32)
        for part in (high, middle, low):
            pieces.append((row_hot * part).astype(BF16))
    lhs = jnp.concatenate(pieces, axis=0)
    spread = lax.dot_general(
        lhs, col_hot, (((1,), (1,)), ((), ())), preferred_element_type=F32
    )
    out = []
    for no in range(count):
        base = 3 * no * sz.rows
        high = spread[base : base + sz.rows]
        middle = spread[base + sz.rows : base + 2 * sz.rows]
        low = spread[base + 2 * sz.rows : base + 3 * sz.rows]
        full = (low + middle) + high
        out.append([full[k * sz.ry : (k + 1) * sz.ry] for k in range(sz.lz)])
    return out


def lane_row(sz, ref):
    return jnp.concatenate([ref[0, 0, j : j + 1, :] for j in range(sz.areal)], axis=1)


def read_slots(sz, recv_ref, first, count):
    return jnp.concatenate(
        [recv_ref[j, first : first + count, 0 : sz.cap] for j in range(sz.areal)], axis=1
    )


def write_slots(sz, send_ref, first, values):
    count = values.shape[0]
    for j in range(sz.areal):
        send_ref[j, first : first + count, 0 : sz.cap] = values[:, j * sz.cap : (j + 1) * sz.cap]


def even_layer(sz):
    place = lax.rem(lax.axis_index("layer"), 2)
    return jnp.full((sz.ry, sz.nx), place, jnp.int32) == 0


def write_halo(sz, send_ref, even_ref, odd_ref, y_up, y_down, z_up, z_down):
    me = lax.axis_index("areal")

    @pl.when(me < sz.areal - 1)
    def _():
        for f, field in enumerate(y_up):
            for k in range(sz.lz):
                send_ref[me + 1, f * sz.lz + k : f * sz.lz + k + 1, :] = field[k][sz.ry - 1 : sz.ry]

    @pl.when(me > 0)
    def _():
        for f, field in enumerate(y_down):
            for k in range(sz.lz):
                send_ref[me - 1, f * sz.lz + k : f * sz.lz + k + 1, :] = field[k][0:1]

    even = even_layer(sz)
    for f in range(len(z_up)):
        top = z_up[f][sz.lz - 1]
        bottom = z_down[f][0] if f < len(z_down) else top
        even_ref[f] = jnp.where(even, top, bottom)
        odd_ref[f] = jnp.where(even, bottom, top)


def read_halo(sz, recv_ref, even_ref, odd_ref, low_fields, high_fields):
    me = lax.axis_index("areal")
    has_low = jnp.full((1, sz.nx), me, jnp.int32) > 0
    has_high = jnp.full((1, sz.nx), me, jnp.int32) < sz.areal - 1
    before = jnp.maximum(me - 1, 0)
    after = jnp.minimum(me + 1, sz.areal - 1)
    even = even_layer(sz)
    lows, highs = [], []
    for f in range(low_fields):
        y_part = [
            jnp.where(has_low, recv_ref[before, f * sz.lz + k : f * sz.lz + k + 1, :], 0.0)
            for k in range(sz.lz)
        ]
        lows.append((y_part, jnp.where(even, odd_ref[f], even_ref[f])))
    for f in range(high_fields):
        y_part = [
            jnp.where(has_high, recv_ref[after, f * sz.lz + k : f * sz.lz + k + 1, :], 0.0)
            for k in range(sz.lz)
        ]
        highs.append((y_part, jnp.where(even, even_ref[f], odd_ref[f])))
    return lows, highs


def x_below(sz, part):
    return pltpu.roll(part, 1, 1)


def x_above(sz, part):
    return pltpu.roll(part, sz.nx - 1, 1)


def y_below(sz, part, edge):
    return jnp.where(iota((sz.ry, sz.nx), 0) == 0, edge, pltpu.roll(part, 1, 0))


def y_above(sz, part, edge):
    return jnp.where(iota((sz.ry, sz.nx), 0) == sz.ry - 1, edge, pltpu.roll(part, sz.ry - 1, 0))


def neighbours(sz, field, k, low, high):
    below = field[k - 1] if k > 0 else low[1]
    above = field[k + 1] if k < sz.lz - 1 else high[1]
    return (
        x_below(sz, field[k]),
        x_above(sz, field[k]),
        y_below(sz, field[k], low[0][k]),
        y_above(sz, field[k], high[0][k]),
        below,
        above,
    )


def mobility(sat_water, sat_gas):
    sat_oil = 1.0 - sat_water - sat_gas
    mobile = (
        sat_water * sat_water * 2.0,
        sat_oil * sat_oil * 0.5,
        sat_gas * sat_gas * 5.0,
    )
    slopes = (4.0 * sat_water, -sat_oil, 10.0 * sat_gas)
    return mobile, slopes


def pack_kernel(
    sz, p_ref, sat_ref, act_ref, trans_ref, up_ref, cell_ref,
    send_ref, even_ref, odd_ref, col_ref, row_ref, mine_ref,
):
    cell = lane_row(sz, cell_ref)
    row_start = iota((sz.rows, sz.slots), 0) * sz.nx
    in_row = (cell >= row_start) & (cell < row_start + sz.nx)
    row_hot = jnp.where(in_row, 1.0, 0.0)
    column = cell - jnp.sum(jnp.where(in_row, row_start, 0), axis=0, keepdims=True)
    col_hot = jnp.where(iota((sz.nx, sz.slots), 0) == column, 1.0, 0.0).astype(BF16)
    row_ref[...] = row_hot
    col_ref[...] = col_hot
    pressure = layers_of(sz, p_ref)
    water = layers_of(sz, sat_ref, 0)
    gas = layers_of(sz, sat_ref, 1)
    act = [part.astype(F32) for part in layers_of(sz, act_ref)]
    ty = [t * a for t, a in zip(layers_of(sz, trans_ref, 1), act)]
    tz = [t * a for t, a in zip(layers_of(sz, trans_ref, 2), act)]
    uy = [u.astype(F32) for u in layers_of(sz, up_ref, 1)]
    uz = [u.astype(F32) for u in layers_of(sz, up_ref, 2)]
    four = [pressure, water, gas, act]
    write_halo(
        sz, send_ref, even_ref, odd_ref,
        [pressure, water, gas, ty, uy], four, [pressure, water, gas, tz, uz], four,
    )
    mine = gather_slots(sz, four, row_hot, col_hot)
    mine_ref[...] = mine
    write_slots(sz, send_ref, 5 * sz.lz, mine)


def setup_kernel(
    sz, recv_ref, even_in, odd_in, p_ref, old_ref, sat_ref, sat_old_ref, pore_ref, trans_ref,
    up_ref, act_ref, live_ref, fup_ref, ftrans_ref, col_ref, row_ref, mine_ref,
    resid_ref, start_ref, total_ref, image_ref, sat_co_ref, inv_ref, slot_ref,
    rhs_ref, guess_ref, send_ref, even_ref, odd_ref,
):
    row_hot = row_ref[...]
    col_hot = col_ref[...]
    mine = mine_ref[...]
    their = read_slots(sz, recv_ref, 5 * sz.lz, 4)
    live = lane_row(sz, live_ref).astype(F32)
    high = lane_row(sz, fup_ref) > 0
    tau = lane_row(sz, ftrans_ref) * live * mine[3:4] * their[3:4]
    drop = their[0:1] - mine[0:1]
    mobile, slopes = mobility(
        jnp.where(high, their[1:2], mine[1:2]), jnp.where(high, their[2:3], mine[2:3])
    )
    flow = [tau * part for part in mobile]
    bend = [tau * drop * part for part in slopes]
    flow_sum = flow[0] + flow[1] + flow[2]
    slot_ref[...] = jnp.concatenate(
        [flow_sum]
        + flow
        + [jnp.where(high, 0.0, part) for part in bend]
        + [jnp.where(high, part, 0.0) for part in bend],
        axis=0,
    )
    scattered = scatter_slots(
        sz,
        jnp.concatenate(flow + [part * drop for part in flow], axis=0),
        row_hot,
        col_hot,
    )
    lows, highs = read_halo(sz, recv_ref, even_in, odd_in, 5, 4)
    pressure = layers_of(sz, p_ref)
    water = layers_of(sz, sat_ref, 0)
    gas = layers_of(sz, sat_ref, 1)
    act = [part.astype(F32) for part in layers_of(sz, act_ref)]
    trans = [layers_of(sz, trans_ref, axis) for axis in range(3)]
    flags = [[u.astype(F32) for u in layers_of(sz, up_ref, axis)] for axis in range(3)]
    carried = [[t * a for t, a in zip(trans[axis], act)] for axis in range(3)]
    lane = iota((sz.ry, sz.nx), 1)
    guesses = []
    for k in range(sz.lz):
        own_act = act[k]
        spare = 1.0 - own_act
        near = [
            neighbours(sz, field, k, lows[f], highs[f])
            for f, field in enumerate((pressure, water, gas, act))
        ]
        below_y = y_below(sz, carried[1][k], lows[3][0][k])
        flag_y = y_below(sz, flags[1][k], lows[4][0][k])
        below_z = carried[2][k - 1] if k > 0 else lows[3][1]
        flag_z = flags[2][k - 1] if k > 0 else lows[4][1]
        taus = (
            jnp.where(lane > 0, x_below(sz, carried[0][k]) * own_act, 0.0),
            jnp.where(lane < sz.nx - 1, carried[0][k] * near[3][1], 0.0),
            below_y * own_act,
            carried[1][k] * near[3][3],
            below_z * own_act,
            carried[2][k] * near[3][5],
        )
        other_up = (
            x_below(sz, flags[0][k]) < 0.5,
            flags[0][k] > 0.5,
            flag_y < 0.5,
            flags[1][k] > 0.5,
            flag_z < 0.5,
            flags[2][k] > 0.5,
        )
        change = pressure[k] - old_ref[k]
        oil = 1.0 - water[k] - gas[k]
        old_water = sat_old_ref[0, k]
        old_gas = sat_old_ref[1, k]
        now = (water[k], oil, gas[k])
        before = (old_water, 1.0 - old_water - old_gas, old_gas)
        pore = pore_ref[k]
        store_p = [own_act * pore * c * s for c, s in zip(COMPRESS, now)]
        store_s = [pore * (1.0 + c * change) for c in COMPRESS]
        resid = [
            own_act * (pore * (s - b + c * s * change)) for c, s, b in zip(COMPRESS, now, before)
        ]
        image_own = [store_p[0], store_p[1], store_p[2]]
        sat_own = [own_act * store_s[0], -(own_act * store_s[1]), own_act * store_s[2]]
        diag = store_p[0] + store_p[1] + store_p[2]
        for d in range(6):
            step = near[0][d] - pressure[k]
            mobile, slopes = mobility(
                jnp.where(other_up[d], near[1][d], water[k]),
                jnp.where(other_up[d], near[2][d], gas[k]),
            )
            face_flow = [taus[d] * part for part in mobile]
            total = face_flow[0] + face_flow[1] + face_flow[2]
            total_ref[d, k] = total
            diag = diag + total
            slope_tau = taus[d] * step
            for row in range(3):
                resid[row] = resid[row] - face_flow[row] * step
                image_own[row] = image_own[row] + face_flow[row]
                image_ref[3 + 6 * row + d, k] = face_flow[row]
                face_bend = slope_tau * slopes[row]
                sat_co_ref[4 + 6 * row + d, k] = jnp.where(other_up[d], face_bend, 0.0)
                sat_own[row] = sat_own[row] - jnp.where(other_up[d], 0.0, face_bend)
        for row in range(3):
            resid[row] = resid[row] - scattered[3 + row][k]
            image_own[row] = image_own[row] + scattered[row][k]
            resid_ref[row, k] = resid[row]
            start_ref[row, k] = -resid[row]
        diag = diag + (scattered[0][k] + scattered[1][k] + scattered[2][k]) + spare
        image_ref[0, k] = image_own[0] + spare
        image_ref[1, k] = image_own[1]
        image_ref[2, k] = image_own[2]
        sat_co_ref[0, k] = sat_own[0]
        sat_co_ref[1, k] = sat_own[1]
        sat_co_ref[2, k] = sat_own[2] + spare
        sat_co_ref[3, k] = spare
        relax = DAMPING / diag
        inv_ref[0, k] = relax
        inv_ref[1, k] = own_act / store_s[0]
        inv_ref[2, k] = own_act / store_s[2]
        rhs = -(resid[0] + resid[1] + resid[2])
        rhs_ref[k] = rhs
        guess = relax * rhs
        guess_ref[k] = guess
        guesses.append(guess)
    send_one(sz, guesses, row_hot, col_hot, send_ref, even_ref, odd_ref)


def send_one(sz, field, row_hot, col_hot, send_ref, even_ref, odd_ref):
    write_halo(sz, send_ref, even_ref, odd_ref, [field], [field], [field], [field])
    write_slots(sz, send_ref, sz.lz, gather_slots(sz, [field], row_hot, col_hot))


def sweep_kernel(
    sz, recv_ref, even_in, odd_in, guess_in, rhs_ref, total_ref, inv_ref, slot_ref, col_ref,
    row_ref, guess_ref, send_ref, even_ref, odd_ref,
):
    row_hot = row_ref[...]
    col_hot = col_ref[...]
    their = read_slots(sz, recv_ref, sz.lz, 1)
    scattered = scatter_slots(sz, slot_ref[0:1] * their, row_hot, col_hot)[0]
    lows, highs = read_halo(sz, recv_ref, even_in, odd_in, 1, 1)
    old = layers_of(sz, guess_in)
    guesses = []
    for k in range(sz.lz):
        near = neighbours(sz, old, k, lows[0], highs[0])
        total = rhs_ref[k]
        for d in range(6):
            total = total + total_ref[d, k] * near[d]
        total = total + scattered[k]
        guess = (1.0 - DAMPING) * old[k] + inv_ref[0, k] * total
        guess_ref[k] = guess
        guesses.append(guess)
    send_one(sz, guesses, row_hot, col_hot, send_ref, even_ref, odd_ref)


def second_kernel(
    sz, recv_ref, even_in, odd_in, guess_in, vector_ref, image_co_ref, inv_ref, slot_ref, col_ref,
    row_ref, image_ref, moves_ref, picked_ref, send_ref, even_ref, odd_ref,
):
    row_hot = row_ref[...]
    col_hot = col_ref[...]
    their = read_slots(sz, recv_ref, sz.lz, 1)
    scattered = scatter_slots(sz, slot_ref[1:4] * their, row_hot, col_hot)
    lows, highs = read_halo(sz, recv_ref, even_in, odd_in, 1, 1)
    guess = layers_of(sz, guess_in)
    water, gas = [], []
    for k in range(sz.lz):
        near = neighbours(sz, guess, k, lows[0], highs[0])
        for row in range(3):
            value = image_co_ref[row, k] * guess[k]
            for d in range(6):
                value = value - image_co_ref[3 + 6 * row + d, k] * near[d]
            value = value - scattered[row][k]
            image_ref[row, k] = value
            if row == 0:
                move = inv_ref[1, k] * (vector_ref[0, k] - value)
                moves_ref[0, k] = move
                water.append(move)
            if row == 2:
                move = inv_ref[2, k] * (vector_ref[2, k] - value)
                moves_ref[1, k] = move
                gas.append(move)
    both = [water, gas]
    write_halo(sz, send_ref, even_ref, odd_ref, both, both, both, both)
    picked = gather_slots(sz, both, row_hot, col_hot)
    picked_ref[...] = picked
    write_slots(sz, send_ref, 2 * sz.lz, picked)


def apply_sat(sz, recv_ref, even_in, odd_in, moves_ref, picked_ref, image_ref, co_ref, slot_ref,
              col_hot, row_hot):
    their = read_slots(sz, recv_ref, 2 * sz.lz, 2)
    mine = picked_ref[...]
    mine_rows = (mine[0:1], mine[0:1] + mine[1:2], mine[1:2])
    their_rows = (their[0:1], their[0:1] + their[1:2], their[1:2])
    values = jnp.concatenate(
        [
            slot_ref[4 + row : 5 + row] * mine_rows[row]
            + slot_ref[7 + row : 8 + row] * their_rows[row]
            for row in range(3)
        ],
        axis=0,
    )
    scattered = scatter_slots(sz, values, row_hot, col_hot)
    lows, highs = read_halo(sz, recv_ref, even_in, odd_in, 2, 2)
    water = layers_of(sz, moves_ref, 0)
    gas = layers_of(sz, moves_ref, 1)
    rows = []
    for k in range(sz.lz):
        near_w = neighbours(sz, water, k, lows[0], highs[0])
        near_g = neighbours(sz, gas, k, lows[1], highs[1])
        near = (near_w, [w + g for w, g in zip(near_w, near_g)], near_g)
        own = (water[k], water[k] + gas[k], gas[k])
        layer_rows = []
        for row in range(3):
            value = image_ref[row, k] + co_ref[row, k] * own[row]
            if row == 1:
                value = value + co_ref[3, k] * water[k]
            for d in range(6):
                value = value - co_ref[4 + 6 * row + d, k] * near[row][d]
            layer_rows.append(value - scattered[row][k])
        rows.append(layer_rows)
    return rows


def next_kernel(
    sz, recv_ref, even_in, odd_in, moves_ref, picked_ref, image_ref, vector_ref, co_ref, inv_ref,
    slot_ref, col_ref, row_ref, shifted_ref, rhs_ref, guess_ref, send_ref, even_ref, odd_ref,
):
    row_hot = row_ref[...]
    col_hot = col_ref[...]
    rows = apply_sat(
        sz, recv_ref, even_in, odd_in, moves_ref, picked_ref, image_ref, co_ref, slot_ref, col_hot,
        row_hot,
    )
    guesses = []
    for k in range(sz.lz):
        shifted = [rows[k][row] - vector_ref[row, k] for row in range(3)]
        for row in range(3):
            shifted_ref[row, k] = shifted[row]
        rhs = shifted[0] + shifted[1] + shifted[2]
        rhs_ref[k] = rhs
        guess = inv_ref[0, k] * rhs
        guess_ref[k] = guess
        guesses.append(guess)
    send_one(sz, guesses, row_hot, col_hot, send_ref, even_ref, odd_ref)


def gram_kernel(
    sz, recv_ref, even_in, odd_in, moves_ref, picked_ref, image_ref, start_ref, vector_ref, co_ref,
    slot_ref, col_ref, row_ref, sums_ref,
):
    rows = apply_sat(
        sz, recv_ref, even_in, odd_in, moves_ref, picked_ref, image_ref, co_ref, slot_ref,
        col_ref[...], row_ref[...],
    )
    sums = [jnp.zeros((sz.ry, sz.nx), F32) for _ in range(6)]
    for k in range(sz.lz):
        for row in range(3):
            first = start_ref[row, k]
            second = vector_ref[row, k]
            third = rows[k][row] - second
            pairs = (
                (first, first), (first, second), (second, second),
                (first, third), (second, third), (third, third),
            )
            sums = [total + a * b for total, (a, b) in zip(sums, pairs)]
    lane = iota((1, sz.nx), 1)
    line = jnp.zeros((1, sz.nx), F32)
    for no, total in enumerate(sums):
        value = jnp.sum(jnp.sum(total, axis=0, keepdims=True), axis=1, keepdims=True)
        line = jnp.where(lane == no, value, line)
    sums_ref[...] = jnp.broadcast_to(line.reshape(1, 1, sz.nx), sums_ref.shape)


def weights_of(gram):
    rr, rx, xx, ry, xy, yy = gram
    beta = jnp.sqrt(rr)
    along = rx / rr
    norm_sq = jnp.maximum(xx - along * rx, 0.0)
    norm = jnp.sqrt(norm_sq)
    h11 = 1.0 + along
    h21 = norm / beta
    on_first = (ry - along * rx) / (norm * beta)
    on_second = (xy - along * xx - along * ry + along * along * rx) / norm_sq
    length = (yy - 2.0 * along * xy + along * along * xx) / norm_sq
    h12 = on_first
    h22 = 1.0 + on_second
    h32 = jnp.sqrt(jnp.maximum(length - on_first * on_first - on_second * on_second, 0.0))
    radius = jnp.sqrt(h11 * h11 + h21 * h21)
    cosine = h11 / radius
    sine = h21 / radius
    top = cosine * h12 + sine * h22
    low = -sine * h12 + cosine * h22
    target_top = cosine * beta
    target_low = -sine * beta
    second_radius = jnp.sqrt(low * low + h32 * h32)
    weight_two = (low / second_radius) * target_low / second_radius
    weight_one = (target_top - top * weight_two) / radius
    scale_two = weight_two / norm
    return weight_one / beta - scale_two * along, scale_two


def update_kernel(
    sz, sums_ref, guess_one, moves_one, guess_two, moves_two, update_ref,
):
    line = jnp.sum(sums_ref[...], axis=0)
    lane = iota((1, sz.nx), 1)
    gram = [
        jnp.sum(jnp.where(lane == no, line, 0.0), axis=1, keepdims=True) for no in range(6)
    ]
    one, two = weights_of(gram)
    for k in range(sz.lz):
        update_ref[0, k] = one * guess_one[k] + two * guess_two[k]
        update_ref[1, k] = one * moves_one[0, k] + two * moves_two[0, k]
        update_ref[2, k] = one * moves_one[1, k] + two * moves_two[1, k]


def call(kernel, sz, outs, *args):
    space = pl.BlockSpec(memory_space=pltpu.VMEM)
    return pl.pallas_call(
        functools.partial(kernel, sz),
        out_shape=[jax.ShapeDtypeStruct(shape, dtype) for shape, dtype in outs],
        in_specs=[space] * len(args),
        out_specs=[space] * len(outs),
        compiler_params=pltpu.CompilerParams(vmem_limit_bytes=16 * 2**20),
    )(*args)


def pair_swap(sz, value, first):
    pairs = []
    for low in range(first, sz.layer - 1, 2):
        pairs += [(low, low + 1), (low + 1, low)]
    return lax.ppermute(value, "layer", pairs)


def exchange(sz, send, even, odd):
    return (
        lax.all_to_all(send, "areal", split_axis=0, concat_axis=0, tiled=True),
        pair_swap(sz, even, 0),
        pair_swap(sz, odd, 1),
    )


def local(
    pressure,
    pressure_old,
    saturations,
    saturations_old,
    pore_volume,
    trans,
    upwind,
    active,
    fault_cell,
    fault_live,
    fault_up,
    fault_trans,
):
    sz = Sizes(
        lax.axis_size("areal"), lax.axis_size("layer"), pressure.shape, fault_cell.shape[3]
    )
    cells = pressure.shape

    def field(count):
        return ((count,) + cells, F32)

    def sends(y_fields, slot_fields, z_fields):
        return [
            ((sz.areal, sz.block_rows(y_fields, slot_fields), sz.nx), F32),
            ((z_fields, sz.ry, sz.nx), F32),
            ((z_fields, sz.ry, sz.nx), F32),
        ]

    one_field = sends(1, 1, 1)
    two_fields = sends(2, 2, 2)
    scalar = (cells, F32)
    *out, col_hot, row_hot, mine = call(
        pack_kernel,
        sz,
        sends(5, 4, 5)
        + [((sz.nx, sz.slots), BF16), ((sz.rows, sz.slots), F32), ((4, sz.slots), F32)],
        pressure, saturations, active, trans, upwind, fault_cell,
    )
    moved = exchange(sz, *out)
    resid, start, total_co, image_co, sat_co, inverse, slots, rhs, guess, *out = call(
        setup_kernel,
        sz,
        [field(3), field(3), field(6), field(21), field(22), field(3), ((10, sz.slots), F32),
         scalar, scalar] + one_field,
        *moved, pressure, pressure_old, saturations, saturations_old, pore_volume, trans, upwind,
        active, fault_live, fault_up, fault_trans, col_hot, row_hot, mine,
    )

    def precondition(vector, rhs, guess, out):
        for _ in range(SWEEPS - 1):
            moved = exchange(sz, *out)
            guess, *out = call(
                sweep_kernel, sz, [scalar] + one_field,
                *moved, guess, rhs, total_co, inverse, slots, col_hot, row_hot,
            )
        moved = exchange(sz, *out)
        image, moves, picked, *out = call(
            second_kernel, sz, [field(3), field(2), ((2, sz.slots), F32)] + two_fields,
            *moved, guess, vector, image_co, inverse, slots, col_hot, row_hot,
        )
        return guess, moves, picked, image, exchange(sz, *out)

    guess_one, moves_one, picked, image, moved = precondition(start, rhs, guess, out)
    shifted, rhs, guess, *out = call(
        next_kernel, sz, [field(3), scalar, scalar] + one_field,
        *moved, moves_one, picked, image, start, sat_co, inverse, slots, col_hot, row_hot,
    )
    guess_two, moves_two, picked, image, moved = precondition(shifted, rhs, guess, out)
    (sums,) = call(
        gram_kernel, sz, [((sz.areal * sz.layer, 1, sz.nx), F32)],
        *moved, moves_two, picked, image, start, shifted, sat_co, slots, col_hot, row_hot,
    )
    sums = lax.all_to_all(sums, ("areal", "layer"), split_axis=0, concat_axis=0, tiled=True)
    (update,) = call(
        update_kernel, sz, [field(3)], sums, guess_one, moves_one, guess_two, moves_two
    )
    return (resid, update)


def solution(mesh):
    cell = P("layer", "areal", None)
    rows = P(None, "layer", "areal", None)
    fault = P("layer", "areal", None, None)
    return jax.shard_map(
        local,
        mesh=mesh,
        in_specs=(cell, cell, rows, rows, cell, rows, rows, cell, fault, fault, fault, fault),
        out_specs=(rows, rows),
        check_vma=False,
    )
```

profile of v0, /device:TPU:0, one launch (start us, length us, event | category | flops | bytes accessed | tf_op | source)
XLA Modules:
  0.0 144.0 jit_solution(3496411880990110097)
XLA Ops:
  6.8 5.3 %all-to-all-start = ((f32[8,24,128]{2,1,0:T(8,128)}), f32[8,24,128]{2,1,0:T(8,128)S(1)}, u32[]{:S(2)}, u32[]{:S(2)}) async-start(f32[8,24,128]{2,1,0:T(8,128)} %get-tuple-element.62), calls=%async_computation | async-start | bytes 196608 | tf_op jit(solution)/shard_map/all_to_all | solution.py:571
  14.4 1.8 %collective-permute-done.even_in = f32[5,16,128]{2,1,0:T(8,128)S(1)} collective-permute-done((f32[5,16,128]{2,1,0:T(8,128)S(1)}, f32[5,16,128]{2,1,0:T(8,128)S(1)}, u32[]{:S(2)}, u32[]{:S(2)}) %collective-permute-start) | collective-permute-done | bytes 40992 | tf_op jit(solution)/shard_map/ppermute | solution.py:566
  17.4 1.8 %shard_map.132 = (f32[3,4,16,128]{3,2,1,0:T(8,128)}, f32[3,4,16,128]{3,2,1,0:T(8,128)S(1)}, f32[6,4,16,128]{3,2,1,0:T(8,128)S(1)}, f32[21,4,16,128]{3,2,1,0:T(8,...) custom-call(f32[8,24,128]{2,1,0:T(8,128)S(1)} %all-to-all-done.recv_, ...), custom_call_target="tpu_custom_call" | custom-call | tf_op jit(solution)/shard_map/pallas_call | solution.py:553
  19.1 3.3 %all-to-all-start.1 = ((f32[8,8,128]{2,1,0:T(8,128)}), f32[8,8,128]{2,1,0:T(8,128)S(1)}, u32[]{:S(2)}, u32[]{:S(2)}) async-start(f32[8,8,128]{2,1,0:T(8,128)} %get-tuple-element.69), calls=%async_computation.1 | async-start | bytes 65536 | tf_op jit(solution)/shard_map/all_to_all | solution.py:571
  22.5 4.3 %collective-permute-start.2 = (f32[1,16,128]{2,1,0:T(8,128)S(1)}, f32[1,16,128]{2,1,0:T(8,128)S(1)}, u32[]{:S(2)}, u32[]{:S(2)}) collective-permute-start(f32[1,16,128]{2,1,0:T(8,128)S(1)} %get-tuple-element.70), channel_id=1, source_target_pairs={{0,1},{1,0},{2,3},{3,2},{4,5},{5,4},{6,7},{7,6},{8,9},{9,8},{10,11... | collective-permute-start | bytes 24584 | tf_op jit(solution)/shard_map/ppermute | solution.py:566
  29.6 4.2 %all-to-all-start.2 = ((f32[8,8,128]{2,1,0:T(8,128)}), f32[8,8,128]{2,1,0:T(8,128)S(1)}, u32[]{:S(2)}, u32[]{:S(2)}) async-start(f32[8,8,128]{2,1,0:T(8,128)} %get-tuple-element.77), calls=%async_computation.2 | async-start | bytes 65536 | tf_op jit(solution)/shard_map/all_to_all | solution.py:571
  33.8 3.9 %collective-permute-start.4 = (f32[1,16,128]{2,1,0:T(8,128)S(1)}, f32[1,16,128]{2,1,0:T(8,128)S(1)}, u32[]{:S(2)}, u32[]{:S(2)}) collective-permute-start(f32[1,16,128]{2,1,0:T(8,128)S(1)} %get-tuple-element.78), channel_id=1, source_target_pairs={{0,1},{1,0},{2,3},{3,2},{4,5},{5,4},{6,7},{7,6},{8,9},{9,8},{10,11... | collective-permute-start | bytes 24584 | tf_op jit(solution)/shard_map/ppermute | solution.py:566
  40.4 4.2 %all-to-all-start.3 = ((f32[8,8,128]{2,1,0:T(8,128)}), f32[8,8,128]{2,1,0:T(8,128)S(1)}, u32[]{:S(2)}, u32[]{:S(2)}) async-start(f32[8,8,128]{2,1,0:T(8,128)} %get-tuple-element.81), calls=%async_computation.3 | async-start | bytes 65536 | tf_op jit(solution)/shard_map/all_to_all | solution.py:571
  44.6 3.9 %collective-permute-start.6 = (f32[1,16,128]{2,1,0:T(8,128)S(1)}, f32[1,16,128]{2,1,0:T(8,128)S(1)}, u32[]{:S(2)}, u32[]{:S(2)}) collective-permute-start(f32[1,16,128]{2,1,0:T(8,128)S(1)} %get-tuple-element.82), channel_id=1, source_target_pairs={{0,1},{1,0},{2,3},{3,2},{4,5},{5,4},{6,7},{7,6},{8,9},{9,8},{10,11... | collective-permute-start | bytes 24584 | tf_op jit(solution)/shard_map/ppermute | solution.py:566
  51.4 4.2 %all-to-all-start.4 = ((f32[8,8,128]{2,1,0:T(8,128)}), f32[8,8,128]{2,1,0:T(8,128)S(1)}, u32[]{:S(2)}, u32[]{:S(2)}) async-start(f32[8,8,128]{2,1,0:T(8,128)} %get-tuple-element.85), calls=%async_computation.4 | async-start | bytes 65536 | tf_op jit(solution)/shard_map/all_to_all | solution.py:571
  55.6 3.9 %collective-permute-start.8 = (f32[1,16,128]{2,1,0:T(8,128)S(1)}, f32[1,16,128]{2,1,0:T(8,128)S(1)}, u32[]{:S(2)}, u32[]{:S(2)}) collective-permute-start(f32[1,16,128]{2,1,0:T(8,128)S(1)} %get-tuple-element.86), channel_id=1, source_target_pairs={{0,1},{1,0},{2,3},{3,2},{4,5},{5,4},{6,7},{7,6},{8,9},{9,8},{10,11... | collective-permute-start | bytes 24584 | tf_op jit(solution)/shard_map/ppermute | solution.py:566
  62.6 4.2 %all-to-all-start.5 = ((f32[8,16,128]{2,1,0:T(8,128)}), f32[8,16,128]{2,1,0:T(8,128)S(1)}, u32[]{:S(2)}, u32[]{:S(2)}) async-start(f32[8,16,128]{2,1,0:T(8,128)} %get-tuple-element.91), calls=%async_computation.5 | async-start | bytes 131072 | tf_op jit(solution)/shard_map/all_to_all | solution.py:571
  66.8 3.9 %collective-permute-start.10 = (f32[2,16,128]{2,1,0:T(8,128)S(1)}, f32[2,16,128]{2,1,0:T(8,128)S(1)}, u32[]{:S(2)}, u32[]{:S(2)}) collective-permute-start(f32[2,16,128]{2,1,0:T(8,128)S(1)} %get-tuple-element.92), channel_id=1, source_target_pairs={{0,1},{1,0},{2,3},{3,2},{4,5},{5,4},{6,7},{7,6},{8,9},{9,8},{10,11... | collective-permute-start | bytes 49160 | tf_op jit(solution)/shard_map/ppermute | solution.py:566
  73.8 4.2 %all-to-all-start.6 = ((f32[8,8,128]{2,1,0:T(8,128)}), f32[8,8,128]{2,1,0:T(8,128)S(1)}, u32[]{:S(2)}, u32[]{:S(2)}) async-start(f32[8,8,128]{2,1,0:T(8,128)} %get-tuple-element.98), calls=%async_computation.6 | async-start | bytes 65536 | tf_op jit(solution)/shard_map/all_to_all | solution.py:571
  78.0 3.9 %collective-permute-start.12 = (f32[1,16,128]{2,1,0:T(8,128)S(1)}, f32[1,16,128]{2,1,0:T(8,128)S(1)}, u32[]{:S(2)}, u32[]{:S(2)}) collective-permute-start(f32[1,16,128]{2,1,0:T(8,128)S(1)} %get-tuple-element.99), channel_id=1, source_target_pairs={{0,1},{1,0},{2,3},{3,2},{4,5},{5,4},{6,7},{7,6},{8,9},{9,8},{10,11... | collective-permute-start | bytes 24584 | tf_op jit(solution)/shard_map/ppermute | solution.py:566
  84.7 4.2 %all-to-all-start.7 = ((f32[8,8,128]{2,1,0:T(8,128)}), f32[8,8,128]{2,1,0:T(8,128)S(1)}, u32[]{:S(2)}, u32[]{:S(2)}) async-start(f32[8,8,128]{2,1,0:T(8,128)} %get-tuple-element.103), calls=%async_computation.7 | async-start | bytes 65536 | tf_op jit(solution)/shard_map/all_to_all | solution.py:571
  88.9 3.9 %collective-permute-start.14 = (f32[1,16,128]{2,1,0:T(8,128)S(1)}, f32[1,16,128]{2,1,0:T(8,128)S(1)}, u32[]{:S(2)}, u32[]{:S(2)}) collective-permute-start(f32[1,16,128]{2,1,0:T(8,128)S(1)} %get-tuple-element.104), channel_id=1, source_target_pairs={{0,1},{1,0},{2,3},{3,2},{4,5},{5,4},{6,7},{7,6},{8,9},{9,8},{10,11... | collective-permute-start | bytes 24584 | tf_op jit(solution)/shard_map/ppermute | solution.py:566
  95.6 4.2 %all-to-all-start.8 = ((f32[8,8,128]{2,1,0:T(8,128)}), f32[8,8,128]{2,1,0:T(8,128)S(1)}, u32[]{:S(2)}, u32[]{:S(2)}) async-start(f32[8,8,128]{2,1,0:T(8,128)} %get-tuple-element.107), calls=%async_computation.8 | async-start | bytes 65536 | tf_op jit(solution)/shard_map/all_to_all | solution.py:571
  99.8 3.9 %collective-permute-start.16 = (f32[1,16,128]{2,1,0:T(8,128)S(1)}, f32[1,16,128]{2,1,0:T(8,128)S(1)}, u32[]{:S(2)}, u32[]{:S(2)}) collective-permute-start(f32[1,16,128]{2,1,0:T(8,128)S(1)} %get-tuple-element.108), channel_id=1, source_target_pairs={{0,1},{1,0},{2,3},{3,2},{4,5},{5,4},{6,7},{7,6},{8,9},{9,8},{10,11... | collective-permute-start | bytes 24584 | tf_op jit(solution)/shard_map/ppermute | solution.py:566
  106.5 4.2 %all-to-all-start.9 = ((f32[8,8,128]{2,1,0:T(8,128)}), f32[8,8,128]{2,1,0:T(8,128)S(1)}, u32[]{:S(2)}, u32[]{:S(2)}) async-start(f32[8,8,128]{2,1,0:T(8,128)} %get-tuple-element.111), calls=%async_computation.9 | async-start | bytes 65536 | tf_op jit(solution)/shard_map/all_to_all | solution.py:571
  110.7 3.9 %collective-permute-start.18 = (f32[1,16,128]{2,1,0:T(8,128)S(1)}, f32[1,16,128]{2,1,0:T(8,128)S(1)}, u32[]{:S(2)}, u32[]{:S(2)}) collective-permute-start(f32[1,16,128]{2,1,0:T(8,128)S(1)} %get-tuple-element.112), channel_id=1, source_target_pairs={{0,1},{1,0},{2,3},{3,2},{4,5},{5,4},{6,7},{7,6},{8,9},{9,8},{10,11... | collective-permute-start | bytes 24584 | tf_op jit(solution)/shard_map/ppermute | solution.py:566
  117.7 4.2 %all-to-all-start.10 = ((f32[8,16,128]{2,1,0:T(8,128)}), f32[8,16,128]{2,1,0:T(8,128)S(1)}, u32[]{:S(2)}, u32[]{:S(2)}) async-start(f32[8,16,128]{2,1,0:T(8,128)} %get-tuple-element.116), calls=%async_computation.10 | async-start | bytes 131072 | tf_op jit(solution)/shard_map/all_to_all | solution.py:571
  121.9 3.9 %collective-permute-start.20 = (f32[2,16,128]{2,1,0:T(8,128)S(1)}, f32[2,16,128]{2,1,0:T(8,128)S(1)}, u32[]{:S(2)}, u32[]{:S(2)}) collective-permute-start(f32[2,16,128]{2,1,0:T(8,128)S(1)} %get-tuple-element.117), channel_id=1, source_target_pairs={{0,1},{1,0},{2,3},{3,2},{4,5},{5,4},{6,7},{7,6},{8,9},{9,8},{10,11... | collective-permute-start | bytes 49160 | tf_op jit(solution)/shard_map/ppermute | solution.py:566
  128.0 15.1 %all_to_all.60.sums_ref = f32[32,1,128]{2,1,0:T(1,128)S(1)} all-to-all(f32[32,1,128]{2,1,0:T(1,128)S(1)} %shard_map.142), channel_id=1, replica_groups=mesh['areal'=8,'layer'=4] {'areal','layer'}, dimensions={0} | all-to-all | bytes 32768 | tf_op jit(solution)/shard_map/all_to_all | solution.py:650
  (90 shorter events, 38.5 us)
Async XLA Ops:
  6.8 10.5 %all-to-all-start = ((f32[8,24,128]{2,1,0:T(8,128)}), f32[8,24,128]{2,1,0:T(8,128)S(1)}, u32[]{:S(2)}, u32[]{:S(2)}) async-start(f32[8,24,128]{2,1,0:T(8,128)} %get-tuple-element.62), calls=%async_computation | async-start | bytes 196608 | tf_op jit(solution)/shard_map/all_to_all | solution.py:571
  12.1 4.1 %collective-permute-start = (f32[5,16,128]{2,1,0:T(8,128)S(1)}, f32[5,16,128]{2,1,0:T(8,128)S(1)}, u32[]{:S(2)}, u32[]{:S(2)}) collective-permute-start(f32[5,16,128]{2,1,0:T(8,128)S(1)} %get-tuple-element.63), channel_id=1, source_target_pairs={{0,1},{1,0},{2,3},{3,2},{4,5},{5,4},{6,7},{7,6},{8,9},{9,8},{10,11... | collective-permute-start | bytes 122888 | tf_op jit(solution)/shard_map/ppermute | solution.py:566
  13.8 2.4 %collective-permute-start.1 = (f32[5,16,128]{2,1,0:T(8,128)S(1)}, f32[5,16,128]{2,1,0:T(8,128)S(1)}, u32[]{:S(2)}, u32[]{:S(2)}) collective-permute-start(f32[5,16,128]{2,1,0:T(8,128)S(1)} %get-tuple-element.64), channel_id=1, source_target_pairs={{1,2},{2,1},{5,6},{6,5},{9,10},{10,9},{13,14},{14,13},{17,18},{18,... | collective-permute-start | bytes 122888 | tf_op jit(solution)/shard_map/ppermute | solution.py:566
  19.1 9.3 %all-to-all-start.1 = ((f32[8,8,128]{2,1,0:T(8,128)}), f32[8,8,128]{2,1,0:T(8,128)S(1)}, u32[]{:S(2)}, u32[]{:S(2)}) async-start(f32[8,8,128]{2,1,0:T(8,128)} %get-tuple-element.69), calls=%async_computation.1 | async-start | bytes 65536 | tf_op jit(solution)/shard_map/all_to_all | solution.py:571
  22.5 5.9 %collective-permute-start.2 = (f32[1,16,128]{2,1,0:T(8,128)S(1)}, f32[1,16,128]{2,1,0:T(8,128)S(1)}, u32[]{:S(2)}, u32[]{:S(2)}) collective-permute-start(f32[1,16,128]{2,1,0:T(8,128)S(1)} %get-tuple-element.70), channel_id=1, source_target_pairs={{0,1},{1,0},{2,3},{3,2},{4,5},{5,4},{6,7},{7,6},{8,9},{9,8},{10,11... | collective-permute-start | bytes 24584 | tf_op jit(solution)/shard_map/ppermute | solution.py:566
  29.6 9.7 %all-to-all-start.2 = ((f32[8,8,128]{2,1,0:T(8,128)}), f32[8,8,128]{2,1,0:T(8,128)S(1)}, u32[]{:S(2)}, u32[]{:S(2)}) async-start(f32[8,8,128]{2,1,0:T(8,128)} %get-tuple-element.77), calls=%async_computation.2 | async-start | bytes 65536 | tf_op jit(solution)/shard_map/all_to_all | solution.py:571
  33.8 5.5 %collective-permute-start.4 = (f32[1,16,128]{2,1,0:T(8,128)S(1)}, f32[1,16,128]{2,1,0:T(8,128)S(1)}, u32[]{:S(2)}, u32[]{:S(2)}) collective-permute-start(f32[1,16,128]{2,1,0:T(8,128)S(1)} %get-tuple-element.78), channel_id=1, source_target_pairs={{0,1},{1,0},{2,3},{3,2},{4,5},{5,4},{6,7},{7,6},{8,9},{9,8},{10,11... | collective-permute-start | bytes 24584 | tf_op jit(solution)/shard_map/ppermute | solution.py:566
  40.4 9.7 %all-to-all-start.3 = ((f32[8,8,128]{2,1,0:T(8,128)}), f32[8,8,128]{2,1,0:T(8,128)S(1)}, u32[]{:S(2)}, u32[]{:S(2)}) async-start(f32[8,8,128]{2,1,0:T(8,128)} %get-tuple-element.81), calls=%async_computation.3 | async-start | bytes 65536 | tf_op jit(solution)/shard_map/all_to_all | solution.py:571
  44.6 5.5 %collective-permute-start.6 = (f32[1,16,128]{2,1,0:T(8,128)S(1)}, f32[1,16,128]{2,1,0:T(8,128)S(1)}, u32[]{:S(2)}, u32[]{:S(2)}) collective-permute-start(f32[1,16,128]{2,1,0:T(8,128)S(1)} %get-tuple-element.82), channel_id=1, source_target_pairs={{0,1},{1,0},{2,3},{3,2},{4,5},{5,4},{6,7},{7,6},{8,9},{9,8},{10,11... | collective-permute-start | bytes 24584 | tf_op jit(solution)/shard_map/ppermute | solution.py:566
  51.4 9.7 %all-to-all-start.4 = ((f32[8,8,128]{2,1,0:T(8,128)}), f32[8,8,128]{2,1,0:T(8,128)S(1)}, u32[]{:S(2)}, u32[]{:S(2)}) async-start(f32[8,8,128]{2,1,0:T(8,128)} %get-tuple-element.85), calls=%async_computation.4 | async-start | bytes 65536 | tf_op jit(solution)/shard_map/all_to_all | solution.py:571
  55.6 5.5 %collective-permute-start.8 = (f32[1,16,128]{2,1,0:T(8,128)S(1)}, f32[1,16,128]{2,1,0:T(8,128)S(1)}, u32[]{:S(2)}, u32[]{:S(2)}) collective-permute-start(f32[1,16,128]{2,1,0:T(8,128)S(1)} %get-tuple-element.86), channel_id=1, source_target_pairs={{0,1},{1,0},{2,3},{3,2},{4,5},{5,4},{6,7},{7,6},{8,9},{9,8},{10,11... | collective-permute-start | bytes 24584 | tf_op jit(solution)/shard_map/ppermute | solution.py:566
  62.6 9.8 %all-to-all-start.5 = ((f32[8,16,128]{2,1,0:T(8,128)}), f32[8,16,128]{2,1,0:T(8,128)S(1)}, u32[]{:S(2)}, u32[]{:S(2)}) async-start(f32[8,16,128]{2,1,0:T(8,128)} %get-tuple-element.91), calls=%async_computation.5 | async-start | bytes 131072 | tf_op jit(solution)/shard_map/all_to_all | solution.py:571
  66.8 5.6 %collective-permute-start.10 = (f32[2,16,128]{2,1,0:T(8,128)S(1)}, f32[2,16,128]{2,1,0:T(8,128)S(1)}, u32[]{:S(2)}, u32[]{:S(2)}) collective-permute-start(f32[2,16,128]{2,1,0:T(8,128)S(1)} %get-tuple-element.92), channel_id=1, source_target_pairs={{0,1},{1,0},{2,3},{3,2},{4,5},{5,4},{6,7},{7,6},{8,9},{9,8},{10,11... | collective-permute-start | bytes 49160 | tf_op jit(solution)/shard_map/ppermute | solution.py:566
  70.7 1.7 %collective-permute-start.11 = (f32[2,16,128]{2,1,0:T(8,128)S(1)}, f32[2,16,128]{2,1,0:T(8,128)S(1)}, u32[]{:S(2)}, u32[]{:S(2)}) collective-permute-start(f32[2,16,128]{2,1,0:T(8,128)S(1)} %get-tuple-element.93), channel_id=1, source_target_pairs={{1,2},{2,1},{5,6},{6,5},{9,10},{10,9},{13,14},{14,13},{17,18},{18,... | collective-permute-start | bytes 49160 | tf_op jit(solution)/shard_map/ppermute | solution.py:566
  73.8 9.7 %all-to-all-start.6 = ((f32[8,8,128]{2,1,0:T(8,128)}), f32[8,8,128]{2,1,0:T(8,128)S(1)}, u32[]{:S(2)}, u32[]{:S(2)}) async-start(f32[8,8,128]{2,1,0:T(8,128)} %get-tuple-element.98), calls=%async_computation.6 | async-start | bytes 65536 | tf_op jit(solution)/shard_map/all_to_all | solution.py:571
  78.0 5.5 %collective-permute-start.12 = (f32[1,16,128]{2,1,0:T(8,128)S(1)}, f32[1,16,128]{2,1,0:T(8,128)S(1)}, u32[]{:S(2)}, u32[]{:S(2)}) collective-permute-start(f32[1,16,128]{2,1,0:T(8,128)S(1)} %get-tuple-element.99), channel_id=1, source_target_pairs={{0,1},{1,0},{2,3},{3,2},{4,5},{5,4},{6,7},{7,6},{8,9},{9,8},{10,11... | collective-permute-start | bytes 24584 | tf_op jit(solution)/shard_map/ppermute | solution.py:566
  84.7 9.7 %all-to-all-start.7 = ((f32[8,8,128]{2,1,0:T(8,128)}), f32[8,8,128]{2,1,0:T(8,128)S(1)}, u32[]{:S(2)}, u32[]{:S(2)}) async-start(f32[8,8,128]{2,1,0:T(8,128)} %get-tuple-element.103), calls=%async_computation.7 | async-start | bytes 65536 | tf_op jit(solution)/shard_map/all_to_all | solution.py:571
  88.9 5.5 %collective-permute-start.14 = (f32[1,16,128]{2,1,0:T(8,128)S(1)}, f32[1,16,128]{2,1,0:T(8,128)S(1)}, u32[]{:S(2)}, u32[]{:S(2)}) collective-permute-start(f32[1,16,128]{2,1,0:T(8,128)S(1)} %get-tuple-element.104), channel_id=1, source_target_pairs={{0,1},{1,0},{2,3},{3,2},{4,5},{5,4},{6,7},{7,6},{8,9},{9,8},{10,11... | collective-permute-start | bytes 24584 | tf_op jit(solution)/shard_map/ppermute | solution.py:566
  95.6 9.7 %all-to-all-start.8 = ((f32[8,8,128]{2,1,0:T(8,128)}), f32[8,8,128]{2,1,0:T(8,128)S(1)}, u32[]{:S(2)}, u32[]{:S(2)}) async-start(f32[8,8,128]{2,1,0:T(8,128)} %get-tuple-element.107), calls=%async_computation.8 | async-start | bytes 65536 | tf_op jit(solution)/shard_map/all_to_all | solution.py:571
  99.8 5.5 %collective-permute-start.16 = (f32[1,16,128]{2,1,0:T(8,128)S(1)}, f32[1,16,128]{2,1,0:T(8,128)S(1)}, u32[]{:S(2)}, u32[]{:S(2)}) collective-permute-start(f32[1,16,128]{2,1,0:T(8,128)S(1)} %get-tuple-element.108), channel_id=1, source_target_pairs={{0,1},{1,0},{2,3},{3,2},{4,5},{5,4},{6,7},{7,6},{8,9},{9,8},{10,11... | collective-permute-start | bytes 24584 | tf_op jit(solution)/shard_map/ppermute | solution.py:566
  106.5 9.7 %all-to-all-start.9 = ((f32[8,8,128]{2,1,0:T(8,128)}), f32[8,8,128]{2,1,0:T(8,128)S(1)}, u32[]{:S(2)}, u32[]{:S(2)}) async-start(f32[8,8,128]{2,1,0:T(8,128)} %get-tuple-element.111), calls=%async_computation.9 | async-start | bytes 65536 | tf_op jit(solution)/shard_map/all_to_all | solution.py:571
  110.7 5.5 %collective-permute-start.18 = (f32[1,16,128]{2,1,0:T(8,128)S(1)}, f32[1,16,128]{2,1,0:T(8,128)S(1)}, u32[]{:S(2)}, u32[]{:S(2)}) collective-permute-start(f32[1,16,128]{2,1,0:T(8,128)S(1)} %get-tuple-element.112), channel_id=1, source_target_pairs={{0,1},{1,0},{2,3},{3,2},{4,5},{5,4},{6,7},{7,6},{8,9},{9,8},{10,11... | collective-permute-start | bytes 24584 | tf_op jit(solution)/shard_map/ppermute | solution.py:566
  117.7 9.8 %all-to-all-start.10 = ((f32[8,16,128]{2,1,0:T(8,128)}), f32[8,16,128]{2,1,0:T(8,128)S(1)}, u32[]{:S(2)}, u32[]{:S(2)}) async-start(f32[8,16,128]{2,1,0:T(8,128)} %get-tuple-element.116), calls=%async_computation.10 | async-start | bytes 131072 | tf_op jit(solution)/shard_map/all_to_all | solution.py:571
  121.9 5.6 %collective-permute-start.20 = (f32[2,16,128]{2,1,0:T(8,128)S(1)}, f32[2,16,128]{2,1,0:T(8,128)S(1)}, u32[]{:S(2)}, u32[]{:S(2)}) collective-permute-start(f32[2,16,128]{2,1,0:T(8,128)S(1)} %get-tuple-element.117), channel_id=1, source_target_pairs={{0,1},{1,0},{2,3},{3,2},{4,5},{5,4},{6,7},{7,6},{8,9},{9,8},{10,11... | collective-permute-start | bytes 49160 | tf_op jit(solution)/shard_map/ppermute | solution.py:566
  (26 other events, 134.1 us)
where the time goes:
time: 145 us; the launch traced here: 144 us
  starting transfers between devices  94.7 us (65%)
  Pallas kernels  15.6 us (11%)
  blocking collectives  15.1 us (10%)
  waiting for transfers between devices  12.8 us (9%)
  local copies, waits for them, and re-layouts  4.86 us (3%)
    ppermute x22, starting transfers between devices, pair_swap(): return lax.ppermute(value, 'layer', pairs)  48.2 us
    all_to_all x11, starting transfers between devices, exchange(): lax.all_to_all(send, 'areal', split_axis=0, concat_axis=0, tiled=True)  46.5 us
    pallas_call x13, Pallas kernels, call(): pl.pallas_call(functools.partial(kernel, sz), out_shape=[jax.ShapeDtypeSt...  15.6 us
    all_to_all x1, blocking collectives, local(): lax.all_to_all(sums, ('areal', 'layer'), split_axis=0, concat_axis=0, til...  15.1 us
    ppermute x22, waiting for transfers between devices, pair_swap(): return lax.ppermute(value, 'layer', pairs)  11.7 us
    unnamed x34, local copies, waits for them, and re-layouts  4.86 us
  transfers between devices with their start and end apart: 33, of which 12 were waited for; matrix products, arithmetic and copies ran while one was open for 0% of the time, Pallas kernels for 0%

commit v1 on v0

--- a/solution.py
+++ b/solution.py
@@ -96,16 +96,33 @@
     return jnp.concatenate([ref[0, 0, j : j + 1, :] for j in range(sz.areal)], axis=1)
 
 
+def paired_lanes(sz):
+    return 2 * sz.cap == sz.nx and sz.areal % 2 == 0
+
+
 def read_slots(sz, recv_ref, first, count):
+    blocks = [recv_ref[j, first : first + count, :] for j in range(sz.areal)]
+    if not paired_lanes(sz):
+        return jnp.concatenate([block[:, : sz.cap] for block in blocks], axis=1)
+    left = iota((count, sz.nx), 1) < sz.cap
     return jnp.concatenate(
-        [recv_ref[j, first : first + count, 0 : sz.cap] for j in range(sz.areal)], axis=1
+        [jnp.where(left, blocks[j], blocks[j + 1]) for j in range(0, sz.areal, 2)], axis=1
     )
 
 
 def write_slots(sz, send_ref, first, values):
     count = values.shape[0]
-    for j in range(sz.areal):
-        send_ref[j, first : first + count, 0 : sz.cap] = values[:, j * sz.cap : (j + 1) * sz.cap]
+    if not paired_lanes(sz):
+        for j in range(sz.areal):
+            part = values[:, j * sz.cap : (j + 1) * sz.cap]
+            send_ref[j, first : first + count, 0 : sz.cap] = part
+        return
+    left = iota((count, sz.nx), 1) < sz.cap
+    for j in range(0, sz.areal, 2):
+        tile = values[:, j * sz.cap : (j + 2) * sz.cap]
+        turned = pltpu.roll(tile, sz.cap, 1)
+        send_ref[j, first : first + count, :] = jnp.where(left, tile, turned)
+        send_ref[j + 1, first : first + count, :] = jnp.where(left, turned, tile)
 
 
 def even_layer(sz):
@@ -188,6 +205,38 @@
     )
 
 
+def inner_neighbours(sz, field, k):
+    return (
+        x_below(sz, field[k]),
+        x_above(sz, field[k]),
+        y_below(sz, field[k], 0.0),
+        y_above(sz, field[k], 0.0),
+        field[k - 1] if k > 0 else None,
+        field[k + 1] if k < sz.lz - 1 else None,
+    )
+
+
+def weighted(values, ref, lead):
+    total = None
+    for d, value in enumerate(values):
+        if value is not None:
+            term = ref[lead(d)] * value
+            total = term if total is None else total + term
+    return total
+
+
+def edge_values(sz, k, low, high):
+    row = iota((sz.ry, sz.nx), 0)
+    return (
+        None,
+        None,
+        jnp.where(row == 0, low[0][k], 0.0),
+        jnp.where(row == sz.ry - 1, high[0][k], 0.0),
+        low[1] if k == 0 else None,
+        high[1] if k == sz.lz - 1 else None,
+    )
+
+
 def mobility(sat_water, sat_gas):
     sat_oil = 1.0 - sat_water - sat_gas
     mobile = (
@@ -200,40 +249,77 @@
 
 
 def pack_kernel(
-    sz, p_ref, sat_ref, act_ref, trans_ref, up_ref, cell_ref,
-    send_ref, even_ref, odd_ref, col_ref, row_ref, mine_ref,
+    sz, p_hbm, sat_hbm, act_hbm, trans_hbm, up_hbm, cell_hbm,
+    send_hbm, even_ref, odd_ref, col_ref, row_ref, mine_ref,
+    cell_ref, p_ref, sat_ref, act_ref, trans_ref, up_ref, send_ref, in_sems, sem,
 ):
+    moves = [
+        pltpu.make_async_copy(source, target, in_sems.at[no])
+        for no, (source, target) in enumerate(
+            (
+                (cell_hbm, cell_ref),
+                (p_hbm, p_ref),
+                (sat_hbm, sat_ref),
+                (act_hbm, act_ref),
+                (trans_hbm.at[pl.ds(1, 2)], trans_ref),
+                (up_hbm.at[pl.ds(1, 2)], up_ref),
+            )
+        )
+    ]
+    for move in moves:
+        move.start()
+    moves[0].wait()
     cell = lane_row(sz, cell_ref)
     row_start = iota((sz.rows, sz.slots), 0) * sz.nx
     in_row = (cell >= row_start) & (cell < row_start + sz.nx)
     row_hot = jnp.where(in_row, 1.0, 0.0)
     column = cell - jnp.sum(jnp.where(in_row, row_start, 0), axis=0, keepdims=True)
     col_hot = jnp.where(iota((sz.nx, sz.slots), 0) == column, 1.0, 0.0).astype(BF16)
-    row_ref[...] = row_hot
-    col_ref[...] = col_hot
+    for move in moves[1:]:
+        move.wait()
     pressure = layers_of(sz, p_ref)
     water = layers_of(sz, sat_ref, 0)
     gas = layers_of(sz, sat_ref, 1)
     act = [part.astype(F32) for part in layers_of(sz, act_ref)]
-    ty = [t * a for t, a in zip(layers_of(sz, trans_ref, 1), act)]
-    tz = [t * a for t, a in zip(layers_of(sz, trans_ref, 2), act)]
-    uy = [u.astype(F32) for u in layers_of(sz, up_ref, 1)]
-    uz = [u.astype(F32) for u in layers_of(sz, up_ref, 2)]
     four = [pressure, water, gas, act]
+    mine = gather_slots(sz, four, row_hot, col_hot)
+    write_slots(sz, send_ref, 5 * sz.lz, mine)
+    ty = [t * a for t, a in zip(layers_of(sz, trans_ref, 0), act)]
+    tz = [t * a for t, a in zip(layers_of(sz, trans_ref, 1), act)]
+    uy = [u.astype(F32) for u in layers_of(sz, up_ref, 0)]
+    uz = [u.astype(F32) for u in layers_of(sz, up_ref, 1)]
     write_halo(
         sz, send_ref, even_ref, odd_ref,
         [pressure, water, gas, ty, uy], four, [pressure, water, gas, tz, uz], four,
     )
-    mine = gather_slots(sz, four, row_hot, col_hot)
+    out = pltpu.make_async_copy(send_ref, send_hbm, sem)
+    out.start()
+    row_ref[...] = row_hot
+    col_ref[...] = col_hot
     mine_ref[...] = mine
-    write_slots(sz, send_ref, 5 * sz.lz, mine)
+    out.wait()
+
+
+def send_fields(sz, fields, row_hot, col_hot, send_hbm, even_ref, odd_ref, send_ref, sem):
+    picked = gather_slots(sz, fields, row_hot, col_hot)
+    write_halo(sz, send_ref, even_ref, odd_ref, fields, fields, fields, fields)
+    write_slots(sz, send_ref, len(fields) * sz.lz, picked)
+    out = pltpu.make_async_copy(send_ref, send_hbm, sem)
+    out.start()
+    return out, picked
+
+
+def sweep_ready(sz, guesses, rhs, total_ref, relax, ready_ref):
+    for k in range(sz.lz):
+        total = weighted(inner_neighbours(sz, guesses, k), total_ref, lambda d: (d, k))
+        ready_ref[k] = (1.0 - DAMPING) * guesses[k] + relax[k] * (rhs[k] + total)
 
 
 def setup_kernel(
     sz, recv_ref, even_in, odd_in, p_ref, old_ref, sat_ref, sat_old_ref, pore_ref, trans_ref,
     up_ref, act_ref, live_ref, fup_ref, ftrans_ref, col_ref, row_ref, mine_ref,
-    resid_ref, start_ref, total_ref, image_ref, sat_co_ref, inv_ref, slot_ref,
-    rhs_ref, guess_ref, send_ref, even_ref, odd_ref,
+    resid_hbm, start_ref, total_ref, image_ref, sat_co_ref, inv_ref, slot_ref,
+    rhs_ref, ready_ref, send_hbm, even_ref, odd_ref, resid_ref, send_ref, sems,
 ):
     row_hot = row_ref[...]
     col_hot = col_ref[...]
@@ -249,13 +335,6 @@
     flow = [tau * part for part in mobile]
     bend = [tau * drop * part for part in slopes]
     flow_sum = flow[0] + flow[1] + flow[2]
-    slot_ref[...] = jnp.concatenate(
-        [flow_sum]
-        + flow
-        + [jnp.where(high, 0.0, part) for part in bend]
-        + [jnp.where(high, part, 0.0) for part in bend],
-        axis=0,
-    )
     scattered = scatter_slots(
         sz,
         jnp.concatenate(flow + [part * drop for part in flow], axis=0),
@@ -271,7 +350,7 @@
     flags = [[u.astype(F32) for u in layers_of(sz, up_ref, axis)] for axis in range(3)]
     carried = [[t * a for t, a in zip(trans[axis], act)] for axis in range(3)]
     lane = iota((sz.ry, sz.nx), 1)
-    guesses = []
+    guesses, relaxes, rights = [], [], []
     for k in range(sz.lz):
         own_act = act[k]
         spare = 1.0 - own_act
@@ -351,76 +430,126 @@
         inv_ref[2, k] = own_act / store_s[2]
         rhs = -(resid[0] + resid[1] + resid[2])
         rhs_ref[k] = rhs
-        guess = relax * rhs
-        guess_ref[k] = guess
-        guesses.append(guess)
-    send_one(sz, guesses, row_hot, col_hot, send_ref, even_ref, odd_ref)
-
-
-def send_one(sz, field, row_hot, col_hot, send_ref, even_ref, odd_ref):
-    write_halo(sz, send_ref, even_ref, odd_ref, [field], [field], [field], [field])
-    write_slots(sz, send_ref, sz.lz, gather_slots(sz, [field], row_hot, col_hot))
+        relaxes.append(relax)
+        rights.append(rhs)
+        guesses.append(relax * rhs)
+    resid_out = pltpu.make_async_copy(resid_ref, resid_hbm, sems.at[1])
+    resid_out.start()
+    out, _ = send_fields(
+        sz, [guesses], row_hot, col_hot, send_hbm, even_ref, odd_ref, send_ref, sems.at[0]
+    )
+    slot_ref[...] = jnp.concatenate(
+        [flow_sum]
+        + flow
+        + [jnp.where(high, 0.0, part) for part in bend]
+        + [jnp.where(high, part, 0.0) for part in bend],
+        axis=0,
+    )
+    sweep_ready(sz, guesses, rights, total_ref, relaxes, ready_ref)
+    resid_out.wait()
+    out.wait()
+
+
+def next_guess(sz, recv_ref, even_in, odd_in, ready_in, total_ref, inv_ref, slot_ref, row_hot,
+               col_hot):
+    their = read_slots(sz, recv_ref, sz.lz, 1)
+    scattered = scatter_slots(sz, slot_ref[0:1] * their, row_hot, col_hot)[0]
+    lows, highs = read_halo(sz, recv_ref, even_in, odd_in, 1, 1)
+    guesses = []
+    for k in range(sz.lz):
+        outside = weighted(edge_values(sz, k, lows[0], highs[0]), total_ref, lambda d: (d, k))
+        guesses.append(ready_in[k] + inv_ref[0, k] * (outside + scattered[k]))
+    return guesses
 
 
 def sweep_kernel(
-    sz, recv_ref, even_in, odd_in, guess_in, rhs_ref, total_ref, inv_ref, slot_ref, col_ref,
-    row_ref, guess_ref, send_ref, even_ref, odd_ref,
+    sz, recv_ref, even_in, odd_in, ready_in, rhs_ref, total_ref, inv_ref, slot_ref, col_ref,
+    row_ref, ready_ref, send_hbm, even_ref, odd_ref, send_ref, sem,
 ):
     row_hot = row_ref[...]
     col_hot = col_ref[...]
-    their = read_slots(sz, recv_ref, sz.lz, 1)
-    scattered = scatter_slots(sz, slot_ref[0:1] * their, row_hot, col_hot)[0]
-    lows, highs = read_halo(sz, recv_ref, even_in, odd_in, 1, 1)
-    old = layers_of(sz, guess_in)
-    guesses = []
-    for k in range(sz.lz):
-        near = neighbours(sz, old, k, lows[0], highs[0])
-        total = rhs_ref[k]
-        for d in range(6):
-            total = total + total_ref[d, k] * near[d]
-        total = total + scattered[k]
-        guess = (1.0 - DAMPING) * old[k] + inv_ref[0, k] * total
-        guess_ref[k] = guess
-        guesses.append(guess)
-    send_one(sz, guesses, row_hot, col_hot, send_ref, even_ref, odd_ref)
+    guesses = next_guess(
+        sz, recv_ref, even_in, odd_in, ready_in, total_ref, inv_ref, slot_ref, row_hot, col_hot
+    )
+    out, _ = send_fields(
+        sz, [guesses], row_hot, col_hot, send_hbm, even_ref, odd_ref, send_ref, sem
+    )
+    sweep_ready(
+        sz, guesses, layers_of(sz, rhs_ref), total_ref, layers_of(sz, inv_ref, 0), ready_ref
+    )
+    out.wait()
+
+
+def last_sweep_kernel(
+    sz, recv_ref, even_in, odd_in, ready_in, total_ref, inv_ref, image_co_ref, slot_ref, col_ref,
+    row_ref, guess_ref, image_ref, send_hbm, even_ref, odd_ref, send_ref, sem,
+):
+    row_hot = row_ref[...]
+    col_hot = col_ref[...]
+    guesses = next_guess(
+        sz, recv_ref, even_in, odd_in, ready_in, total_ref, inv_ref, slot_ref, row_hot, col_hot
+    )
+    out, _ = send_fields(
+        sz, [guesses], row_hot, col_hot, send_hbm, even_ref, odd_ref, send_ref, sem
+    )
+    for k in range(sz.lz):
+        guess_ref[k] = guesses[k]
+        near = inner_neighbours(sz, guesses, k)
+        for row in range(3):
+            image_ref[row, k] = image_co_ref[row, k] * guesses[k] - weighted(
+                near, image_co_ref, lambda d: (3 + 6 * row + d, k)
+            )
+    out.wait()
 
 
 def second_kernel(
-    sz, recv_ref, even_in, odd_in, guess_in, vector_ref, image_co_ref, inv_ref, slot_ref, col_ref,
-    row_ref, image_ref, moves_ref, picked_ref, send_ref, even_ref, odd_ref,
+    sz, recv_ref, even_in, odd_in, image_in, vector_ref, image_co_ref, sat_co_ref, inv_ref,
+    slot_ref, col_ref, row_ref, moves_ref, rows_ref, picked_ref, send_hbm, even_ref, odd_ref,
+    send_ref, sem,
 ):
     row_hot = row_ref[...]
     col_hot = col_ref[...]
     their = read_slots(sz, recv_ref, sz.lz, 1)
     scattered = scatter_slots(sz, slot_ref[1:4] * their, row_hot, col_hot)
     lows, highs = read_halo(sz, recv_ref, even_in, odd_in, 1, 1)
-    guess = layers_of(sz, guess_in)
-    water, gas = [], []
-    for k in range(sz.lz):
-        near = neighbours(sz, guess, k, lows[0], highs[0])
+    water, gas, images = [], [], []
+    for k in range(sz.lz):
+        outside = edge_values(sz, k, lows[0], highs[0])
+        image = [
+            image_in[row, k]
+            - (
+                weighted(outside, image_co_ref, lambda d: (3 + 6 * row + d, k))
+                + scattered[row][k]
+            )
+            for row in range(3)
+        ]
+        images.append(image)
+        water.append(inv_ref[1, k] * (vector_ref[0, k] - image[0]))
+        gas.append(inv_ref[2, k] * (vector_ref[2, k] - image[2]))
+    out, picked = send_fields(
+        sz, [water, gas], row_hot, col_hot, send_hbm, even_ref, odd_ref, send_ref, sem
+    )
+    picked_ref[...] = picked
+    both = [w + g for w, g in zip(water, gas)]
+    for k in range(sz.lz):
+        moves_ref[0, k] = water[k]
+        moves_ref[1, k] = gas[k]
+        own = (water[k], both[k], gas[k])
+        near_w = inner_neighbours(sz, water, k)
+        near_g = inner_neighbours(sz, gas, k)
+        near = (near_w, [None if w is None else w + g for w, g in zip(near_w, near_g)], near_g)
         for row in range(3):
-            value = image_co_ref[row, k] * guess[k]
-            for d in range(6):
-                value = value - image_co_ref[3 + 6 * row + d, k] * near[d]
-            value = value - scattered[row][k]
-            image_ref[row, k] = value
-            if row == 0:
-                move = inv_ref[1, k] * (vector_ref[0, k] - value)
-                moves_ref[0, k] = move
-                water.append(move)
-            if row == 2:
-                move = inv_ref[2, k] * (vector_ref[2, k] - value)
-                moves_ref[1, k] = move
-                gas.append(move)
-    both = [water, gas]
-    write_halo(sz, send_ref, even_ref, odd_ref, both, both, both, both)
-    picked = gather_slots(sz, both, row_hot, col_hot)
-    picked_ref[...] = picked
-    write_slots(sz, send_ref, 2 * sz.lz, picked)
-
-
-def apply_sat(sz, recv_ref, even_in, odd_in, moves_ref, picked_ref, image_ref, co_ref, slot_ref,
-              col_hot, row_hot):
+            value = images[k][row] + sat_co_ref[row, k] * own[row]
+            if row == 1:
+                value = value + sat_co_ref[3, k] * water[k]
+            rows_ref[row, k] = value - weighted(
+                near[row], sat_co_ref, lambda d: (4 + 6 * row + d, k)
+            )
+    out.wait()
+
+
+def apply_sat(sz, recv_ref, even_in, odd_in, rows_in, picked_ref, co_ref, slot_ref, col_hot,
+              row_hot):
     their = read_slots(sz, recv_ref, 2 * sz.lz, 2)
     mine = picked_ref[...]
     mine_rows = (mine[0:1], mine[0:1] + mine[1:2], mine[1:2])
@@ -435,56 +564,59 @@
     )
     scattered = scatter_slots(sz, values, row_hot, col_hot)
     lows, highs = read_halo(sz, recv_ref, even_in, odd_in, 2, 2)
-    water = layers_of(sz, moves_ref, 0)
-    gas = layers_of(sz, moves_ref, 1)
     rows = []
     for k in range(sz.lz):
-        near_w = neighbours(sz, water, k, lows[0], highs[0])
-        near_g = neighbours(sz, gas, k, lows[1], highs[1])
-        near = (near_w, [w + g for w, g in zip(near_w, near_g)], near_g)
-        own = (water[k], water[k] + gas[k], gas[k])
-        layer_rows = []
-        for row in range(3):
-            value = image_ref[row, k] + co_ref[row, k] * own[row]
-            if row == 1:
-                value = value + co_ref[3, k] * water[k]
-            for d in range(6):
-                value = value - co_ref[4 + 6 * row + d, k] * near[row][d]
-            layer_rows.append(value - scattered[row][k])
-        rows.append(layer_rows)
+        near_w = edge_values(sz, k, lows[0], highs[0])
+        near_g = edge_values(sz, k, lows[1], highs[1])
+        near = (near_w, [None if w is None else w + g for w, g in zip(near_w, near_g)], near_g)
+        rows.append(
+            [
+                rows_in[row, k]
+                - (
+                    weighted(near[row], co_ref, lambda d: (4 + 6 * row + d, k))
+                    + scattered[row][k]
+                )
+                for row in range(3)
+            ]
+        )
     return rows
 
 
 def next_kernel(
-    sz, recv_ref, even_in, odd_in, moves_ref, picked_ref, image_ref, vector_ref, co_ref, inv_ref,
-    slot_ref, col_ref, row_ref, shifted_ref, rhs_ref, guess_ref, send_ref, even_ref, odd_ref,
+    sz, recv_ref, even_in, odd_in, rows_in, picked_ref, vector_ref, sat_co_ref, total_ref, inv_ref,
+    slot_ref, col_ref, row_ref, shifted_ref, rhs_ref, ready_ref, send_hbm, even_ref, odd_ref,
+    send_ref, sem,
 ):
     row_hot = row_ref[...]
     col_hot = col_ref[...]
     rows = apply_sat(
-        sz, recv_ref, even_in, odd_in, moves_ref, picked_ref, image_ref, co_ref, slot_ref, col_hot,
-        row_hot,
-    )
-    guesses = []
+        sz, recv_ref, even_in, odd_in, rows_in, picked_ref, sat_co_ref, slot_ref, col_hot, row_hot
+    )
+    guesses, rights, relaxes = [], [], []
     for k in range(sz.lz):
         shifted = [rows[k][row] - vector_ref[row, k] for row in range(3)]
         for row in range(3):
             shifted_ref[row, k] = shifted[row]
         rhs = shifted[0] + shifted[1] + shifted[2]
         rhs_ref[k] = rhs
-        guess = inv_ref[0, k] * rhs
-        guess_ref[k] = guess
-        guesses.append(guess)
-    send_one(sz, guesses, row_hot, col_hot, send_ref, even_ref, odd_ref)
+        relax = inv_ref[0, k]
+        rights.append(rhs)
+        relaxes.append(relax)
+        guesses.append(relax * rhs)
+    out, _ = send_fields(
+        sz, [guesses], row_hot, col_hot, send_hbm, even_ref, odd_ref, send_ref, sem
+    )
+    sweep_ready(sz, guesses, rights, total_ref, relaxes, ready_ref)
+    out.wait()
 
 
 def gram_kernel(
-    sz, recv_ref, even_in, odd_in, moves_ref, picked_ref, image_ref, start_ref, vector_ref, co_ref,
-    slot_ref, col_ref, row_ref, sums_ref,
+    sz, recv_ref, even_in, odd_in, rows_in, picked_ref, start_ref, vector_ref, co_ref, slot_ref,
+    col_ref, row_ref, sums_ref,
 ):
     rows = apply_sat(
-        sz, recv_ref, even_in, odd_in, moves_ref, picked_ref, image_ref, co_ref, slot_ref,
-        col_ref[...], row_ref[...],
+        sz, recv_ref, even_in, odd_in, rows_in, picked_ref, co_ref, slot_ref, col_ref[...],
+        row_ref[...],
     )
     sums = [jnp.zeros((sz.ry, sz.nx), F32) for _ in range(6)]
     for k in range(sz.lz):
@@ -548,13 +680,15 @@
         update_ref[2, k] = one * moves_one[1, k] + two * moves_two[1, k]
 
 
-def call(kernel, sz, outs, *args):
-    space = pl.BlockSpec(memory_space=pltpu.VMEM)
+def call(kernel, sz, outs, *args, far_in=False, far_out=(), scratch=()):
+    near = pl.BlockSpec(memory_space=pltpu.VMEM)
+    far = pl.BlockSpec(memory_space=pltpu.HBM)
     return pl.pallas_call(
         functools.partial(kernel, sz),
         out_shape=[jax.ShapeDtypeStruct(shape, dtype) for shape, dtype in outs],
-        in_specs=[space] * len(args),
-        out_specs=[space] * len(outs),
+        in_specs=[far if far_in else near] * len(args),
+        out_specs=[far if no in far_out else near for no in range(len(outs))],
+        scratch_shapes=list(scratch),
         compiler_params=pltpu.CompilerParams(vmem_limit_bytes=16 * 2**20),
     )(*args)
 
@@ -603,49 +737,76 @@
             ((z_fields, sz.ry, sz.nx), F32),
         ]
 
+    def sender(kernel, outs, to_send, *args):
+        buffers = [pltpu.VMEM(*to_send[0]), pltpu.SemaphoreType.DMA]
+        *kept, send, even, odd = call(
+            kernel, sz, outs + to_send, *args, far_out=(len(outs),), scratch=buffers
+        )
+        return *kept, exchange(sz, send, even, odd)
+
     one_field = sends(1, 1, 1)
     two_fields = sends(2, 2, 2)
+    state = sends(5, 4, 5)
     scalar = (cells, F32)
     *out, col_hot, row_hot, mine = call(
         pack_kernel,
         sz,
-        sends(5, 4, 5)
-        + [((sz.nx, sz.slots), BF16), ((sz.rows, sz.slots), F32), ((4, sz.slots), F32)],
+        state + [((sz.nx, sz.slots), BF16), ((sz.rows, sz.slots), F32), ((4, sz.slots), F32)],
         pressure, saturations, active, trans, upwind, fault_cell,
+        far_in=True,
+        far_out=(0,),
+        scratch=[
+            pltpu.VMEM(fault_cell.shape, jnp.int32),
+            pltpu.VMEM(cells, F32),
+            pltpu.VMEM((2,) + cells, F32),
+            pltpu.VMEM(cells, jnp.int32),
+            pltpu.VMEM((2,) + cells, F32),
+            pltpu.VMEM((2,) + cells, jnp.int32),
+            pltpu.VMEM(*state[0]),
+            pltpu.SemaphoreType.DMA((6,)),
+            pltpu.SemaphoreType.DMA,
+        ],
     )
     moved = exchange(sz, *out)
-    resid, start, total_co, image_co, sat_co, inverse, slots, rhs, guess, *out = call(
+    resid, start, total_co, image_co, sat_co, inverse, slots, rhs, ready, *out = call(
         setup_kernel,
         sz,
         [field(3), field(3), field(6), field(21), field(22), field(3), ((10, sz.slots), F32),
          scalar, scalar] + one_field,
         *moved, pressure, pressure_old, saturations, saturations_old, pore_volume, trans, upwind,
         active, fault_live, fault_up, fault_trans, col_hot, row_hot, mine,
-    )
-
-    def precondition(vector, rhs, guess, out):
-        for _ in range(SWEEPS - 1):
-            moved = exchange(sz, *out)
-            guess, *out = call(
-                sweep_kernel, sz, [scalar] + one_field,
-                *moved, guess, rhs, total_co, inverse, slots, col_hot, row_hot,
+        far_out=(0, 9),
+        scratch=[
+            pltpu.VMEM(*field(3)), pltpu.VMEM(*one_field[0]), pltpu.SemaphoreType.DMA((2,))
+        ],
+    )
+    moved = exchange(sz, *out)
+
+    def precondition(vector, rhs, ready, moved):
+        for _ in range(SWEEPS - 2):
+            ready, moved = sender(
+                sweep_kernel, [scalar], one_field,
+                *moved, ready, rhs, total_co, inverse, slots, col_hot, row_hot,
             )
-        moved = exchange(sz, *out)
-        image, moves, picked, *out = call(
-            second_kernel, sz, [field(3), field(2), ((2, sz.slots), F32)] + two_fields,
-            *moved, guess, vector, image_co, inverse, slots, col_hot, row_hot,
+        guess, image, moved = sender(
+            last_sweep_kernel, [scalar, field(3)], one_field,
+            *moved, ready, total_co, inverse, image_co, slots, col_hot, row_hot,
         )
-        return guess, moves, picked, image, exchange(sz, *out)
-
-    guess_one, moves_one, picked, image, moved = precondition(start, rhs, guess, out)
-    shifted, rhs, guess, *out = call(
-        next_kernel, sz, [field(3), scalar, scalar] + one_field,
-        *moved, moves_one, picked, image, start, sat_co, inverse, slots, col_hot, row_hot,
-    )
-    guess_two, moves_two, picked, image, moved = precondition(shifted, rhs, guess, out)
+        moves, rows, picked, moved = sender(
+            second_kernel, [field(2), field(3), ((2, sz.slots), F32)], two_fields,
+            *moved, image, vector, image_co, sat_co, inverse, slots, col_hot, row_hot,
+        )
+        return guess, moves, rows, picked, moved
+
+    guess_one, moves_one, rows, picked, moved = precondition(start, rhs, ready, moved)
+    shifted, rhs, ready, moved = sender(
+        next_kernel, [field(3), scalar, scalar], one_field,
+        *moved, rows, picked, start, sat_co, total_co, inverse, slots, col_hot, row_hot,
+    )
+    guess_two, moves_two, rows, picked, moved = precondition(shifted, rhs, ready, moved)
     (sums,) = call(
         gram_kernel, sz, [((sz.areal * sz.layer, 1, sz.nx), F32)],
-        *moved, moves_two, picked, image, start, shifted, sat_co, slots, col_hot, row_hot,
+        *moved, rows, picked, start, shifted, sat_co, slots, col_hot, row_hot,
     )
     sums = lax.all_to_all(sums, ("areal", "layer"), split_axis=0, concat_axis=0, tiled=True)
     (update,) = call(

time: 145 us -> 145 us (level)
  no operation moved by 1% of the time
where the time goes in v1:
time: 145 us; the launch traced here: 144 us
  starting transfers between devices  94.8 us (65%)
  blocking collectives  15.1 us (10%)
  Pallas kernels  15 us (10%)
  waiting for transfers between devices  12.8 us (9%)
  local copies, waits for them, and re-layouts  4.87 us (3%)
    ppermute x22, starting transfers between devices, pair_swap(): return lax.ppermute(value, 'layer', pairs)  48.2 us
    all_to_all x11, starting transfers between devices, exchange(): lax.all_to_all(send, 'areal', split_axis=0, concat_axis=0, tiled=True)  46.6 us
    all_to_all x1, blocking collectives, local(): lax.all_to_all(sums, ('areal', 'layer'), split_axis=0, concat_axis=0, til...  15.1 us
    pallas_call x13, Pallas kernels, call(): pl.pallas_call(functools.partial(kernel, sz), out_shape=[jax.ShapeDtypeSt...  15 us
    ppermute x22, waiting for transfers between devices, pair_swap(): return lax.ppermute(value, 'layer', pairs)  11.7 us
    unnamed x34, local copies, waits for them, and re-layouts  4.87 us
  transfers between devices with their start and end apart: 33, of which 12 were waited for; matrix products, arithmetic and copies ran while one was open for 0% of the time, Pallas kernels for 0%

profile of v1, /device:TPU:0, one launch (start us, length us, event | category | flops | bytes accessed | tf_op | source)
XLA Modules:
  0.0 143.5 jit_solution(17613740533270859284)
XLA Ops:
  7.2 5.3 %all-to-all-start = ((f32[8,24,128]{2,1,0:T(8,128)}), f32[8,24,128]{2,1,0:T(8,128)S(1)}, u32[]{:S(2)}, u32[]{:S(2)}) async-start(f32[8,24,128]{2,1,0:T(8,128)} %get-tuple-element.64), calls=%async_computation | async-start | bytes 196608 | tf_op jit(solution)/shard_map/all_to_all | solution.py:705
  14.8 1.8 %collective-permute-done.even_in = f32[5,16,128]{2,1,0:T(8,128)S(1)} collective-permute-done((f32[5,16,128]{2,1,0:T(8,128)S(1)}, f32[5,16,128]{2,1,0:T(8,128)S(1)}, u32[]{:S(2)}, u32[]{:S(2)}) %collective-permute-start) | collective-permute-done | bytes 40992 | tf_op jit(solution)/shard_map/ppermute | solution.py:700
  17.8 1.7 %shard_map.132 = (f32[3,4,16,128]{3,2,1,0:T(8,128)}, f32[3,4,16,128]{3,2,1,0:T(8,128)S(1)}, f32[6,4,16,128]{3,2,1,0:T(8,128)S(1)}, f32[21,4,16,128]{3,2,1,0:T(8,...) custom-call(f32[8,24,128]{2,1,0:T(8,128)S(1)} %all-to-all-done.recv_, ...), custom_call_target="tpu_custom_call" | custom-call | tf_op jit(solution)/shard_map/pallas_call | solution.py:686
  19.6 3.4 %all-to-all-start.1 = ((f32[8,8,128]{2,1,0:T(8,128)}), f32[8,8,128]{2,1,0:T(8,128)S(1)}, u32[]{:S(2)}, u32[]{:S(2)}) async-start(f32[8,8,128]{2,1,0:T(8,128)} %get-tuple-element.71), calls=%async_computation.1 | async-start | bytes 65536 | tf_op jit(solution)/shard_map/all_to_all | solution.py:705
  22.9 4.3 %collective-permute-start.2 = (f32[1,16,128]{2,1,0:T(8,128)S(1)}, f32[1,16,128]{2,1,0:T(8,128)S(1)}, u32[]{:S(2)}, u32[]{:S(2)}) collective-permute-start(f32[1,16,128]{2,1,0:T(8,128)S(1)} %get-tuple-element.72), channel_id=1, source_target_pairs={{0,1},{1,0},{2,3},{3,2},{4,5},{5,4},{6,7},{7,6},{8,9},{9,8},{10,11... | collective-permute-start | bytes 24584 | tf_op jit(solution)/shard_map/ppermute | solution.py:700
  29.9 4.2 %all-to-all-start.2 = ((f32[8,8,128]{2,1,0:T(8,128)}), f32[8,8,128]{2,1,0:T(8,128)S(1)}, u32[]{:S(2)}, u32[]{:S(2)}) async-start(f32[8,8,128]{2,1,0:T(8,128)} %get-tuple-element.79), calls=%async_computation.2 | async-start | bytes 65536 | tf_op jit(solution)/shard_map/all_to_all | solution.py:705
  34.2 3.9 %collective-permute-start.4 = (f32[1,16,128]{2,1,0:T(8,128)S(1)}, f32[1,16,128]{2,1,0:T(8,128)S(1)}, u32[]{:S(2)}, u32[]{:S(2)}) collective-permute-start(f32[1,16,128]{2,1,0:T(8,128)S(1)} %get-tuple-element.80), channel_id=1, source_target_pairs={{0,1},{1,0},{2,3},{3,2},{4,5},{5,4},{6,7},{7,6},{8,9},{9,8},{10,11... | collective-permute-start | bytes 24584 | tf_op jit(solution)/shard_map/ppermute | solution.py:700
  40.8 4.2 %all-to-all-start.3 = ((f32[8,8,128]{2,1,0:T(8,128)}), f32[8,8,128]{2,1,0:T(8,128)S(1)}, u32[]{:S(2)}, u32[]{:S(2)}) async-start(f32[8,8,128]{2,1,0:T(8,128)} %get-tuple-element.83), calls=%async_computation.3 | async-start | bytes 65536 | tf_op jit(solution)/shard_map/all_to_all | solution.py:705
  45.0 3.9 %collective-permute-start.6 = (f32[1,16,128]{2,1,0:T(8,128)S(1)}, f32[1,16,128]{2,1,0:T(8,128)S(1)}, u32[]{:S(2)}, u32[]{:S(2)}) collective-permute-start(f32[1,16,128]{2,1,0:T(8,128)S(1)} %get-tuple-element.84), channel_id=1, source_target_pairs={{0,1},{1,0},{2,3},{3,2},{4,5},{5,4},{6,7},{7,6},{8,9},{9,8},{10,11... | collective-permute-start | bytes 24584 | tf_op jit(solution)/shard_map/ppermute | solution.py:700
  51.7 4.2 %all-to-all-start.4 = ((f32[8,8,128]{2,1,0:T(8,128)}), f32[8,8,128]{2,1,0:T(8,128)S(1)}, u32[]{:S(2)}, u32[]{:S(2)}) async-start(f32[8,8,128]{2,1,0:T(8,128)} %get-tuple-element.88), calls=%async_computation.4 | async-start | bytes 65536 | tf_op jit(solution)/shard_map/all_to_all | solution.py:705
  55.9 3.9 %collective-permute-start.8 = (f32[1,16,128]{2,1,0:T(8,128)S(1)}, f32[1,16,128]{2,1,0:T(8,128)S(1)}, u32[]{:S(2)}, u32[]{:S(2)}) collective-permute-start(f32[1,16,128]{2,1,0:T(8,128)S(1)} %get-tuple-element.89), channel_id=1, source_target_pairs={{0,1},{1,0},{2,3},{3,2},{4,5},{5,4},{6,7},{7,6},{8,9},{9,8},{10,11... | collective-permute-start | bytes 24584 | tf_op jit(solution)/shard_map/ppermute | solution.py:700
  62.7 4.2 %all-to-all-start.5 = ((f32[8,16,128]{2,1,0:T(8,128)}), f32[8,16,128]{2,1,0:T(8,128)S(1)}, u32[]{:S(2)}, u32[]{:S(2)}) async-start(f32[8,16,128]{2,1,0:T(8,128)} %get-tuple-element.94), calls=%async_computation.5 | async-start | bytes 131072 | tf_op jit(solution)/shard_map/all_to_all | solution.py:705
  66.9 3.9 %collective-permute-start.10 = (f32[2,16,128]{2,1,0:T(8,128)S(1)}, f32[2,16,128]{2,1,0:T(8,128)S(1)}, u32[]{:S(2)}, u32[]{:S(2)}) collective-permute-start(f32[2,16,128]{2,1,0:T(8,128)S(1)} %get-tuple-element.95), channel_id=1, source_target_pairs={{0,1},{1,0},{2,3},{3,2},{4,5},{5,4},{6,7},{7,6},{8,9},{9,8},{10,11... | collective-permute-start | bytes 49160 | tf_op jit(solution)/shard_map/ppermute | solution.py:700
  73.8 4.2 %all-to-all-start.6 = ((f32[8,8,128]{2,1,0:T(8,128)}), f32[8,8,128]{2,1,0:T(8,128)S(1)}, u32[]{:S(2)}, u32[]{:S(2)}) async-start(f32[8,8,128]{2,1,0:T(8,128)} %get-tuple-element.99), calls=%async_computation.6 | async-start | bytes 65536 | tf_op jit(solution)/shard_map/all_to_all | solution.py:705
  78.0 3.9 %collective-permute-start.12 = (f32[1,16,128]{2,1,0:T(8,128)S(1)}, f32[1,16,128]{2,1,0:T(8,128)S(1)}, u32[]{:S(2)}, u32[]{:S(2)}) collective-permute-start(f32[1,16,128]{2,1,0:T(8,128)S(1)} %get-tuple-element.100), channel_id=1, source_target_pairs={{0,1},{1,0},{2,3},{3,2},{4,5},{5,4},{6,7},{7,6},{8,9},{9,8},{10,11... | collective-permute-start | bytes 24584 | tf_op jit(solution)/shard_map/ppermute | solution.py:700
  84.6 4.2 %all-to-all-start.7 = ((f32[8,8,128]{2,1,0:T(8,128)}), f32[8,8,128]{2,1,0:T(8,128)S(1)}, u32[]{:S(2)}, u32[]{:S(2)}) async-start(f32[8,8,128]{2,1,0:T(8,128)} %get-tuple-element.104), calls=%async_computation.7 | async-start | bytes 65536 | tf_op jit(solution)/shard_map/all_to_all | solution.py:705
  88.8 3.9 %collective-permute-start.14 = (f32[1,16,128]{2,1,0:T(8,128)S(1)}, f32[1,16,128]{2,1,0:T(8,128)S(1)}, u32[]{:S(2)}, u32[]{:S(2)}) collective-permute-start(f32[1,16,128]{2,1,0:T(8,128)S(1)} %get-tuple-element.105), channel_id=1, source_target_pairs={{0,1},{1,0},{2,3},{3,2},{4,5},{5,4},{6,7},{7,6},{8,9},{9,8},{10,11... | collective-permute-start | bytes 24584 | tf_op jit(solution)/shard_map/ppermute | solution.py:700
  95.5 4.2 %all-to-all-start.8 = ((f32[8,8,128]{2,1,0:T(8,128)}), f32[8,8,128]{2,1,0:T(8,128)S(1)}, u32[]{:S(2)}, u32[]{:S(2)}) async-start(f32[8,8,128]{2,1,0:T(8,128)} %get-tuple-element.108), calls=%async_computation.8 | async-start | bytes 65536 | tf_op jit(solution)/shard_map/all_to_all | solution.py:705
  99.7 3.9 %collective-permute-start.16 = (f32[1,16,128]{2,1,0:T(8,128)S(1)}, f32[1,16,128]{2,1,0:T(8,128)S(1)}, u32[]{:S(2)}, u32[]{:S(2)}) collective-permute-start(f32[1,16,128]{2,1,0:T(8,128)S(1)} %get-tuple-element.109), channel_id=1, source_target_pairs={{0,1},{1,0},{2,3},{3,2},{4,5},{5,4},{6,7},{7,6},{8,9},{9,8},{10,11... | collective-permute-start | bytes 24584 | tf_op jit(solution)/shard_map/ppermute | solution.py:700
  106.4 4.2 %all-to-all-start.9 = ((f32[8,8,128]{2,1,0:T(8,128)}), f32[8,8,128]{2,1,0:T(8,128)S(1)}, u32[]{:S(2)}, u32[]{:S(2)}) async-start(f32[8,8,128]{2,1,0:T(8,128)} %get-tuple-element.112), calls=%async_computation.9 | async-start | bytes 65536 | tf_op jit(solution)/shard_map/all_to_all | solution.py:705
  110.6 3.9 %collective-permute-start.18 = (f32[1,16,128]{2,1,0:T(8,128)S(1)}, f32[1,16,128]{2,1,0:T(8,128)S(1)}, u32[]{:S(2)}, u32[]{:S(2)}) collective-permute-start(f32[1,16,128]{2,1,0:T(8,128)S(1)} %get-tuple-element.113), channel_id=1, source_target_pairs={{0,1},{1,0},{2,3},{3,2},{4,5},{5,4},{6,7},{7,6},{8,9},{9,8},{10,11... | collective-permute-start | bytes 24584 | tf_op jit(solution)/shard_map/ppermute | solution.py:700
  117.4 4.2 %all-to-all-start.10 = ((f32[8,16,128]{2,1,0:T(8,128)}), f32[8,16,128]{2,1,0:T(8,128)S(1)}, u32[]{:S(2)}, u32[]{:S(2)}) async-start(f32[8,16,128]{2,1,0:T(8,128)} %get-tuple-element.117), calls=%async_computation.10 | async-start | bytes 131072 | tf_op jit(solution)/shard_map/all_to_all | solution.py:705
  121.6 3.9 %collective-permute-start.20 = (f32[2,16,128]{2,1,0:T(8,128)S(1)}, f32[2,16,128]{2,1,0:T(8,128)S(1)}, u32[]{:S(2)}, u32[]{:S(2)}) collective-permute-start(f32[2,16,128]{2,1,0:T(8,128)S(1)} %get-tuple-element.118), channel_id=1, source_target_pairs={{0,1},{1,0},{2,3},{3,2},{4,5},{5,4},{6,7},{7,6},{8,9},{9,8},{10,11... | collective-permute-start | bytes 49160 | tf_op jit(solution)/shard_map/ppermute | solution.py:700
  127.6 15.1 %all_to_all.60.sums_ref = f32[32,1,128]{2,1,0:T(1,128)S(1)} all-to-all(f32[32,1,128]{2,1,0:T(1,128)S(1)} %shard_map.142), channel_id=1, replica_groups=mesh['areal'=8,'layer'=4] {'areal','layer'}, dimensions={0} | all-to-all | bytes 32768 | tf_op jit(solution)/shard_map/all_to_all | solution.py:811
  (90 shorter events, 37.9 us)
Async XLA Ops:
  7.2 10.5 %all-to-all-start = ((f32[8,24,128]{2,1,0:T(8,128)}), f32[8,24,128]{2,1,0:T(8,128)S(1)}, u32[]{:S(2)}, u32[]{:S(2)}) async-start(f32[8,24,128]{2,1,0:T(8,128)} %get-tuple-element.64), calls=%async_computation | async-start | bytes 196608 | tf_op jit(solution)/shard_map/all_to_all | solution.py:705
  12.5 4.1 %collective-permute-start = (f32[5,16,128]{2,1,0:T(8,128)S(1)}, f32[5,16,128]{2,1,0:T(8,128)S(1)}, u32[]{:S(2)}, u32[]{:S(2)}) collective-permute-start(f32[5,16,128]{2,1,0:T(8,128)S(1)} %get-tuple-element.65), channel_id=1, source_target_pairs={{0,1},{1,0},{2,3},{3,2},{4,5},{5,4},{6,7},{7,6},{8,9},{9,8},{10,11... | collective-permute-start | bytes 122888 | tf_op jit(solution)/shard_map/ppermute | solution.py:700
  14.2 2.4 %collective-permute-start.1 = (f32[5,16,128]{2,1,0:T(8,128)S(1)}, f32[5,16,128]{2,1,0:T(8,128)S(1)}, u32[]{:S(2)}, u32[]{:S(2)}) collective-permute-start(f32[5,16,128]{2,1,0:T(8,128)S(1)} %get-tuple-element.66), channel_id=1, source_target_pairs={{1,2},{2,1},{5,6},{6,5},{9,10},{10,9},{13,14},{14,13},{17,18},{18,... | collective-permute-start | bytes 122888 | tf_op jit(solution)/shard_map/ppermute | solution.py:700
  19.6 9.3 %all-to-all-start.1 = ((f32[8,8,128]{2,1,0:T(8,128)}), f32[8,8,128]{2,1,0:T(8,128)S(1)}, u32[]{:S(2)}, u32[]{:S(2)}) async-start(f32[8,8,128]{2,1,0:T(8,128)} %get-tuple-element.71), calls=%async_computation.1 | async-start | bytes 65536 | tf_op jit(solution)/shard_map/all_to_all | solution.py:705
  22.9 5.9 %collective-permute-start.2 = (f32[1,16,128]{2,1,0:T(8,128)S(1)}, f32[1,16,128]{2,1,0:T(8,128)S(1)}, u32[]{:S(2)}, u32[]{:S(2)}) collective-permute-start(f32[1,16,128]{2,1,0:T(8,128)S(1)} %get-tuple-element.72), channel_id=1, source_target_pairs={{0,1},{1,0},{2,3},{3,2},{4,5},{5,4},{6,7},{7,6},{8,9},{9,8},{10,11... | collective-permute-start | bytes 24584 | tf_op jit(solution)/shard_map/ppermute | solution.py:700
  29.9 9.8 %all-to-all-start.2 = ((f32[8,8,128]{2,1,0:T(8,128)}), f32[8,8,128]{2,1,0:T(8,128)S(1)}, u32[]{:S(2)}, u32[]{:S(2)}) async-start(f32[8,8,128]{2,1,0:T(8,128)} %get-tuple-element.79), calls=%async_computation.2 | async-start | bytes 65536 | tf_op jit(solution)/shard_map/all_to_all | solution.py:705
  34.2 5.5 %collective-permute-start.4 = (f32[1,16,128]{2,1,0:T(8,128)S(1)}, f32[1,16,128]{2,1,0:T(8,128)S(1)}, u32[]{:S(2)}, u32[]{:S(2)}) collective-permute-start(f32[1,16,128]{2,1,0:T(8,128)S(1)} %get-tuple-element.80), channel_id=1, source_target_pairs={{0,1},{1,0},{2,3},{3,2},{4,5},{5,4},{6,7},{7,6},{8,9},{9,8},{10,11... | collective-permute-start | bytes 24584 | tf_op jit(solution)/shard_map/ppermute | solution.py:700
  40.8 9.7 %all-to-all-start.3 = ((f32[8,8,128]{2,1,0:T(8,128)}), f32[8,8,128]{2,1,0:T(8,128)S(1)}, u32[]{:S(2)}, u32[]{:S(2)}) async-start(f32[8,8,128]{2,1,0:T(8,128)} %get-tuple-element.83), calls=%async_computation.3 | async-start | bytes 65536 | tf_op jit(solution)/shard_map/all_to_all | solution.py:705
  45.0 5.5 %collective-permute-start.6 = (f32[1,16,128]{2,1,0:T(8,128)S(1)}, f32[1,16,128]{2,1,0:T(8,128)S(1)}, u32[]{:S(2)}, u32[]{:S(2)}) collective-permute-start(f32[1,16,128]{2,1,0:T(8,128)S(1)} %get-tuple-element.84), channel_id=1, source_target_pairs={{0,1},{1,0},{2,3},{3,2},{4,5},{5,4},{6,7},{7,6},{8,9},{9,8},{10,11... | collective-permute-start | bytes 24584 | tf_op jit(solution)/shard_map/ppermute | solution.py:700
  51.7 9.8 %all-to-all-start.4 = ((f32[8,8,128]{2,1,0:T(8,128)}), f32[8,8,128]{2,1,0:T(8,128)S(1)}, u32[]{:S(2)}, u32[]{:S(2)}) async-start(f32[8,8,128]{2,1,0:T(8,128)} %get-tuple-element.88), calls=%async_computation.4 | async-start | bytes 65536 | tf_op jit(solution)/shard_map/all_to_all | solution.py:705
  55.9 5.5 %collective-permute-start.8 = (f32[1,16,128]{2,1,0:T(8,128)S(1)}, f32[1,16,128]{2,1,0:T(8,128)S(1)}, u32[]{:S(2)}, u32[]{:S(2)}) collective-permute-start(f32[1,16,128]{2,1,0:T(8,128)S(1)} %get-tuple-element.89), channel_id=1, source_target_pairs={{0,1},{1,0},{2,3},{3,2},{4,5},{5,4},{6,7},{7,6},{8,9},{9,8},{10,11... | collective-permute-start | bytes 24584 | tf_op jit(solution)/shard_map/ppermute | solution.py:700
  62.7 9.8 %all-to-all-start.5 = ((f32[8,16,128]{2,1,0:T(8,128)}), f32[8,16,128]{2,1,0:T(8,128)S(1)}, u32[]{:S(2)}, u32[]{:S(2)}) async-start(f32[8,16,128]{2,1,0:T(8,128)} %get-tuple-element.94), calls=%async_computation.5 | async-start | bytes 131072 | tf_op jit(solution)/shard_map/all_to_all | solution.py:705
  66.9 5.6 %collective-permute-start.10 = (f32[2,16,128]{2,1,0:T(8,128)S(1)}, f32[2,16,128]{2,1,0:T(8,128)S(1)}, u32[]{:S(2)}, u32[]{:S(2)}) collective-permute-start(f32[2,16,128]{2,1,0:T(8,128)S(1)} %get-tuple-element.95), channel_id=1, source_target_pairs={{0,1},{1,0},{2,3},{3,2},{4,5},{5,4},{6,7},{7,6},{8,9},{9,8},{10,11... | collective-permute-start | bytes 49160 | tf_op jit(solution)/shard_map/ppermute | solution.py:700
  70.8 1.7 %collective-permute-start.11 = (f32[2,16,128]{2,1,0:T(8,128)S(1)}, f32[2,16,128]{2,1,0:T(8,128)S(1)}, u32[]{:S(2)}, u32[]{:S(2)}) collective-permute-start(f32[2,16,128]{2,1,0:T(8,128)S(1)} %get-tuple-element.96), channel_id=1, source_target_pairs={{1,2},{2,1},{5,6},{6,5},{9,10},{10,9},{13,14},{14,13},{17,18},{18,... | collective-permute-start | bytes 49160 | tf_op jit(solution)/shard_map/ppermute | solution.py:700
  73.8 9.7 %all-to-all-start.6 = ((f32[8,8,128]{2,1,0:T(8,128)}), f32[8,8,128]{2,1,0:T(8,128)S(1)}, u32[]{:S(2)}, u32[]{:S(2)}) async-start(f32[8,8,128]{2,1,0:T(8,128)} %get-tuple-element.99), calls=%async_computation.6 | async-start | bytes 65536 | tf_op jit(solution)/shard_map/all_to_all | solution.py:705
  78.0 5.5 %collective-permute-start.12 = (f32[1,16,128]{2,1,0:T(8,128)S(1)}, f32[1,16,128]{2,1,0:T(8,128)S(1)}, u32[]{:S(2)}, u32[]{:S(2)}) collective-permute-start(f32[1,16,128]{2,1,0:T(8,128)S(1)} %get-tuple-element.100), channel_id=1, source_target_pairs={{0,1},{1,0},{2,3},{3,2},{4,5},{5,4},{6,7},{7,6},{8,9},{9,8},{10,11... | collective-permute-start | bytes 24584 | tf_op jit(solution)/shard_map/ppermute | solution.py:700
  84.6 9.7 %all-to-all-start.7 = ((f32[8,8,128]{2,1,0:T(8,128)}), f32[8,8,128]{2,1,0:T(8,128)S(1)}, u32[]{:S(2)}, u32[]{:S(2)}) async-start(f32[8,8,128]{2,1,0:T(8,128)} %get-tuple-element.104), calls=%async_computation.7 | async-start | bytes 65536 | tf_op jit(solution)/shard_map/all_to_all | solution.py:705
  88.8 5.5 %collective-permute-start.14 = (f32[1,16,128]{2,1,0:T(8,128)S(1)}, f32[1,16,128]{2,1,0:T(8,128)S(1)}, u32[]{:S(2)}, u32[]{:S(2)}) collective-permute-start(f32[1,16,128]{2,1,0:T(8,128)S(1)} %get-tuple-element.105), channel_id=1, source_target_pairs={{0,1},{1,0},{2,3},{3,2},{4,5},{5,4},{6,7},{7,6},{8,9},{9,8},{10,11... | collective-permute-start | bytes 24584 | tf_op jit(solution)/shard_map/ppermute | solution.py:700
  95.5 9.7 %all-to-all-start.8 = ((f32[8,8,128]{2,1,0:T(8,128)}), f32[8,8,128]{2,1,0:T(8,128)S(1)}, u32[]{:S(2)}, u32[]{:S(2)}) async-start(f32[8,8,128]{2,1,0:T(8,128)} %get-tuple-element.108), calls=%async_computation.8 | async-start | bytes 65536 | tf_op jit(solution)/shard_map/all_to_all | solution.py:705
  99.7 5.5 %collective-permute-start.16 = (f32[1,16,128]{2,1,0:T(8,128)S(1)}, f32[1,16,128]{2,1,0:T(8,128)S(1)}, u32[]{:S(2)}, u32[]{:S(2)}) collective-permute-start(f32[1,16,128]{2,1,0:T(8,128)S(1)} %get-tuple-element.109), channel_id=1, source_target_pairs={{0,1},{1,0},{2,3},{3,2},{4,5},{5,4},{6,7},{7,6},{8,9},{9,8},{10,11... | collective-permute-start | bytes 24584 | tf_op jit(solution)/shard_map/ppermute | solution.py:700
  106.4 9.7 %all-to-all-start.9 = ((f32[8,8,128]{2,1,0:T(8,128)}), f32[8,8,128]{2,1,0:T(8,128)S(1)}, u32[]{:S(2)}, u32[]{:S(2)}) async-start(f32[8,8,128]{2,1,0:T(8,128)} %get-tuple-element.112), calls=%async_computation.9 | async-start | bytes 65536 | tf_op jit(solution)/shard_map/all_to_all | solution.py:705
  110.6 5.5 %collective-permute-start.18 = (f32[1,16,128]{2,1,0:T(8,128)S(1)}, f32[1,16,128]{2,1,0:T(8,128)S(1)}, u32[]{:S(2)}, u32[]{:S(2)}) collective-permute-start(f32[1,16,128]{2,1,0:T(8,128)S(1)} %get-tuple-element.113), channel_id=1, source_target_pairs={{0,1},{1,0},{2,3},{3,2},{4,5},{5,4},{6,7},{7,6},{8,9},{9,8},{10,11... | collective-permute-start | bytes 24584 | tf_op jit(solution)/shard_map/ppermute | solution.py:700
  117.4 9.8 %all-to-all-start.10 = ((f32[8,16,128]{2,1,0:T(8,128)}), f32[8,16,128]{2,1,0:T(8,128)S(1)}, u32[]{:S(2)}, u32[]{:S(2)}) async-start(f32[8,16,128]{2,1,0:T(8,128)} %get-tuple-element.117), calls=%async_computation.10 | async-start | bytes 131072 | tf_op jit(solution)/shard_map/all_to_all | solution.py:705
  121.6 5.6 %collective-permute-start.20 = (f32[2,16,128]{2,1,0:T(8,128)S(1)}, f32[2,16,128]{2,1,0:T(8,128)S(1)}, u32[]{:S(2)}, u32[]{:S(2)}) collective-permute-start(f32[2,16,128]{2,1,0:T(8,128)S(1)} %get-tuple-element.118), channel_id=1, source_target_pairs={{0,1},{1,0},{2,3},{3,2},{4,5},{5,4},{6,7},{7,6},{8,9},{9,8},{10,11... | collective-permute-start | bytes 49160 | tf_op jit(solution)/shard_map/ppermute | solution.py:700
  (26 other events, 137.2 us)

commit v2 on v1

--- a/solution.py
+++ b/solution.py
@@ -249,54 +249,34 @@
 
 
 def pack_kernel(
-    sz, p_hbm, sat_hbm, act_hbm, trans_hbm, up_hbm, cell_hbm,
-    send_hbm, even_ref, odd_ref, col_ref, row_ref, mine_ref,
-    cell_ref, p_ref, sat_ref, act_ref, trans_ref, up_ref, send_ref, in_sems, sem,
+    sz, state_ref, cell_in,
+    send_hbm, even_ref, odd_ref, col_ref, row_ref, mine_ref, send_ref, sem,
 ):
-    moves = [
-        pltpu.make_async_copy(source, target, in_sems.at[no])
-        for no, (source, target) in enumerate(
-            (
-                (cell_hbm, cell_ref),
-                (p_hbm, p_ref),
-                (sat_hbm, sat_ref),
-                (act_hbm, act_ref),
-                (trans_hbm.at[pl.ds(1, 2)], trans_ref),
-                (up_hbm.at[pl.ds(1, 2)], up_ref),
-            )
-        )
-    ]
-    for move in moves:
-        move.start()
-    moves[0].wait()
-    cell = lane_row(sz, cell_ref)
+    cell = lane_row(sz, cell_in)
     row_start = iota((sz.rows, sz.slots), 0) * sz.nx
     in_row = (cell >= row_start) & (cell < row_start + sz.nx)
     row_hot = jnp.where(in_row, 1.0, 0.0)
     column = cell - jnp.sum(jnp.where(in_row, row_start, 0), axis=0, keepdims=True)
     col_hot = jnp.where(iota((sz.nx, sz.slots), 0) == column, 1.0, 0.0).astype(BF16)
-    for move in moves[1:]:
-        move.wait()
-    pressure = layers_of(sz, p_ref)
-    water = layers_of(sz, sat_ref, 0)
-    gas = layers_of(sz, sat_ref, 1)
-    act = [part.astype(F32) for part in layers_of(sz, act_ref)]
+    pressure, water, gas, act, _, ty, tz, _, uy, uz = [
+        layers_of(sz, state_ref, no) for no in range(10)
+    ]
     four = [pressure, water, gas, act]
     mine = gather_slots(sz, four, row_hot, col_hot)
     write_slots(sz, send_ref, 5 * sz.lz, mine)
-    ty = [t * a for t, a in zip(layers_of(sz, trans_ref, 0), act)]
-    tz = [t * a for t, a in zip(layers_of(sz, trans_ref, 1), act)]
-    uy = [u.astype(F32) for u in layers_of(sz, up_ref, 0)]
-    uz = [u.astype(F32) for u in layers_of(sz, up_ref, 1)]
     write_halo(
         sz, send_ref, even_ref, odd_ref,
         [pressure, water, gas, ty, uy], four, [pressure, water, gas, tz, uz], four,
     )
     out = pltpu.make_async_copy(send_ref, send_hbm, sem)
     out.start()
-    row_ref[...] = row_hot
-    col_ref[...] = col_hot
-    mine_ref[...] = mine
+
+    @meanwhile
+    def _():
+        row_ref[...] = row_hot
+        col_ref[...] = col_hot
+        mine_ref[...] = mine
+
     out.wait()
 
 
@@ -309,6 +289,10 @@
     return out, picked
 
 
+def meanwhile(body):
+    pl.when(lax.axis_index("areal") >= 0)(body)
+
+
 def sweep_ready(sz, guesses, rhs, total_ref, relax, ready_ref):
     for k in range(sz.lz):
         total = weighted(inner_neighbours(sz, guesses, k), total_ref, lambda d: (d, k))
@@ -316,8 +300,8 @@
 
 
 def setup_kernel(
-    sz, recv_ref, even_in, odd_in, p_ref, old_ref, sat_ref, sat_old_ref, pore_ref, trans_ref,
-    up_ref, act_ref, live_ref, fup_ref, ftrans_ref, col_ref, row_ref, mine_ref,
+    sz, recv_ref, even_in, odd_in, state_ref, old_ref, sat_old_ref, pore_ref,
+    live_ref, fup_ref, ftrans_ref, col_ref, row_ref, mine_ref,
     resid_hbm, start_ref, total_ref, image_ref, sat_co_ref, inv_ref, slot_ref,
     rhs_ref, ready_ref, send_hbm, even_ref, odd_ref, resid_ref, send_ref, sems,
 ):
@@ -342,13 +326,8 @@
         col_hot,
     )
     lows, highs = read_halo(sz, recv_ref, even_in, odd_in, 5, 4)
-    pressure = layers_of(sz, p_ref)
-    water = layers_of(sz, sat_ref, 0)
-    gas = layers_of(sz, sat_ref, 1)
-    act = [part.astype(F32) for part in layers_of(sz, act_ref)]
-    trans = [layers_of(sz, trans_ref, axis) for axis in range(3)]
-    flags = [[u.astype(F32) for u in layers_of(sz, up_ref, axis)] for axis in range(3)]
-    carried = [[t * a for t, a in zip(trans[axis], act)] for axis in range(3)]
+    pressure, water, gas, act, *faces = [layers_of(sz, state_ref, no) for no in range(10)]
+    carried, flags = faces[:3], faces[3:]
     lane = iota((sz.ry, sz.nx), 1)
     guesses, relaxes, rights = [], [], []
     for k in range(sz.lz):
@@ -438,14 +417,18 @@
     out, _ = send_fields(
         sz, [guesses], row_hot, col_hot, send_hbm, even_ref, odd_ref, send_ref, sems.at[0]
     )
-    slot_ref[...] = jnp.concatenate(
-        [flow_sum]
-        + flow
-        + [jnp.where(high, 0.0, part) for part in bend]
-        + [jnp.where(high, part, 0.0) for part in bend],
-        axis=0,
-    )
-    sweep_ready(sz, guesses, rights, total_ref, relaxes, ready_ref)
+
+    @meanwhile
+    def _():
+        slot_ref[...] = jnp.concatenate(
+            [flow_sum]
+            + flow
+            + [jnp.where(high, 0.0, part) for part in bend]
+            + [jnp.where(high, part, 0.0) for part in bend],
+            axis=0,
+        )
+        sweep_ready(sz, guesses, rights, total_ref, relaxes, ready_ref)
+
     resid_out.wait()
     out.wait()
 
@@ -474,9 +457,13 @@
     out, _ = send_fields(
         sz, [guesses], row_hot, col_hot, send_hbm, even_ref, odd_ref, send_ref, sem
     )
-    sweep_ready(
-        sz, guesses, layers_of(sz, rhs_ref), total_ref, layers_of(sz, inv_ref, 0), ready_ref
-    )
+
+    @meanwhile
+    def _():
+        sweep_ready(
+            sz, guesses, layers_of(sz, rhs_ref), total_ref, layers_of(sz, inv_ref, 0), ready_ref
+        )
+
     out.wait()
 
 
@@ -492,13 +479,17 @@
     out, _ = send_fields(
         sz, [guesses], row_hot, col_hot, send_hbm, even_ref, odd_ref, send_ref, sem
     )
-    for k in range(sz.lz):
-        guess_ref[k] = guesses[k]
-        near = inner_neighbours(sz, guesses, k)
-        for row in range(3):
-            image_ref[row, k] = image_co_ref[row, k] * guesses[k] - weighted(
-                near, image_co_ref, lambda d: (3 + 6 * row + d, k)
-            )
+
+    @meanwhile
+    def _():
+        for k in range(sz.lz):
+            guess_ref[k] = guesses[k]
+            near = inner_neighbours(sz, guesses, k)
+            for row in range(3):
+                image_ref[row, k] = image_co_ref[row, k] * guesses[k] - weighted(
+                    near, image_co_ref, lambda d: (3 + 6 * row + d, k)
+                )
+
     out.wait()
 
 
@@ -529,22 +520,26 @@
     out, picked = send_fields(
         sz, [water, gas], row_hot, col_hot, send_hbm, even_ref, odd_ref, send_ref, sem
     )
-    picked_ref[...] = picked
-    both = [w + g for w, g in zip(water, gas)]
-    for k in range(sz.lz):
-        moves_ref[0, k] = water[k]
-        moves_ref[1, k] = gas[k]
-        own = (water[k], both[k], gas[k])
-        near_w = inner_neighbours(sz, water, k)
-        near_g = inner_neighbours(sz, gas, k)
-        near = (near_w, [None if w is None else w + g for w, g in zip(near_w, near_g)], near_g)
-        for row in range(3):
-            value = images[k][row] + sat_co_ref[row, k] * own[row]
-            if row == 1:
-                value = value + sat_co_ref[3, k] * water[k]
-            rows_ref[row, k] = value - weighted(
-                near[row], sat_co_ref, lambda d: (4 + 6 * row + d, k)
-            )
+
+    @meanwhile
+    def _():
+        picked_ref[...] = picked
+        both = [w + g for w, g in zip(water, gas)]
+        for k in range(sz.lz):
+            moves_ref[0, k] = water[k]
+            moves_ref[1, k] = gas[k]
+            own = (water[k], both[k], gas[k])
+            near_w = inner_neighbours(sz, water, k)
+            near_g = inner_neighbours(sz, gas, k)
+            near = (near_w, [None if w is None else w + g for w, g in zip(near_w, near_g)], near_g)
+            for row in range(3):
+                value = images[k][row] + sat_co_ref[row, k] * own[row]
+                if row == 1:
+                    value = value + sat_co_ref[3, k] * water[k]
+                rows_ref[row, k] = value - weighted(
+                    near[row], sat_co_ref, lambda d: (4 + 6 * row + d, k)
+                )
+
     out.wait()
 
 
@@ -606,7 +601,11 @@
     out, _ = send_fields(
         sz, [guesses], row_hot, col_hot, send_hbm, even_ref, odd_ref, send_ref, sem
     )
-    sweep_ready(sz, guesses, rights, total_ref, relaxes, ready_ref)
+
+    @meanwhile
+    def _():
+        sweep_ready(sz, guesses, rights, total_ref, relaxes, ready_ref)
+
     out.wait()
 
 
@@ -680,7 +679,7 @@
         update_ref[2, k] = one * moves_one[1, k] + two * moves_two[1, k]
 
 
-def call(kernel, sz, outs, *args, far_in=False, far_out=(), scratch=()):
+def call(kernel, sz, outs, *args, far_in=False, far_out=(), scratch=(), limit=16 * 2**20):
     near = pl.BlockSpec(memory_space=pltpu.VMEM)
     far = pl.BlockSpec(memory_space=pltpu.HBM)
     return pl.pallas_call(
@@ -689,7 +688,7 @@
         in_specs=[far if far_in else near] * len(args),
         out_specs=[far if no in far_out else near for no in range(len(outs))],
         scratch_shapes=list(scratch),
-        compiler_params=pltpu.CompilerParams(vmem_limit_bytes=16 * 2**20),
+        compiler_params=pltpu.CompilerParams(vmem_limit_bytes=limit),
     )(*args)
 
 
@@ -748,24 +747,17 @@
     two_fields = sends(2, 2, 2)
     state = sends(5, 4, 5)
     scalar = (cells, F32)
+    act = active.astype(F32)
+    fields = jnp.concatenate(
+        [pressure[None], saturations, act[None], trans * act, upwind.astype(F32)], axis=0
+    )
     *out, col_hot, row_hot, mine = call(
         pack_kernel,
         sz,
         state + [((sz.nx, sz.slots), BF16), ((sz.rows, sz.slots), F32), ((4, sz.slots), F32)],
-        pressure, saturations, active, trans, upwind, fault_cell,
-        far_in=True,
+        fields, fault_cell,
         far_out=(0,),
-        scratch=[
-            pltpu.VMEM(fault_cell.shape, jnp.int32),
-            pltpu.VMEM(cells, F32),
-            pltpu.VMEM((2,) + cells, F32),
-            pltpu.VMEM(cells, jnp.int32),
-            pltpu.VMEM((2,) + cells, F32),
-            pltpu.VMEM((2,) + cells, jnp.int32),
-            pltpu.VMEM(*state[0]),
-            pltpu.SemaphoreType.DMA((6,)),
-            pltpu.SemaphoreType.DMA,
-        ],
+        scratch=[pltpu.VMEM(*state[0]), pltpu.SemaphoreType.DMA],
     )
     moved = exchange(sz, *out)
     resid, start, total_co, image_co, sat_co, inverse, slots, rhs, ready, *out = call(
@@ -773,8 +765,8 @@
         sz,
         [field(3), field(3), field(6), field(21), field(22), field(3), ((10, sz.slots), F32),
          scalar, scalar] + one_field,
-        *moved, pressure, pressure_old, saturations, saturations_old, pore_volume, trans, upwind,
-        active, fault_live, fault_up, fault_trans, col_hot, row_hot, mine,
+        *moved, fields, pressure_old, saturations_old, pore_volume, fault_live, fault_up,
+        fault_trans, col_hot, row_hot, mine,
         far_out=(0, 9),
         scratch=[
             pltpu.VMEM(*field(3)), pltpu.VMEM(*one_field[0]), pltpu.SemaphoreType.DMA((2,))

time: 145 us -> 143 us (0.986)
  local copies, waits for them, and re-layouts: 4.87 us -> 2.53 us
    unnamed x34 -> x26, local copies, waits for them, and re-layouts: 4.87 us -> 2.53 us
where the time goes in v2:
time: 143 us; the launch traced here: 141 us
  starting transfers between devices  94.8 us (66%)
  blocking collectives  15.1 us (11%)
  Pallas kernels  14.3 us (10%)
  waiting for transfers between devices  12.8 us (9%)
  local copies, waits for them, and re-layouts  2.53 us (2%)
    ppermute x22, starting transfers between devices, pair_swap(): return lax.ppermute(value, 'layer', pairs)  48.2 us
    all_to_all x11, starting transfers between devices, exchange(): lax.all_to_all(send, 'areal', split_axis=0, concat_axis=0, tiled=True)  46.6 us
    all_to_all x1, blocking collectives, local(): lax.all_to_all(sums, ('areal', 'layer'), split_axis=0, concat_axis=0, til...  15.1 us
    pallas_call x13, Pallas kernels, call(): pl.pallas_call(functools.partial(kernel, sz), out_shape=[jax.ShapeDtypeSt...  14.3 us
    ppermute x22, waiting for transfers between devices, pair_swap(): return lax.ppermute(value, 'layer', pairs)  11.7 us
  transfers between devices with their start and end apart: 33, of which 12 were waited for; matrix products, arithmetic and copies ran while one was open for 0% of the time, Pallas kernels for 0%

profile of v2, /device:TPU:0, one launch (start us, length us, event | category | flops | bytes accessed | tf_op | source)
XLA Modules:
  0.0 141.3 jit_solution(9706356747270051226)
XLA Ops:
  5.2 5.3 %all-to-all-start = ((f32[8,24,128]{2,1,0:T(8,128)}), f32[8,24,128]{2,1,0:T(8,128)S(1)}, u32[]{:S(2)}, u32[]{:S(2)}) async-start(f32[8,24,128]{2,1,0:T(8,128)} %get-tuple-element.64), calls=%async_computation | async-start | bytes 196608 | tf_op jit(solution)/shard_map/all_to_all | solution.py:704
  12.9 1.8 %collective-permute-done.even_in = f32[5,16,128]{2,1,0:T(8,128)S(1)} collective-permute-done((f32[5,16,128]{2,1,0:T(8,128)S(1)}, f32[5,16,128]{2,1,0:T(8,128)S(1)}, u32[]{:S(2)}, u32[]{:S(2)}) %collective-permute-start) | collective-permute-done | bytes 40992 | tf_op jit(solution)/shard_map/ppermute | solution.py:699
  15.8 1.7 %shard_map.132 = (f32[3,4,16,128]{3,2,1,0:T(8,128)}, f32[3,4,16,128]{3,2,1,0:T(8,128)S(1)}, f32[6,4,16,128]{3,2,1,0:T(8,128)S(1)}, f32[21,4,16,128]{3,2,1,0:T(8,...) custom-call(f32[8,24,128]{2,1,0:T(8,128)S(1)} %all-to-all-done.recv_, ...), custom_call_target="tpu_custom_call" | custom-call | tf_op jit(solution)/shard_map/pallas_call | solution.py:685
  17.5 3.4 %all-to-all-start.1 = ((f32[8,8,128]{2,1,0:T(8,128)}), f32[8,8,128]{2,1,0:T(8,128)S(1)}, u32[]{:S(2)}, u32[]{:S(2)}) async-start(f32[8,8,128]{2,1,0:T(8,128)} %get-tuple-element.71), calls=%async_computation.1 | async-start | bytes 65536 | tf_op jit(solution)/shard_map/all_to_all | solution.py:704
  20.9 4.3 %collective-permute-start.2 = (f32[1,16,128]{2,1,0:T(8,128)S(1)}, f32[1,16,128]{2,1,0:T(8,128)S(1)}, u32[]{:S(2)}, u32[]{:S(2)}) collective-permute-start(f32[1,16,128]{2,1,0:T(8,128)S(1)} %get-tuple-element.72), channel_id=1, source_target_pairs={{0,1},{1,0},{2,3},{3,2},{4,5},{5,4},{6,7},{7,6},{8,9},{9,8},{10,11... | collective-permute-start | bytes 24584 | tf_op jit(solution)/shard_map/ppermute | solution.py:699
  27.9 4.2 %all-to-all-start.2 = ((f32[8,8,128]{2,1,0:T(8,128)}), f32[8,8,128]{2,1,0:T(8,128)S(1)}, u32[]{:S(2)}, u32[]{:S(2)}) async-start(f32[8,8,128]{2,1,0:T(8,128)} %get-tuple-element.79), calls=%async_computation.2 | async-start | bytes 65536 | tf_op jit(solution)/shard_map/all_to_all | solution.py:704
  32.1 3.9 %collective-permute-start.4 = (f32[1,16,128]{2,1,0:T(8,128)S(1)}, f32[1,16,128]{2,1,0:T(8,128)S(1)}, u32[]{:S(2)}, u32[]{:S(2)}) collective-permute-start(f32[1,16,128]{2,1,0:T(8,128)S(1)} %get-tuple-element.80), channel_id=1, source_target_pairs={{0,1},{1,0},{2,3},{3,2},{4,5},{5,4},{6,7},{7,6},{8,9},{9,8},{10,11... | collective-permute-start | bytes 24584 | tf_op jit(solution)/shard_map/ppermute | solution.py:699
  38.8 4.2 %all-to-all-start.3 = ((f32[8,8,128]{2,1,0:T(8,128)}), f32[8,8,128]{2,1,0:T(8,128)S(1)}, u32[]{:S(2)}, u32[]{:S(2)}) async-start(f32[8,8,128]{2,1,0:T(8,128)} %get-tuple-element.83), calls=%async_computation.3 | async-start | bytes 65536 | tf_op jit(solution)/shard_map/all_to_all | solution.py:704
  43.0 3.9 %collective-permute-start.6 = (f32[1,16,128]{2,1,0:T(8,128)S(1)}, f32[1,16,128]{2,1,0:T(8,128)S(1)}, u32[]{:S(2)}, u32[]{:S(2)}) collective-permute-start(f32[1,16,128]{2,1,0:T(8,128)S(1)} %get-tuple-element.84), channel_id=1, source_target_pairs={{0,1},{1,0},{2,3},{3,2},{4,5},{5,4},{6,7},{7,6},{8,9},{9,8},{10,11... | collective-permute-start | bytes 24584 | tf_op jit(solution)/shard_map/ppermute | solution.py:699
  49.6 4.2 %all-to-all-start.4 = ((f32[8,8,128]{2,1,0:T(8,128)}), f32[8,8,128]{2,1,0:T(8,128)S(1)}, u32[]{:S(2)}, u32[]{:S(2)}) async-start(f32[8,8,128]{2,1,0:T(8,128)} %get-tuple-element.88), calls=%async_computation.4 | async-start | bytes 65536 | tf_op jit(solution)/shard_map/all_to_all | solution.py:704
  53.8 3.9 %collective-permute-start.8 = (f32[1,16,128]{2,1,0:T(8,128)S(1)}, f32[1,16,128]{2,1,0:T(8,128)S(1)}, u32[]{:S(2)}, u32[]{:S(2)}) collective-permute-start(f32[1,16,128]{2,1,0:T(8,128)S(1)} %get-tuple-element.89), channel_id=1, source_target_pairs={{0,1},{1,0},{2,3},{3,2},{4,5},{5,4},{6,7},{7,6},{8,9},{9,8},{10,11... | collective-permute-start | bytes 24584 | tf_op jit(solution)/shard_map/ppermute | solution.py:699
  60.6 4.2 %all-to-all-start.5 = ((f32[8,16,128]{2,1,0:T(8,128)}), f32[8,16,128]{2,1,0:T(8,128)S(1)}, u32[]{:S(2)}, u32[]{:S(2)}) async-start(f32[8,16,128]{2,1,0:T(8,128)} %get-tuple-element.94), calls=%async_computation.5 | async-start | bytes 131072 | tf_op jit(solution)/shard_map/all_to_all | solution.py:704
  64.8 3.9 %collective-permute-start.10 = (f32[2,16,128]{2,1,0:T(8,128)S(1)}, f32[2,16,128]{2,1,0:T(8,128)S(1)}, u32[]{:S(2)}, u32[]{:S(2)}) collective-permute-start(f32[2,16,128]{2,1,0:T(8,128)S(1)} %get-tuple-element.95), channel_id=1, source_target_pairs={{0,1},{1,0},{2,3},{3,2},{4,5},{5,4},{6,7},{7,6},{8,9},{9,8},{10,11... | collective-permute-start | bytes 49160 | tf_op jit(solution)/shard_map/ppermute | solution.py:699
  71.6 4.2 %all-to-all-start.6 = ((f32[8,8,128]{2,1,0:T(8,128)}), f32[8,8,128]{2,1,0:T(8,128)S(1)}, u32[]{:S(2)}, u32[]{:S(2)}) async-start(f32[8,8,128]{2,1,0:T(8,128)} %get-tuple-element.99), calls=%async_computation.6 | async-start | bytes 65536 | tf_op jit(solution)/shard_map/all_to_all | solution.py:704
  75.8 3.9 %collective-permute-start.12 = (f32[1,16,128]{2,1,0:T(8,128)S(1)}, f32[1,16,128]{2,1,0:T(8,128)S(1)}, u32[]{:S(2)}, u32[]{:S(2)}) collective-permute-start(f32[1,16,128]{2,1,0:T(8,128)S(1)} %get-tuple-element.100), channel_id=1, source_target_pairs={{0,1},{1,0},{2,3},{3,2},{4,5},{5,4},{6,7},{7,6},{8,9},{9,8},{10,11... | collective-permute-start | bytes 24584 | tf_op jit(solution)/shard_map/ppermute | solution.py:699
  82.5 4.2 %all-to-all-start.7 = ((f32[8,8,128]{2,1,0:T(8,128)}), f32[8,8,128]{2,1,0:T(8,128)S(1)}, u32[]{:S(2)}, u32[]{:S(2)}) async-start(f32[8,8,128]{2,1,0:T(8,128)} %get-tuple-element.104), calls=%async_computation.7 | async-start | bytes 65536 | tf_op jit(solution)/shard_map/all_to_all | solution.py:704
  86.7 3.9 %collective-permute-start.14 = (f32[1,16,128]{2,1,0:T(8,128)S(1)}, f32[1,16,128]{2,1,0:T(8,128)S(1)}, u32[]{:S(2)}, u32[]{:S(2)}) collective-permute-start(f32[1,16,128]{2,1,0:T(8,128)S(1)} %get-tuple-element.105), channel_id=1, source_target_pairs={{0,1},{1,0},{2,3},{3,2},{4,5},{5,4},{6,7},{7,6},{8,9},{9,8},{10,11... | collective-permute-start | bytes 24584 | tf_op jit(solution)/shard_map/ppermute | solution.py:699
  93.3 4.2 %all-to-all-start.8 = ((f32[8,8,128]{2,1,0:T(8,128)}), f32[8,8,128]{2,1,0:T(8,128)S(1)}, u32[]{:S(2)}, u32[]{:S(2)}) async-start(f32[8,8,128]{2,1,0:T(8,128)} %get-tuple-element.108), calls=%async_computation.8 | async-start | bytes 65536 | tf_op jit(solution)/shard_map/all_to_all | solution.py:704
  97.5 3.9 %collective-permute-start.16 = (f32[1,16,128]{2,1,0:T(8,128)S(1)}, f32[1,16,128]{2,1,0:T(8,128)S(1)}, u32[]{:S(2)}, u32[]{:S(2)}) collective-permute-start(f32[1,16,128]{2,1,0:T(8,128)S(1)} %get-tuple-element.109), channel_id=1, source_target_pairs={{0,1},{1,0},{2,3},{3,2},{4,5},{5,4},{6,7},{7,6},{8,9},{9,8},{10,11... | collective-permute-start | bytes 24584 | tf_op jit(solution)/shard_map/ppermute | solution.py:699
  104.2 4.2 %all-to-all-start.9 = ((f32[8,8,128]{2,1,0:T(8,128)}), f32[8,8,128]{2,1,0:T(8,128)S(1)}, u32[]{:S(2)}, u32[]{:S(2)}) async-start(f32[8,8,128]{2,1,0:T(8,128)} %get-tuple-element.112), calls=%async_computation.9 | async-start | bytes 65536 | tf_op jit(solution)/shard_map/all_to_all | solution.py:704
  108.4 3.9 %collective-permute-start.18 = (f32[1,16,128]{2,1,0:T(8,128)S(1)}, f32[1,16,128]{2,1,0:T(8,128)S(1)}, u32[]{:S(2)}, u32[]{:S(2)}) collective-permute-start(f32[1,16,128]{2,1,0:T(8,128)S(1)} %get-tuple-element.113), channel_id=1, source_target_pairs={{0,1},{1,0},{2,3},{3,2},{4,5},{5,4},{6,7},{7,6},{8,9},{9,8},{10,11... | collective-permute-start | bytes 24584 | tf_op jit(solution)/shard_map/ppermute | solution.py:699
  115.1 4.2 %all-to-all-start.10 = ((f32[8,16,128]{2,1,0:T(8,128)}), f32[8,16,128]{2,1,0:T(8,128)S(1)}, u32[]{:S(2)}, u32[]{:S(2)}) async-start(f32[8,16,128]{2,1,0:T(8,128)} %get-tuple-element.117), calls=%async_computation.10 | async-start | bytes 131072 | tf_op jit(solution)/shard_map/all_to_all | solution.py:704
  119.4 3.9 %collective-permute-start.20 = (f32[2,16,128]{2,1,0:T(8,128)S(1)}, f32[2,16,128]{2,1,0:T(8,128)S(1)}, u32[]{:S(2)}, u32[]{:S(2)}) collective-permute-start(f32[2,16,128]{2,1,0:T(8,128)S(1)} %get-tuple-element.118), channel_id=1, source_target_pairs={{0,1},{1,0},{2,3},{3,2},{4,5},{5,4},{6,7},{7,6},{8,9},{9,8},{10,11... | collective-permute-start | bytes 49160 | tf_op jit(solution)/shard_map/ppermute | solution.py:699
  125.4 15.1 %all_to_all.60.sums_ref = f32[32,1,128]{2,1,0:T(1,128)S(1)} all-to-all(f32[32,1,128]{2,1,0:T(1,128)S(1)} %shard_map.142), channel_id=1, replica_groups=mesh['areal'=8,'layer'=4] {'areal','layer'}, dimensions={0} | all-to-all | bytes 32768 | tf_op jit(solution)/shard_map/all_to_all | solution.py:803
  (86 shorter events, 35.8 us)
Async XLA Ops:
  5.2 10.5 %all-to-all-start = ((f32[8,24,128]{2,1,0:T(8,128)}), f32[8,24,128]{2,1,0:T(8,128)S(1)}, u32[]{:S(2)}, u32[]{:S(2)}) async-start(f32[8,24,128]{2,1,0:T(8,128)} %get-tuple-element.64), calls=%async_computation | async-start | bytes 196608 | tf_op jit(solution)/shard_map/all_to_all | solution.py:704
  10.6 4.1 %collective-permute-start = (f32[5,16,128]{2,1,0:T(8,128)S(1)}, f32[5,16,128]{2,1,0:T(8,128)S(1)}, u32[]{:S(2)}, u32[]{:S(2)}) collective-permute-start(f32[5,16,128]{2,1,0:T(8,128)S(1)} %get-tuple-element.65), channel_id=1, source_target_pairs={{0,1},{1,0},{2,3},{3,2},{4,5},{5,4},{6,7},{7,6},{8,9},{9,8},{10,11... | collective-permute-start | bytes 122888 | tf_op jit(solution)/shard_map/ppermute | solution.py:699
  12.3 2.4 %collective-permute-start.1 = (f32[5,16,128]{2,1,0:T(8,128)S(1)}, f32[5,16,128]{2,1,0:T(8,128)S(1)}, u32[]{:S(2)}, u32[]{:S(2)}) collective-permute-start(f32[5,16,128]{2,1,0:T(8,128)S(1)} %get-tuple-element.66), channel_id=1, source_target_pairs={{1,2},{2,1},{5,6},{6,5},{9,10},{10,9},{13,14},{14,13},{17,18},{18,... | collective-permute-start | bytes 122888 | tf_op jit(solution)/shard_map/ppermute | solution.py:699
  17.5 9.3 %all-to-all-start.1 = ((f32[8,8,128]{2,1,0:T(8,128)}), f32[8,8,128]{2,1,0:T(8,128)S(1)}, u32[]{:S(2)}, u32[]{:S(2)}) async-start(f32[8,8,128]{2,1,0:T(8,128)} %get-tuple-element.71), calls=%async_computation.1 | async-start | bytes 65536 | tf_op jit(solution)/shard_map/all_to_all | solution.py:704
  20.9 5.9 %collective-permute-start.2 = (f32[1,16,128]{2,1,0:T(8,128)S(1)}, f32[1,16,128]{2,1,0:T(8,128)S(1)}, u32[]{:S(2)}, u32[]{:S(2)}) collective-permute-start(f32[1,16,128]{2,1,0:T(8,128)S(1)} %get-tuple-element.72), channel_id=1, source_target_pairs={{0,1},{1,0},{2,3},{3,2},{4,5},{5,4},{6,7},{7,6},{8,9},{9,8},{10,11... | collective-permute-start | bytes 24584 | tf_op jit(solution)/shard_map/ppermute | solution.py:699
  27.9 9.8 %all-to-all-start.2 = ((f32[8,8,128]{2,1,0:T(8,128)}), f32[8,8,128]{2,1,0:T(8,128)S(1)}, u32[]{:S(2)}, u32[]{:S(2)}) async-start(f32[8,8,128]{2,1,0:T(8,128)} %get-tuple-element.79), calls=%async_computation.2 | async-start | bytes 65536 | tf_op jit(solution)/shard_map/all_to_all | solution.py:704
  32.1 5.5 %collective-permute-start.4 = (f32[1,16,128]{2,1,0:T(8,128)S(1)}, f32[1,16,128]{2,1,0:T(8,128)S(1)}, u32[]{:S(2)}, u32[]{:S(2)}) collective-permute-start(f32[1,16,128]{2,1,0:T(8,128)S(1)} %get-tuple-element.80), channel_id=1, source_target_pairs={{0,1},{1,0},{2,3},{3,2},{4,5},{5,4},{6,7},{7,6},{8,9},{9,8},{10,11... | collective-permute-start | bytes 24584 | tf_op jit(solution)/shard_map/ppermute | solution.py:699
  38.8 9.8 %all-to-all-start.3 = ((f32[8,8,128]{2,1,0:T(8,128)}), f32[8,8,128]{2,1,0:T(8,128)S(1)}, u32[]{:S(2)}, u32[]{:S(2)}) async-start(f32[8,8,128]{2,1,0:T(8,128)} %get-tuple-element.83), calls=%async_computation.3 | async-start | bytes 65536 | tf_op jit(solution)/shard_map/all_to_all | solution.py:704
  43.0 5.5 %collective-permute-start.6 = (f32[1,16,128]{2,1,0:T(8,128)S(1)}, f32[1,16,128]{2,1,0:T(8,128)S(1)}, u32[]{:S(2)}, u32[]{:S(2)}) collective-permute-start(f32[1,16,128]{2,1,0:T(8,128)S(1)} %get-tuple-element.84), channel_id=1, source_target_pairs={{0,1},{1,0},{2,3},{3,2},{4,5},{5,4},{6,7},{7,6},{8,9},{9,8},{10,11... | collective-permute-start | bytes 24584 | tf_op jit(solution)/shard_map/ppermute | solution.py:699
  49.6 9.7 %all-to-all-start.4 = ((f32[8,8,128]{2,1,0:T(8,128)}), f32[8,8,128]{2,1,0:T(8,128)S(1)}, u32[]{:S(2)}, u32[]{:S(2)}) async-start(f32[8,8,128]{2,1,0:T(8,128)} %get-tuple-element.88), calls=%async_computation.4 | async-start | bytes 65536 | tf_op jit(solution)/shard_map/all_to_all | solution.py:704
  53.8 5.5 %collective-permute-start.8 = (f32[1,16,128]{2,1,0:T(8,128)S(1)}, f32[1,16,128]{2,1,0:T(8,128)S(1)}, u32[]{:S(2)}, u32[]{:S(2)}) collective-permute-start(f32[1,16,128]{2,1,0:T(8,128)S(1)} %get-tuple-element.89), channel_id=1, source_target_pairs={{0,1},{1,0},{2,3},{3,2},{4,5},{5,4},{6,7},{7,6},{8,9},{9,8},{10,11... | collective-permute-start | bytes 24584 | tf_op jit(solution)/shard_map/ppermute | solution.py:699
  60.6 9.8 %all-to-all-start.5 = ((f32[8,16,128]{2,1,0:T(8,128)}), f32[8,16,128]{2,1,0:T(8,128)S(1)}, u32[]{:S(2)}, u32[]{:S(2)}) async-start(f32[8,16,128]{2,1,0:T(8,128)} %get-tuple-element.94), calls=%async_computation.5 | async-start | bytes 131072 | tf_op jit(solution)/shard_map/all_to_all | solution.py:704
  64.8 5.6 %collective-permute-start.10 = (f32[2,16,128]{2,1,0:T(8,128)S(1)}, f32[2,16,128]{2,1,0:T(8,128)S(1)}, u32[]{:S(2)}, u32[]{:S(2)}) collective-permute-start(f32[2,16,128]{2,1,0:T(8,128)S(1)} %get-tuple-element.95), channel_id=1, source_target_pairs={{0,1},{1,0},{2,3},{3,2},{4,5},{5,4},{6,7},{7,6},{8,9},{9,8},{10,11... | collective-permute-start | bytes 49160 | tf_op jit(solution)/shard_map/ppermute | solution.py:699
  68.7 1.7 %collective-permute-start.11 = (f32[2,16,128]{2,1,0:T(8,128)S(1)}, f32[2,16,128]{2,1,0:T(8,128)S(1)}, u32[]{:S(2)}, u32[]{:S(2)}) collective-permute-start(f32[2,16,128]{2,1,0:T(8,128)S(1)} %get-tuple-element.96), channel_id=1, source_target_pairs={{1,2},{2,1},{5,6},{6,5},{9,10},{10,9},{13,14},{14,13},{17,18},{18,... | collective-permute-start | bytes 49160 | tf_op jit(solution)/shard_map/ppermute | solution.py:699
  71.6 9.8 %all-to-all-start.6 = ((f32[8,8,128]{2,1,0:T(8,128)}), f32[8,8,128]{2,1,0:T(8,128)S(1)}, u32[]{:S(2)}, u32[]{:S(2)}) async-start(f32[8,8,128]{2,1,0:T(8,128)} %get-tuple-element.99), calls=%async_computation.6 | async-start | bytes 65536 | tf_op jit(solution)/shard_map/all_to_all | solution.py:704
  75.8 5.5 %collective-permute-start.12 = (f32[1,16,128]{2,1,0:T(8,128)S(1)}, f32[1,16,128]{2,1,0:T(8,128)S(1)}, u32[]{:S(2)}, u32[]{:S(2)}) collective-permute-start(f32[1,16,128]{2,1,0:T(8,128)S(1)} %get-tuple-element.100), channel_id=1, source_target_pairs={{0,1},{1,0},{2,3},{3,2},{4,5},{5,4},{6,7},{7,6},{8,9},{9,8},{10,11... | collective-permute-start | bytes 24584 | tf_op jit(solution)/shard_map/ppermute | solution.py:699
  82.5 9.8 %all-to-all-start.7 = ((f32[8,8,128]{2,1,0:T(8,128)}), f32[8,8,128]{2,1,0:T(8,128)S(1)}, u32[]{:S(2)}, u32[]{:S(2)}) async-start(f32[8,8,128]{2,1,0:T(8,128)} %get-tuple-element.104), calls=%async_computation.7 | async-start | bytes 65536 | tf_op jit(solution)/shard_map/all_to_all | solution.py:704
  86.7 5.5 %collective-permute-start.14 = (f32[1,16,128]{2,1,0:T(8,128)S(1)}, f32[1,16,128]{2,1,0:T(8,128)S(1)}, u32[]{:S(2)}, u32[]{:S(2)}) collective-permute-start(f32[1,16,128]{2,1,0:T(8,128)S(1)} %get-tuple-element.105), channel_id=1, source_target_pairs={{0,1},{1,0},{2,3},{3,2},{4,5},{5,4},{6,7},{7,6},{8,9},{9,8},{10,11... | collective-permute-start | bytes 24584 | tf_op jit(solution)/shard_map/ppermute | solution.py:699
  93.3 9.7 %all-to-all-start.8 = ((f32[8,8,128]{2,1,0:T(8,128)}), f32[8,8,128]{2,1,0:T(8,128)S(1)}, u32[]{:S(2)}, u32[]{:S(2)}) async-start(f32[8,8,128]{2,1,0:T(8,128)} %get-tuple-element.108), calls=%async_computation.8 | async-start | bytes 65536 | tf_op jit(solution)/shard_map/all_to_all | solution.py:704
  97.5 5.5 %collective-permute-start.16 = (f32[1,16,128]{2,1,0:T(8,128)S(1)}, f32[1,16,128]{2,1,0:T(8,128)S(1)}, u32[]{:S(2)}, u32[]{:S(2)}) collective-permute-start(f32[1,16,128]{2,1,0:T(8,128)S(1)} %get-tuple-element.109), channel_id=1, source_target_pairs={{0,1},{1,0},{2,3},{3,2},{4,5},{5,4},{6,7},{7,6},{8,9},{9,8},{10,11... | collective-permute-start | bytes 24584 | tf_op jit(solution)/shard_map/ppermute | solution.py:699
  104.2 9.7 %all-to-all-start.9 = ((f32[8,8,128]{2,1,0:T(8,128)}), f32[8,8,128]{2,1,0:T(8,128)S(1)}, u32[]{:S(2)}, u32[]{:S(2)}) async-start(f32[8,8,128]{2,1,0:T(8,128)} %get-tuple-element.112), calls=%async_computation.9 | async-start | bytes 65536 | tf_op jit(solution)/shard_map/all_to_all | solution.py:704
  108.4 5.5 %collective-permute-start.18 = (f32[1,16,128]{2,1,0:T(8,128)S(1)}, f32[1,16,128]{2,1,0:T(8,128)S(1)}, u32[]{:S(2)}, u32[]{:S(2)}) collective-permute-start(f32[1,16,128]{2,1,0:T(8,128)S(1)} %get-tuple-element.113), channel_id=1, source_target_pairs={{0,1},{1,0},{2,3},{3,2},{4,5},{5,4},{6,7},{7,6},{8,9},{9,8},{10,11... | collective-permute-start | bytes 24584 | tf_op jit(solution)/shard_map/ppermute | solution.py:699
  115.1 9.8 %all-to-all-start.10 = ((f32[8,16,128]{2,1,0:T(8,128)}), f32[8,16,128]{2,1,0:T(8,128)S(1)}, u32[]{:S(2)}, u32[]{:S(2)}) async-start(f32[8,16,128]{2,1,0:T(8,128)} %get-tuple-element.117), calls=%async_computation.10 | async-start | bytes 131072 | tf_op jit(solution)/shard_map/all_to_all | solution.py:704
  119.4 5.6 %collective-permute-start.20 = (f32[2,16,128]{2,1,0:T(8,128)S(1)}, f32[2,16,128]{2,1,0:T(8,128)S(1)}, u32[]{:S(2)}, u32[]{:S(2)}) collective-permute-start(f32[2,16,128]{2,1,0:T(8,128)S(1)} %get-tuple-element.118), channel_id=1, source_target_pairs={{0,1},{1,0},{2,3},{3,2},{4,5},{5,4},{6,7},{7,6},{8,9},{9,8},{10,11... | collective-permute-start | bytes 49160 | tf_op jit(solution)/shard_map/ppermute | solution.py:699
  (21 other events, 72.4 us)

commit v3 on v2

--- a/solution.py
+++ b/solution.py
@@ -250,7 +250,7 @@
 
 def pack_kernel(
     sz, state_ref, cell_in,
-    send_hbm, even_ref, odd_ref, col_ref, row_ref, mine_ref, send_ref, sem,
+    send_ref, even_ref, odd_ref, col_ref, row_ref, mine_ref,
 ):
     cell = lane_row(sz, cell_in)
     row_start = iota((sz.rows, sz.slots), 0) * sz.nx
@@ -268,8 +268,6 @@
         sz, send_ref, even_ref, odd_ref,
         [pressure, water, gas, ty, uy], four, [pressure, water, gas, tz, uz], four,
     )
-    out = pltpu.make_async_copy(send_ref, send_hbm, sem)
-    out.start()
 
     @meanwhile
     def _():
@@ -277,20 +275,16 @@
         col_ref[...] = col_hot
         mine_ref[...] = mine
 
-    out.wait()
-
-
-def send_fields(sz, fields, row_hot, col_hot, send_hbm, even_ref, odd_ref, send_ref, sem):
+
+def send_fields(sz, fields, row_hot, col_hot, send_ref, even_ref, odd_ref):
     picked = gather_slots(sz, fields, row_hot, col_hot)
     write_halo(sz, send_ref, even_ref, odd_ref, fields, fields, fields, fields)
     write_slots(sz, send_ref, len(fields) * sz.lz, picked)
-    out = pltpu.make_async_copy(send_ref, send_hbm, sem)
-    out.start()
-    return out, picked
+    return picked
 
 
 def meanwhile(body):
-    pl.when(lax.axis_index("areal") >= 0)(body)
+    body()
 
 
 def sweep_ready(sz, guesses, rhs, total_ref, relax, ready_ref):
@@ -303,7 +297,7 @@
     sz, recv_ref, even_in, odd_in, state_ref, old_ref, sat_old_ref, pore_ref,
     live_ref, fup_ref, ftrans_ref, col_ref, row_ref, mine_ref,
     resid_hbm, start_ref, total_ref, image_ref, sat_co_ref, inv_ref, slot_ref,
-    rhs_ref, ready_ref, send_hbm, even_ref, odd_ref, resid_ref, send_ref, sems,
+    rhs_ref, ready_ref, send_ref, even_ref, odd_ref, resid_ref, sem,
 ):
     row_hot = row_ref[...]
     col_hot = col_ref[...]
@@ -412,10 +406,10 @@
         relaxes.append(relax)
         rights.append(rhs)
         guesses.append(relax * rhs)
-    resid_out = pltpu.make_async_copy(resid_ref, resid_hbm, sems.at[1])
+    resid_out = pltpu.make_async_copy(resid_ref, resid_hbm, sem)
     resid_out.start()
-    out, _ = send_fields(
-        sz, [guesses], row_hot, col_hot, send_hbm, even_ref, odd_ref, send_ref, sems.at[0]
+    send_fields(
+        sz, [guesses], row_hot, col_hot, send_ref, even_ref, odd_ref
     )
 
     @meanwhile
@@ -430,7 +424,6 @@
         sweep_ready(sz, guesses, rights, total_ref, relaxes, ready_ref)
 
     resid_out.wait()
-    out.wait()
 
 
 def next_guess(sz, recv_ref, even_in, odd_in, ready_in, total_ref, inv_ref, slot_ref, row_hot,
@@ -447,15 +440,15 @@
 
 def sweep_kernel(
     sz, recv_ref, even_in, odd_in, ready_in, rhs_ref, total_ref, inv_ref, slot_ref, col_ref,
-    row_ref, ready_ref, send_hbm, even_ref, odd_ref, send_ref, sem,
+    row_ref, ready_ref, send_ref, even_ref, odd_ref,
 ):
     row_hot = row_ref[...]
     col_hot = col_ref[...]
     guesses = next_guess(
         sz, recv_ref, even_in, odd_in, ready_in, total_ref, inv_ref, slot_ref, row_hot, col_hot
     )
-    out, _ = send_fields(
-        sz, [guesses], row_hot, col_hot, send_hbm, even_ref, odd_ref, send_ref, sem
+    send_fields(
+        sz, [guesses], row_hot, col_hot, send_ref, even_ref, odd_ref
     )
 
     @meanwhile
@@ -464,20 +457,18 @@
             sz, guesses, layers_of(sz, rhs_ref), total_ref, layers_of(sz, inv_ref, 0), ready_ref
         )
 
-    out.wait()
-
 
 def last_sweep_kernel(
     sz, recv_ref, even_in, odd_in, ready_in, total_ref, inv_ref, image_co_ref, slot_ref, col_ref,
-    row_ref, guess_ref, image_ref, send_hbm, even_ref, odd_ref, send_ref, sem,
+    row_ref, guess_ref, image_ref, send_ref, even_ref, odd_ref,
 ):
     row_hot = row_ref[...]
     col_hot = col_ref[...]
     guesses = next_guess(
         sz, recv_ref, even_in, odd_in, ready_in, total_ref, inv_ref, slot_ref, row_hot, col_hot
     )
-    out, _ = send_fields(
-        sz, [guesses], row_hot, col_hot, send_hbm, even_ref, odd_ref, send_ref, sem
+    send_fields(
+        sz, [guesses], row_hot, col_hot, send_ref, even_ref, odd_ref
     )
 
     @meanwhile
@@ -490,13 +481,10 @@
                     near, image_co_ref, lambda d: (3 + 6 * row + d, k)
                 )
 
-    out.wait()
-
 
 def second_kernel(
     sz, recv_ref, even_in, odd_in, image_in, vector_ref, image_co_ref, sat_co_ref, inv_ref,
-    slot_ref, col_ref, row_ref, moves_ref, rows_ref, picked_ref, send_hbm, even_ref, odd_ref,
-    send_ref, sem,
+    slot_ref, col_ref, row_ref, moves_ref, rows_ref, picked_ref, send_ref, even_ref, odd_ref,
 ):
     row_hot = row_ref[...]
     col_hot = col_ref[...]
@@ -517,8 +505,8 @@
         images.append(image)
         water.append(inv_ref[1, k] * (vector_ref[0, k] - image[0]))
         gas.append(inv_ref[2, k] * (vector_ref[2, k] - image[2]))
-    out, picked = send_fields(
-        sz, [water, gas], row_hot, col_hot, send_hbm, even_ref, odd_ref, send_ref, sem
+    picked = send_fields(
+        sz, [water, gas], row_hot, col_hot, send_ref, even_ref, odd_ref
     )
 
     @meanwhile
@@ -540,8 +528,6 @@
                     near[row], sat_co_ref, lambda d: (4 + 6 * row + d, k)
                 )
 
-    out.wait()
-
 
 def apply_sat(sz, recv_ref, even_in, odd_in, rows_in, picked_ref, co_ref, slot_ref, col_hot,
               row_hot):
@@ -579,8 +565,7 @@
 
 def next_kernel(
     sz, recv_ref, even_in, odd_in, rows_in, picked_ref, vector_ref, sat_co_ref, total_ref, inv_ref,
-    slot_ref, col_ref, row_ref, shifted_ref, rhs_ref, ready_ref, send_hbm, even_ref, odd_ref,
-    send_ref, sem,
+    slot_ref, col_ref, row_ref, shifted_ref, rhs_ref, ready_ref, send_ref, even_ref, odd_ref,
 ):
     row_hot = row_ref[...]
     col_hot = col_ref[...]
@@ -598,15 +583,13 @@
         rights.append(rhs)
         relaxes.append(relax)
         guesses.append(relax * rhs)
-    out, _ = send_fields(
-        sz, [guesses], row_hot, col_hot, send_hbm, even_ref, odd_ref, send_ref, sem
+    send_fields(
+        sz, [guesses], row_hot, col_hot, send_ref, even_ref, odd_ref
     )
 
     @meanwhile
     def _():
         sweep_ready(sz, guesses, rights, total_ref, relaxes, ready_ref)
-
-    out.wait()
 
 
 def gram_kernel(
@@ -701,7 +684,14 @@
 
 def exchange(sz, send, even, odd):
     return (
-        lax.all_to_all(send, "areal", split_axis=0, concat_axis=0, tiled=True),
+        lax.cond(
+            lax.axis_index("areal") < sz.areal,
+            lambda value: lax.all_to_all(
+                value, "areal", split_axis=0, concat_axis=0, tiled=True
+            ),
+            jnp.zeros_like,
+            send,
+        ),
         pair_swap(sz, even, 0),
         pair_swap(sz, odd, 1),
     )
@@ -737,10 +727,7 @@
         ]
 
     def sender(kernel, outs, to_send, *args):
-        buffers = [pltpu.VMEM(*to_send[0]), pltpu.SemaphoreType.DMA]
-        *kept, send, even, odd = call(
-            kernel, sz, outs + to_send, *args, far_out=(len(outs),), scratch=buffers
-        )
+        *kept, send, even, odd = call(kernel, sz, outs + to_send, *args)
         return *kept, exchange(sz, send, even, odd)
 
     one_field = sends(1, 1, 1)
@@ -756,8 +743,6 @@
         sz,
         state + [((sz.nx, sz.slots), BF16), ((sz.rows, sz.slots), F32), ((4, sz.slots), F32)],
         fields, fault_cell,
-        far_out=(0,),
-        scratch=[pltpu.VMEM(*state[0]), pltpu.SemaphoreType.DMA],
     )
     moved = exchange(sz, *out)
     resid, start, total_co, image_co, sat_co, inverse, slots, rhs, ready, *out = call(
@@ -767,9 +752,9 @@
          scalar, scalar] + one_field,
         *moved, fields, pressure_old, saturations_old, pore_volume, fault_live, fault_up,
         fault_trans, col_hot, row_hot, mine,
-        far_out=(0, 9),
+        far_out=(0,),
         scratch=[
-            pltpu.VMEM(*field(3)), pltpu.VMEM(*one_field[0]), pltpu.SemaphoreType.DMA((2,))
+            pltpu.VMEM(*field(3)), pltpu.SemaphoreType.DMA
         ],
     )
     moved = exchange(sz, *out)

time: 143 us -> 141 us (0.986)
  blocking collectives: 15.1 us -> 91.5 us
  starting transfers between devices: 94.8 us -> 35.6 us
  waiting for transfers between devices: 12.8 us -> 0.06 us
  Pallas kernels: 14.3 us -> 7.98 us
    all_to_all x0 -> x11, blocking collectives: none -> 81.4 us  [exchange(): lax.all_to_all(value, 'areal', split_axis=0, concat_axis=0, tiled=True)]
    all_to_all x11 -> x0, starting transfers between devices: 46.6 us -> none  [exchange(): lax.all_to_all(send, 'areal', split_axis=0, concat_axis=0, tiled=True)]
    ppermute x22, starting transfers between devices: 48.2 us -> 35.6 us  [pair_swap(): return lax.ppermute(value, 'layer', pairs)]
    ppermute x22, waiting for transfers between devices: 11.7 us -> 0.06 us  [pair_swap(): return lax.ppermute(value, 'layer', pairs)]
    pallas_call x13, Pallas kernels: 14.3 us -> 7.98 us  [call(): pl.pallas_call(functools.partial(kernel, sz), out_shape=[jax.ShapeDtypeSt...]
    all_to_all x1, blocking collectives: 15.1 us -> 10.1 us  [local(): lax.all_to_all(sums, ('areal', 'layer'), split_axis=0, concat_axis=0, til...]
  transfers between devices with their start and end apart: 33 -> 22, of which waited for: 12 -> 0; matrix products, arithmetic and copies ran while one was open for 0% -> 0% of each run, Pallas kernels for 0% -> 0%
where the time goes in v3:
time: 141 us; the launch traced here: 140 us
  blocking collectives  91.5 us (65%)
  starting transfers between devices  35.6 us (25%)
  Pallas kernels  7.98 us (6%)
  local copies, waits for them, and re-layouts  3.16 us (2%)
    all_to_all x11, blocking collectives, exchange(): lax.all_to_all(value, 'areal', split_axis=0, concat_axis=0, tiled=True)  81.4 us
    ppermute x22, starting transfers between devices, pair_swap(): return lax.ppermute(value, 'layer', pairs)  35.6 us
    all_to_all x1, blocking collectives, local(): lax.all_to_all(sums, ('areal', 'layer'), split_axis=0, concat_axis=0, til...  10.1 us
    pallas_call x13, Pallas kernels, call(): pl.pallas_call(functools.partial(kernel, sz), out_shape=[jax.ShapeDtypeSt...  7.98 us
    unnamed x26, local copies, waits for them, and re-layouts  3.16 us
  transfers between devices with their start and end apart: 22, of which 0 were waited for; matrix products, arithmetic and copies ran while one was open for 0% of the time, Pallas kernels for 0%

profile of v3, /device:TPU:0, one launch (start us, length us, event | category | flops | bytes accessed | tf_op | source)
XLA Modules:
  0.0 140.1 jit_solution(11146949301447905026)
XLA Ops:
  8.4 8.9 %conditional.11 = (f32[8,24,128]{2,1,0:T(8,128)S(1)}) conditional(s32[]{:T(128)} %convert_element_type.6, () %tuple.74, f32[8,24,128]{2,1,0:T(8,128)S(1)} %get-tuple-element.108), branch_computations={%region_0.0_spmd, %region_1.0_spmd} | conditional | bytes 196616 | solution.py:687
  8.4 8.9 %all_to_all.49 = f32[8,24,128]{2,1,0:T(8,128)S(1)} all-to-all(f32[8,24,128]{2,1,0:T(8,128)S(1)} %param.1), channel_id=1, replica_groups=mesh['areal'=8,'layer'=4] {'areal'}, dimensions={0} | all-to-all | bytes 196608 | tf_op jit(solution)/shard_map/cond/branch_1_fun/all_to_all | solution.py:689
  19.4 4.5 %collective-permute-start.2 = (f32[1,16,128]{2,1,0:T(8,128)S(1)}, f32[1,16,128]{2,1,0:T(8,128)S(1)}, u32[]{:S(2)}, u32[]{:S(2)}) collective-permute-start(f32[1,16,128]{2,1,0:T(8,128)S(1)} %get-tuple-element.116), channel_id=1, source_target_pairs={{0,1},{1,0},{2,3},{3,2},{4,5},{5,4},{6,7},{7,6},{8,9},{9,8},{10,11... | collective-permute-start | bytes 24584 | tf_op jit(solution)/shard_map/ppermute | solution.py:682
  24.5 7.2 %conditional.12 = (f32[8,8,128]{2,1,0:T(8,128)S(1)}) conditional(s32[]{:T(128)} %convert_element_type.6, () %tuple.84, f32[8,8,128]{2,1,0:T(8,128)S(1)} %get-tuple-element.115), branch_computations={%region_2.0_spmd, %region_3.0_spmd} | conditional | bytes 65544 | solution.py:687
  24.5 7.2 %all_to_all.50 = f32[8,8,128]{2,1,0:T(8,128)S(1)} all-to-all(f32[8,8,128]{2,1,0:T(8,128)S(1)} %param.3), channel_id=1, replica_groups=mesh['areal'=8,'layer'=4] {'areal'}, dimensions={0} | all-to-all | bytes 65536 | tf_op jit(solution)/shard_map/cond/branch_1_fun/all_to_all | solution.py:689
  34.2 7.2 %conditional.13 = (f32[8,8,128]{2,1,0:T(8,128)S(1)}) conditional(s32[]{:T(128)} %convert_element_type.6, () %tuple.83, f32[8,8,128]{2,1,0:T(8,128)S(1)} %get-tuple-element.123), branch_computations={%region_4.0_spmd, %region_5.0_spmd} | conditional | bytes 65544 | solution.py:687
  34.2 7.2 %all_to_all.51 = f32[8,8,128]{2,1,0:T(8,128)S(1)} all-to-all(f32[8,8,128]{2,1,0:T(8,128)S(1)} %param.5), channel_id=1, replica_groups=mesh['areal'=8,'layer'=4] {'areal'}, dimensions={0} | all-to-all | bytes 65536 | tf_op jit(solution)/shard_map/cond/branch_1_fun/all_to_all | solution.py:689
  46.0 7.2 %conditional.14 = (f32[8,8,128]{2,1,0:T(8,128)S(1)}) conditional(s32[]{:T(128)} %convert_element_type.6, () %tuple.82, f32[8,8,128]{2,1,0:T(8,128)S(1)} %get-tuple-element.127), branch_computations={%region_6.0_spmd, %region_7.0_spmd} | conditional | bytes 65544 | solution.py:687
  46.0 7.2 %all_to_all.52 = f32[8,8,128]{2,1,0:T(8,128)S(1)} all-to-all(f32[8,8,128]{2,1,0:T(8,128)S(1)} %param.7), channel_id=1, replica_groups=mesh['areal'=8,'layer'=4] {'areal'}, dimensions={0} | all-to-all | bytes 65536 | tf_op jit(solution)/shard_map/cond/branch_1_fun/all_to_all | solution.py:689
  56.4 7.2 %conditional.15 = (f32[8,8,128]{2,1,0:T(8,128)S(1)}) conditional(s32[]{:T(128)} %convert_element_type.6, () %tuple.81, f32[8,8,128]{2,1,0:T(8,128)S(1)} %get-tuple-element.132), branch_computations={%region_8.0_spmd, %region_9.0_spmd} | conditional | bytes 65544 | solution.py:687
  56.4 7.2 %all_to_all.53 = f32[8,8,128]{2,1,0:T(8,128)S(1)} all-to-all(f32[8,8,128]{2,1,0:T(8,128)S(1)} %param.9), channel_id=1, replica_groups=mesh['areal'=8,'layer'=4] {'areal'}, dimensions={0} | all-to-all | bytes 65536 | tf_op jit(solution)/shard_map/cond/branch_1_fun/all_to_all | solution.py:689
  67.6 7.4 %conditional.16 = (f32[8,16,128]{2,1,0:T(8,128)S(1)}) conditional(s32[]{:T(128)} %convert_element_type.6, () %tuple.80, f32[8,16,128]{2,1,0:T(8,128)S(1)} %get-tuple-element.138), branch_computations={%region_10.0_spmd, %region_11.0_spmd} | conditional | bytes 131080 | solution.py:687
  67.6 7.4 %all_to_all.54 = f32[8,16,128]{2,1,0:T(8,128)S(1)} all-to-all(f32[8,16,128]{2,1,0:T(8,128)S(1)} %param.11), channel_id=1, replica_groups=mesh['areal'=8,'layer'=4] {'areal'}, dimensions={0} | all-to-all | bytes 131072 | tf_op jit(solution)/shard_map/cond/branch_1_fun/all_to_all | solution.py:689
  78.3 7.2 %conditional.17 = (f32[8,8,128]{2,1,0:T(8,128)S(1)}) conditional(s32[]{:T(128)} %convert_element_type.6, () %tuple.79, f32[8,8,128]{2,1,0:T(8,128)S(1)} %get-tuple-element.143), branch_computations={%region_12.0_spmd, %region_13.0_spmd} | conditional | bytes 65544 | solution.py:687
  78.3 7.2 %all_to_all.55 = f32[8,8,128]{2,1,0:T(8,128)S(1)} all-to-all(f32[8,8,128]{2,1,0:T(8,128)S(1)} %param.13), channel_id=1, replica_groups=mesh['areal'=8,'layer'=4] {'areal'}, dimensions={0} | all-to-all | bytes 65536 | tf_op jit(solution)/shard_map/cond/branch_1_fun/all_to_all | solution.py:689
  89.3 7.2 %conditional.18 = (f32[8,8,128]{2,1,0:T(8,128)S(1)}) conditional(s32[]{:T(128)} %convert_element_type.6, () %tuple.78, f32[8,8,128]{2,1,0:T(8,128)S(1)} %get-tuple-element.148), branch_computations={%region_14.0_spmd, %region_15.0_spmd} | conditional | bytes 65544 | solution.py:687
  89.3 7.2 %all_to_all.56 = f32[8,8,128]{2,1,0:T(8,128)S(1)} all-to-all(f32[8,8,128]{2,1,0:T(8,128)S(1)} %param.15), channel_id=1, replica_groups=mesh['areal'=8,'layer'=4] {'areal'}, dimensions={0} | all-to-all | bytes 65536 | tf_op jit(solution)/shard_map/cond/branch_1_fun/all_to_all | solution.py:689
  99.8 7.2 %conditional.19 = (f32[8,8,128]{2,1,0:T(8,128)S(1)}) conditional(s32[]{:T(128)} %convert_element_type.6, () %tuple.77, f32[8,8,128]{2,1,0:T(8,128)S(1)} %get-tuple-element.152), branch_computations={%region_16.0_spmd, %region_17.0_spmd} | conditional | bytes 65544 | solution.py:687
  99.8 7.2 %all_to_all.57 = f32[8,8,128]{2,1,0:T(8,128)S(1)} all-to-all(f32[8,8,128]{2,1,0:T(8,128)S(1)} %param.17), channel_id=1, replica_groups=mesh['areal'=8,'layer'=4] {'areal'}, dimensions={0} | all-to-all | bytes 65536 | tf_op jit(solution)/shard_map/cond/branch_1_fun/all_to_all | solution.py:689
  110.8 7.2 %conditional.20 = (f32[8,8,128]{2,1,0:T(8,128)S(1)}) conditional(s32[]{:T(128)} %convert_element_type.6, () %tuple.76, f32[8,8,128]{2,1,0:T(8,128)S(1)} %get-tuple-element.156), branch_computations={%region_18.0_spmd, %region_19.0_spmd} | conditional | bytes 65544 | solution.py:687
  110.8 7.2 %all_to_all.58 = f32[8,8,128]{2,1,0:T(8,128)S(1)} all-to-all(f32[8,8,128]{2,1,0:T(8,128)S(1)} %param.19), channel_id=1, replica_groups=mesh['areal'=8,'layer'=4] {'areal'}, dimensions={0} | all-to-all | bytes 65536 | tf_op jit(solution)/shard_map/cond/branch_1_fun/all_to_all | solution.py:689
  121.4 7.4 %conditional.21 = (f32[8,16,128]{2,1,0:T(8,128)S(1)}) conditional(s32[]{:T(128)} %convert_element_type.6, () %tuple.75, f32[8,16,128]{2,1,0:T(8,128)S(1)} %get-tuple-element.161), branch_computations={%region_20.0_spmd, %region_21.0_spmd} | conditional | bytes 131080 | solution.py:687
  121.4 7.4 %all_to_all.59 = f32[8,16,128]{2,1,0:T(8,128)S(1)} all-to-all(f32[8,16,128]{2,1,0:T(8,128)S(1)} %param.21), channel_id=1, replica_groups=mesh['areal'=8,'layer'=4] {'areal'}, dimensions={0} | all-to-all | bytes 131072 | tf_op jit(solution)/shard_map/cond/branch_1_fun/all_to_all | solution.py:689
  129.2 10.1 %all_to_all.60.sums_ref = f32[32,1,128]{2,1,0:T(1,128)S(1)} all-to-all(f32[32,1,128]{2,1,0:T(1,128)S(1)} %shard_map.142), channel_id=1, replica_groups=mesh['areal'=8,'layer'=4] {'areal','layer'}, dimensions={0} | all-to-all | bytes 32768 | tf_op jit(solution)/shard_map/all_to_all | solution.py:788
  (86 shorter events, 43.1 us)
Async XLA Ops:
  4.6 12.7 %collective-permute-start = (f32[5,16,128]{2,1,0:T(8,128)S(1)}, f32[5,16,128]{2,1,0:T(8,128)S(1)}, u32[]{:S(2)}, u32[]{:S(2)}) collective-permute-start(f32[5,16,128]{2,1,0:T(8,128)S(1)} %get-tuple-element.109), channel_id=1, source_target_pairs={{0,1},{1,0},{2,3},{3,2},{4,5},{5,4},{6,7},{7,6},{8,9},{9,8},{10,11... | collective-permute-start | bytes 122888 | tf_op jit(solution)/shard_map/ppermute | solution.py:682
  7.7 9.6 %collective-permute-start.1 = (f32[5,16,128]{2,1,0:T(8,128)S(1)}, f32[5,16,128]{2,1,0:T(8,128)S(1)}, u32[]{:S(2)}, u32[]{:S(2)}) collective-permute-start(f32[5,16,128]{2,1,0:T(8,128)S(1)} %get-tuple-element.110), channel_id=1, source_target_pairs={{1,2},{2,1},{5,6},{6,5},{9,10},{10,9},{13,14},{14,13},{17,18},{18,... | collective-permute-start | bytes 122888 | tf_op jit(solution)/shard_map/ppermute | solution.py:682
  8.3 8.9 %copy-start = (f32[2,4,16,128]{3,2,1,0:T(8,128)S(1)}, f32[2,4,16,128]{3,2,1,0:T(8,128)}, u32[]{:S(2)}) copy-start(f32[2,4,16,128]{3,2,1,0:T(8,128)} %sat_old_ref.1) | copy-start | bytes 196612
  8.4 8.9 %copy-start.1 = (f32[4,16,128]{2,1,0:T(8,128)S(1)}, f32[4,16,128]{2,1,0:T(8,128)}, u32[]{:S(2)}) copy-start(f32[4,16,128]{2,1,0:T(8,128)} %old_ref.1) | copy-start | bytes 98308
  19.4 12.3 %collective-permute-start.2 = (f32[1,16,128]{2,1,0:T(8,128)S(1)}, f32[1,16,128]{2,1,0:T(8,128)S(1)}, u32[]{:S(2)}, u32[]{:S(2)}) collective-permute-start(f32[1,16,128]{2,1,0:T(8,128)S(1)} %get-tuple-element.116), channel_id=1, source_target_pairs={{0,1},{1,0},{2,3},{3,2},{4,5},{5,4},{6,7},{7,6},{8,9},{9,8},{10,11... | collective-permute-start | bytes 24584 | tf_op jit(solution)/shard_map/ppermute | solution.py:682
  23.9 7.9 %collective-permute-start.3 = (f32[1,16,128]{2,1,0:T(8,128)S(1)}, f32[1,16,128]{2,1,0:T(8,128)S(1)}, u32[]{:S(2)}, u32[]{:S(2)}) collective-permute-start(f32[1,16,128]{2,1,0:T(8,128)S(1)} %get-tuple-element.117), channel_id=1, source_target_pairs={{1,2},{2,1},{5,6},{6,5},{9,10},{10,9},{13,14},{14,13},{17,18},{18,... | collective-permute-start | bytes 24584 | tf_op jit(solution)/shard_map/ppermute | solution.py:682
  32.2 9.2 %collective-permute-start.4 = (f32[1,16,128]{2,1,0:T(8,128)S(1)}, f32[1,16,128]{2,1,0:T(8,128)S(1)}, u32[]{:S(2)}, u32[]{:S(2)}) collective-permute-start(f32[1,16,128]{2,1,0:T(8,128)S(1)} %get-tuple-element.124), channel_id=1, source_target_pairs={{0,1},{1,0},{2,3},{3,2},{4,5},{5,4},{6,7},{7,6},{8,9},{9,8},{10,11... | collective-permute-start | bytes 24584 | tf_op jit(solution)/shard_map/ppermute | solution.py:682
  33.6 7.9 %collective-permute-start.5 = (f32[1,16,128]{2,1,0:T(8,128)S(1)}, f32[1,16,128]{2,1,0:T(8,128)S(1)}, u32[]{:S(2)}, u32[]{:S(2)}) collective-permute-start(f32[1,16,128]{2,1,0:T(8,128)S(1)} %get-tuple-element.125), channel_id=1, source_target_pairs={{1,2},{2,1},{5,6},{6,5},{9,10},{10,9},{13,14},{14,13},{17,18},{18,... | collective-permute-start | bytes 24584 | tf_op jit(solution)/shard_map/ppermute | solution.py:682
  42.0 11.2 %collective-permute-start.6 = (f32[1,16,128]{2,1,0:T(8,128)S(1)}, f32[1,16,128]{2,1,0:T(8,128)S(1)}, u32[]{:S(2)}, u32[]{:S(2)}) collective-permute-start(f32[1,16,128]{2,1,0:T(8,128)S(1)} %get-tuple-element.128), channel_id=1, source_target_pairs={{0,1},{1,0},{2,3},{3,2},{4,5},{5,4},{6,7},{7,6},{8,9},{9,8},{10,11... | collective-permute-start | bytes 24584 | tf_op jit(solution)/shard_map/ppermute | solution.py:682
  45.3 7.9 %collective-permute-start.7 = (f32[1,16,128]{2,1,0:T(8,128)S(1)}, f32[1,16,128]{2,1,0:T(8,128)S(1)}, u32[]{:S(2)}, u32[]{:S(2)}) collective-permute-start(f32[1,16,128]{2,1,0:T(8,128)S(1)} %get-tuple-element.129), channel_id=1, source_target_pairs={{1,2},{2,1},{5,6},{6,5},{9,10},{10,9},{13,14},{14,13},{17,18},{18,... | collective-permute-start | bytes 24584 | tf_op jit(solution)/shard_map/ppermute | solution.py:682
  53.7 9.9 %collective-permute-start.8 = (f32[1,16,128]{2,1,0:T(8,128)S(1)}, f32[1,16,128]{2,1,0:T(8,128)S(1)}, u32[]{:S(2)}, u32[]{:S(2)}) collective-permute-start(f32[1,16,128]{2,1,0:T(8,128)S(1)} %get-tuple-element.133), channel_id=1, source_target_pairs={{0,1},{1,0},{2,3},{3,2},{4,5},{5,4},{6,7},{7,6},{8,9},{9,8},{10,11... | collective-permute-start | bytes 24584 | tf_op jit(solution)/shard_map/ppermute | solution.py:682
  55.8 7.9 %collective-permute-start.9 = (f32[1,16,128]{2,1,0:T(8,128)S(1)}, f32[1,16,128]{2,1,0:T(8,128)S(1)}, u32[]{:S(2)}, u32[]{:S(2)}) collective-permute-start(f32[1,16,128]{2,1,0:T(8,128)S(1)} %get-tuple-element.134), channel_id=1, source_target_pairs={{1,2},{2,1},{5,6},{6,5},{9,10},{10,9},{13,14},{14,13},{17,18},{18,... | collective-permute-start | bytes 24584 | tf_op jit(solution)/shard_map/ppermute | solution.py:682
  64.3 10.7 %collective-permute-start.10 = (f32[2,16,128]{2,1,0:T(8,128)S(1)}, f32[2,16,128]{2,1,0:T(8,128)S(1)}, u32[]{:S(2)}, u32[]{:S(2)}) collective-permute-start(f32[2,16,128]{2,1,0:T(8,128)S(1)} %get-tuple-element.139), channel_id=1, source_target_pairs={{0,1},{1,0},{2,3},{3,2},{4,5},{5,4},{6,7},{7,6},{8,9},{9,8},{10,11... | collective-permute-start | bytes 49160 | tf_op jit(solution)/shard_map/ppermute | solution.py:682
  66.9 8.1 %collective-permute-start.11 = (f32[2,16,128]{2,1,0:T(8,128)S(1)}, f32[2,16,128]{2,1,0:T(8,128)S(1)}, u32[]{:S(2)}, u32[]{:S(2)}) collective-permute-start(f32[2,16,128]{2,1,0:T(8,128)S(1)} %get-tuple-element.140), channel_id=1, source_target_pairs={{1,2},{2,1},{5,6},{6,5},{9,10},{10,9},{13,14},{14,13},{17,18},{18,... | collective-permute-start | bytes 49160 | tf_op jit(solution)/shard_map/ppermute | solution.py:682
  75.6 9.9 %collective-permute-start.12 = (f32[1,16,128]{2,1,0:T(8,128)S(1)}, f32[1,16,128]{2,1,0:T(8,128)S(1)}, u32[]{:S(2)}, u32[]{:S(2)}) collective-permute-start(f32[1,16,128]{2,1,0:T(8,128)S(1)} %get-tuple-element.144), channel_id=1, source_target_pairs={{0,1},{1,0},{2,3},{3,2},{4,5},{5,4},{6,7},{7,6},{8,9},{9,8},{10,11... | collective-permute-start | bytes 24584 | tf_op jit(solution)/shard_map/ppermute | solution.py:682
  77.6 7.9 %collective-permute-start.13 = (f32[1,16,128]{2,1,0:T(8,128)S(1)}, f32[1,16,128]{2,1,0:T(8,128)S(1)}, u32[]{:S(2)}, u32[]{:S(2)}) collective-permute-start(f32[1,16,128]{2,1,0:T(8,128)S(1)} %get-tuple-element.145), channel_id=1, source_target_pairs={{1,2},{2,1},{5,6},{6,5},{9,10},{10,9},{13,14},{14,13},{17,18},{18,... | collective-permute-start | bytes 24584 | tf_op jit(solution)/shard_map/ppermute | solution.py:682
  86.0 10.5 %collective-permute-start.14 = (f32[1,16,128]{2,1,0:T(8,128)S(1)}, f32[1,16,128]{2,1,0:T(8,128)S(1)}, u32[]{:S(2)}, u32[]{:S(2)}) collective-permute-start(f32[1,16,128]{2,1,0:T(8,128)S(1)} %get-tuple-element.149), channel_id=1, source_target_pairs={{0,1},{1,0},{2,3},{3,2},{4,5},{5,4},{6,7},{7,6},{8,9},{9,8},{10,11... | collective-permute-start | bytes 24584 | tf_op jit(solution)/shard_map/ppermute | solution.py:682
  88.7 7.9 %collective-permute-start.15 = (f32[1,16,128]{2,1,0:T(8,128)S(1)}, f32[1,16,128]{2,1,0:T(8,128)S(1)}, u32[]{:S(2)}, u32[]{:S(2)}) collective-permute-start(f32[1,16,128]{2,1,0:T(8,128)S(1)} %get-tuple-element.150), channel_id=1, source_target_pairs={{1,2},{2,1},{5,6},{6,5},{9,10},{10,9},{13,14},{14,13},{17,18},{18,... | collective-permute-start | bytes 24584 | tf_op jit(solution)/shard_map/ppermute | solution.py:682
  97.0 9.9 %collective-permute-start.16 = (f32[1,16,128]{2,1,0:T(8,128)S(1)}, f32[1,16,128]{2,1,0:T(8,128)S(1)}, u32[]{:S(2)}, u32[]{:S(2)}) collective-permute-start(f32[1,16,128]{2,1,0:T(8,128)S(1)} %get-tuple-element.153), channel_id=1, source_target_pairs={{0,1},{1,0},{2,3},{3,2},{4,5},{5,4},{6,7},{7,6},{8,9},{9,8},{10,11... | collective-permute-start | bytes 24584 | tf_op jit(solution)/shard_map/ppermute | solution.py:682
  99.1 7.9 %collective-permute-start.17 = (f32[1,16,128]{2,1,0:T(8,128)S(1)}, f32[1,16,128]{2,1,0:T(8,128)S(1)}, u32[]{:S(2)}, u32[]{:S(2)}) collective-permute-start(f32[1,16,128]{2,1,0:T(8,128)S(1)} %get-tuple-element.154), channel_id=1, source_target_pairs={{1,2},{2,1},{5,6},{6,5},{9,10},{10,9},{13,14},{14,13},{17,18},{18,... | collective-permute-start | bytes 24584 | tf_op jit(solution)/shard_map/ppermute | solution.py:682
  107.5 10.5 %collective-permute-start.18 = (f32[1,16,128]{2,1,0:T(8,128)S(1)}, f32[1,16,128]{2,1,0:T(8,128)S(1)}, u32[]{:S(2)}, u32[]{:S(2)}) collective-permute-start(f32[1,16,128]{2,1,0:T(8,128)S(1)} %get-tuple-element.157), channel_id=1, source_target_pairs={{0,1},{1,0},{2,3},{3,2},{4,5},{5,4},{6,7},{7,6},{8,9},{9,8},{10,11... | collective-permute-start | bytes 24584 | tf_op jit(solution)/shard_map/ppermute | solution.py:682
  110.1 7.9 %collective-permute-start.19 = (f32[1,16,128]{2,1,0:T(8,128)S(1)}, f32[1,16,128]{2,1,0:T(8,128)S(1)}, u32[]{:S(2)}, u32[]{:S(2)}) collective-permute-start(f32[1,16,128]{2,1,0:T(8,128)S(1)} %get-tuple-element.158), channel_id=1, source_target_pairs={{1,2},{2,1},{5,6},{6,5},{9,10},{10,9},{13,14},{14,13},{17,18},{18,... | collective-permute-start | bytes 24584 | tf_op jit(solution)/shard_map/ppermute | solution.py:682
  118.6 10.1 %collective-permute-start.20 = (f32[2,16,128]{2,1,0:T(8,128)S(1)}, f32[2,16,128]{2,1,0:T(8,128)S(1)}, u32[]{:S(2)}, u32[]{:S(2)}) collective-permute-start(f32[2,16,128]{2,1,0:T(8,128)S(1)} %get-tuple-element.162), channel_id=1, source_target_pairs={{0,1},{1,0},{2,3},{3,2},{4,5},{5,4},{6,7},{7,6},{8,9},{9,8},{10,11... | collective-permute-start | bytes 49160 | tf_op jit(solution)/shard_map/ppermute | solution.py:682
  120.7 8.1 %collective-permute-start.21 = (f32[2,16,128]{2,1,0:T(8,128)S(1)}, f32[2,16,128]{2,1,0:T(8,128)S(1)}, u32[]{:S(2)}, u32[]{:S(2)}) collective-permute-start(f32[2,16,128]{2,1,0:T(8,128)S(1)} %get-tuple-element.163), channel_id=1, source_target_pairs={{1,2},{2,1},{5,6},{6,5},{9,10},{10,9},{13,14},{14,13},{17,18},{18,... | collective-permute-start | bytes 49160 | tf_op jit(solution)/shard_map/ppermute | solution.py:682
  (10 other events, 32.4 us)

commit v4 on v3

--- a/solution.py
+++ b/solution.py
@@ -249,31 +249,68 @@
 
 
 def pack_kernel(
-    sz, state_ref, cell_in,
-    send_ref, even_ref, odd_ref, col_ref, row_ref, mine_ref,
+    sz, cell_hbm, p_hbm, sat_hbm, act_hbm, trans_hbm, up_hbm, old_hbm, sat_old_hbm, pore_hbm,
+    live_hbm, fup_hbm, ftrans_hbm,
+    send_ref, even_ref, odd_ref, col_ref, row_ref, line_ref, state_ref,
+    cell_ref, act_ref, trans_ref, up_ref, live_ref, fup_ref, ftrans_ref, sems,
 ):
-    cell = lane_row(sz, cell_in)
+    moves = [
+        pltpu.make_async_copy(source, target, sems.at[no])
+        for no, (source, target) in enumerate(
+            (
+                (cell_hbm, cell_ref),
+                (p_hbm, state_ref.at[0]),
+                (sat_hbm, state_ref.at[pl.ds(1, 2)]),
+                (act_hbm, act_ref),
+                (trans_hbm, trans_ref),
+                (up_hbm, up_ref),
+                (live_hbm, live_ref),
+                (fup_hbm, fup_ref),
+                (ftrans_hbm, ftrans_ref),
+                (old_hbm, state_ref.at[10]),
+                (sat_old_hbm, state_ref.at[pl.ds(11, 2)]),
+                (pore_hbm, state_ref.at[13]),
+            )
+        )
+    ]
+    for move in moves:
+        move.start()
+    moves[0].wait()
+    cell = lane_row(sz, cell_ref)
     row_start = iota((sz.rows, sz.slots), 0) * sz.nx
     in_row = (cell >= row_start) & (cell < row_start + sz.nx)
     row_hot = jnp.where(in_row, 1.0, 0.0)
     column = cell - jnp.sum(jnp.where(in_row, row_start, 0), axis=0, keepdims=True)
     col_hot = jnp.where(iota((sz.nx, sz.slots), 0) == column, 1.0, 0.0).astype(BF16)
-    pressure, water, gas, act, _, ty, tz, _, uy, uz = [
-        layers_of(sz, state_ref, no) for no in range(10)
-    ]
+    row_ref[...] = row_hot
+    col_ref[...] = col_hot
+    for move in moves[1:]:
+        move.wait()
+    pressure, water, gas = [layers_of(sz, state_ref, no) for no in range(3)]
+    act = [part.astype(F32) for part in layers_of(sz, act_ref)]
+    put_layers(state_ref, (3,), act)
+    faces = []
+    for axis in range(3):
+        carried = [t * a for t, a in zip(layers_of(sz, trans_ref, axis), act)]
+        flags = [u.astype(F32) for u in layers_of(sz, up_ref, axis)]
+        put_layers(state_ref, (4 + axis,), carried)
+        put_layers(state_ref, (7 + axis,), flags)
+        faces.append((carried, flags))
     four = [pressure, water, gas, act]
     mine = gather_slots(sz, four, row_hot, col_hot)
     write_slots(sz, send_ref, 5 * sz.lz, mine)
     write_halo(
         sz, send_ref, even_ref, odd_ref,
-        [pressure, water, gas, ty, uy], four, [pressure, water, gas, tz, uz], four,
-    )
-
-    @meanwhile
-    def _():
-        row_ref[...] = row_hot
-        col_ref[...] = col_hot
-        mine_ref[...] = mine
+        [pressure, water, gas, *faces[1]], four, [pressure, water, gas, *faces[2]], four,
+    )
+    line_ref[...] = jnp.concatenate(
+        [
+            mine,
+            lane_row(sz, ftrans_ref) * lane_row(sz, live_ref).astype(F32),
+            lane_row(sz, fup_ref).astype(F32),
+        ],
+        axis=0,
+    )
 
 
 def send_fields(sz, fields, row_hot, col_hot, send_ref, even_ref, odd_ref):
@@ -294,18 +331,16 @@
 
 
 def setup_kernel(
-    sz, recv_ref, even_in, odd_in, state_ref, old_ref, sat_old_ref, pore_ref,
-    live_ref, fup_ref, ftrans_ref, col_ref, row_ref, mine_ref,
+    sz, recv_ref, even_in, odd_in, state_ref, line_ref, col_ref, row_ref,
     resid_hbm, start_ref, total_ref, image_ref, sat_co_ref, inv_ref, slot_ref,
     rhs_ref, ready_ref, send_ref, even_ref, odd_ref, resid_ref, sem,
 ):
     row_hot = row_ref[...]
     col_hot = col_ref[...]
-    mine = mine_ref[...]
+    mine = line_ref[0:4]
     their = read_slots(sz, recv_ref, 5 * sz.lz, 4)
-    live = lane_row(sz, live_ref).astype(F32)
-    high = lane_row(sz, fup_ref) > 0
-    tau = lane_row(sz, ftrans_ref) * live * mine[3:4] * their[3:4]
+    high = line_ref[5:6] > 0.5
+    tau = line_ref[4:5] * mine[3:4] * their[3:4]
     drop = their[0:1] - mine[0:1]
     mobile, slopes = mobility(
         jnp.where(high, their[1:2], mine[1:2]), jnp.where(high, their[2:3], mine[2:3])
@@ -320,8 +355,9 @@
         col_hot,
     )
     lows, highs = read_halo(sz, recv_ref, even_in, odd_in, 5, 4)
-    pressure, water, gas, act, *faces = [layers_of(sz, state_ref, no) for no in range(10)]
-    carried, flags = faces[:3], faces[3:]
+    pressure, water, gas, act, *faces = [layers_of(sz, state_ref, no) for no in range(14)]
+    carried, flags = faces[:3], faces[3:6]
+    old, old_waters, old_gases, pores = faces[6:]
     lane = iota((sz.ry, sz.nx), 1)
     guesses, relaxes, rights = [], [], []
     for k in range(sz.lz):
@@ -351,13 +387,13 @@
             flag_z < 0.5,
             flags[2][k] > 0.5,
         )
-        change = pressure[k] - old_ref[k]
+        change = pressure[k] - old[k]
         oil = 1.0 - water[k] - gas[k]
-        old_water = sat_old_ref[0, k]
-        old_gas = sat_old_ref[1, k]
+        old_water = old_waters[k]
+        old_gas = old_gases[k]
         now = (water[k], oil, gas[k])
         before = (old_water, 1.0 - old_water - old_gas, old_gas)
-        pore = pore_ref[k]
+        pore = pores[k]
         store_p = [own_act * pore * c * s for c, s in zip(COMPRESS, now)]
         store_s = [pore * (1.0 + c * change) for c in COMPRESS]
         resid = [
@@ -734,15 +770,25 @@
     two_fields = sends(2, 2, 2)
     state = sends(5, 4, 5)
     scalar = (cells, F32)
-    act = active.astype(F32)
-    fields = jnp.concatenate(
-        [pressure[None], saturations, act[None], trans * act, upwind.astype(F32)], axis=0
-    )
-    *out, col_hot, row_hot, mine = call(
+    inputs = (
+        fault_cell, pressure, saturations, active, trans, upwind, pressure_old, saturations_old,
+        pore_volume, fault_live, fault_up, fault_trans,
+    )
+    *out, col_hot, row_hot, lines, fields = call(
         pack_kernel,
         sz,
-        state + [((sz.nx, sz.slots), BF16), ((sz.rows, sz.slots), F32), ((4, sz.slots), F32)],
-        fields, fault_cell,
+        state
+        + [((sz.nx, sz.slots), BF16), ((sz.rows, sz.slots), F32), ((6, sz.slots), F32), field(14)],
+        *inputs,
+        far_in=True,
+        limit=67043328,
+        scratch=[
+            pltpu.VMEM(value.shape, value.dtype)
+            for value in (
+                fault_cell, active, trans, upwind, fault_live, fault_up, fault_trans
+            )
+        ]
+        + [pltpu.SemaphoreType.DMA((len(inputs),))],
     )
     moved = exchange(sz, *out)
     resid, start, total_co, image_co, sat_co, inverse, slots, rhs, ready, *out = call(
@@ -750,8 +796,7 @@
         sz,
         [field(3), field(3), field(6), field(21), field(22), field(3), ((10, sz.slots), F32),
          scalar, scalar] + one_field,
-        *moved, fields, pressure_old, saturations_old, pore_volume, fault_live, fault_up,
-        fault_trans, col_hot, row_hot, mine,
+        *moved, fields, lines, col_hot, row_hot,
         far_out=(0,),
         scratch=[
             pltpu.VMEM(*field(3)), pltpu.SemaphoreType.DMA

time: 141 us -> 140 us (level)
  local copies, waits for them, and re-layouts: 3.16 us -> 1.02 us
  Pallas kernels: 7.98 us -> 9.91 us
    unnamed x26 -> x8, local copies, waits for them, and re-layouts: 3.16 us -> 1.02 us
    pallas_call x13, Pallas kernels: 7.98 us -> 9.91 us  [call(): pl.pallas_call(functools.partial(kernel, sz), out_shape=[jax.ShapeDtypeSt...]
where the time goes in v4:
time: 140 us; the launch traced here: 139 us
  blocking collectives  91.7 us (66%)
  starting transfers between devices  35.6 us (25%)
  Pallas kernels  9.91 us (7%)
    all_to_all x11, blocking collectives, exchange(): lax.all_to_all(value, 'areal', split_axis=0, concat_axis=0, tiled=True)  81.6 us
    ppermute x22, starting transfers between devices, pair_swap(): return lax.ppermute(value, 'layer', pairs)  35.6 us
    all_to_all x1, blocking collectives, local(): lax.all_to_all(sums, ('areal', 'layer'), split_axis=0, concat_axis=0, til...  10.1 us
    pallas_call x13, Pallas kernels, call(): pl.pallas_call(functools.partial(kernel, sz), out_shape=[jax.ShapeDtypeSt...  9.91 us
  transfers between devices with their start and end apart: 22, of which 0 were waited for; matrix products, arithmetic and copies ran while one was open for 0% of the time, Pallas kernels for 0%

profile of v4, /device:TPU:0, one launch (start us, length us, event | category | flops | bytes accessed | tf_op | source)
XLA Modules:
  0.0 139.3 jit_solution(16261412170181914535)
XLA Ops:
  7.0 9.1 %conditional.11 = (f32[8,24,128]{2,1,0:T(8,128)S(1)}) conditional(s32[]{:T(128)} %convert_element_type.2, () %tuple.74, f32[8,24,128]{2,1,0:T(8,128)} %get-tuple-element.109), branch_computations={%region_0.0_spmd, %region_1.0_spmd} | conditional | bytes 196616 | solution.py:723
  7.0 9.1 %all_to_all.49 = f32[8,24,128]{2,1,0:T(8,128)S(1)} all-to-all(f32[8,24,128]{2,1,0:T(8,128)} %param.1), channel_id=1, replica_groups=mesh['areal'=8,'layer'=4] {'areal'}, dimensions={0} | all-to-all | bytes 196608 | tf_op jit(solution)/shard_map/cond/branch_1_fun/all_to_all | solution.py:725
  18.5 4.5 %collective-permute-start.2 = (f32[1,16,128]{2,1,0:T(8,128)S(1)}, f32[1,16,128]{2,1,0:T(8,128)S(1)}, u32[]{:S(2)}, u32[]{:S(2)}) collective-permute-start(f32[1,16,128]{2,1,0:T(8,128)S(1)} %get-tuple-element.118), channel_id=1, source_target_pairs={{0,1},{1,0},{2,3},{3,2},{4,5},{5,4},{6,7},{7,6},{8,9},{9,8},{10,11... | collective-permute-start | bytes 24584 | tf_op jit(solution)/shard_map/ppermute | solution.py:718
  23.6 7.2 %conditional.12 = (f32[8,8,128]{2,1,0:T(8,128)S(1)}) conditional(s32[]{:T(128)} %convert_element_type.2, () %tuple.84, f32[8,8,128]{2,1,0:T(8,128)S(1)} %get-tuple-element.117), branch_computations={%region_2.0_spmd, %region_3.0_spmd} | conditional | bytes 65544 | solution.py:723
  23.7 7.2 %all_to_all.50 = f32[8,8,128]{2,1,0:T(8,128)S(1)} all-to-all(f32[8,8,128]{2,1,0:T(8,128)S(1)} %param.3), channel_id=1, replica_groups=mesh['areal'=8,'layer'=4] {'areal'}, dimensions={0} | all-to-all | bytes 65536 | tf_op jit(solution)/shard_map/cond/branch_1_fun/all_to_all | solution.py:725
  33.4 7.2 %conditional.13 = (f32[8,8,128]{2,1,0:T(8,128)S(1)}) conditional(s32[]{:T(128)} %convert_element_type.2, () %tuple.83, f32[8,8,128]{2,1,0:T(8,128)S(1)} %get-tuple-element.125), branch_computations={%region_4.0_spmd, %region_5.0_spmd} | conditional | bytes 65544 | solution.py:723
  33.4 7.2 %all_to_all.51 = f32[8,8,128]{2,1,0:T(8,128)S(1)} all-to-all(f32[8,8,128]{2,1,0:T(8,128)S(1)} %param.5), channel_id=1, replica_groups=mesh['areal'=8,'layer'=4] {'areal'}, dimensions={0} | all-to-all | bytes 65536 | tf_op jit(solution)/shard_map/cond/branch_1_fun/all_to_all | solution.py:725
  45.1 7.2 %conditional.14 = (f32[8,8,128]{2,1,0:T(8,128)S(1)}) conditional(s32[]{:T(128)} %convert_element_type.2, () %tuple.82, f32[8,8,128]{2,1,0:T(8,128)S(1)} %get-tuple-element.129), branch_computations={%region_6.0_spmd, %region_7.0_spmd} | conditional | bytes 65544 | solution.py:723
  45.1 7.2 %all_to_all.52 = f32[8,8,128]{2,1,0:T(8,128)S(1)} all-to-all(f32[8,8,128]{2,1,0:T(8,128)S(1)} %param.7), channel_id=1, replica_groups=mesh['areal'=8,'layer'=4] {'areal'}, dimensions={0} | all-to-all | bytes 65536 | tf_op jit(solution)/shard_map/cond/branch_1_fun/all_to_all | solution.py:725
  55.5 7.2 %conditional.15 = (f32[8,8,128]{2,1,0:T(8,128)S(1)}) conditional(s32[]{:T(128)} %convert_element_type.2, () %tuple.81, f32[8,8,128]{2,1,0:T(8,128)S(1)} %get-tuple-element.134), branch_computations={%region_8.0_spmd, %region_9.0_spmd} | conditional | bytes 65544 | solution.py:723
  55.6 7.2 %all_to_all.53 = f32[8,8,128]{2,1,0:T(8,128)S(1)} all-to-all(f32[8,8,128]{2,1,0:T(8,128)S(1)} %param.9), channel_id=1, replica_groups=mesh['areal'=8,'layer'=4] {'areal'}, dimensions={0} | all-to-all | bytes 65536 | tf_op jit(solution)/shard_map/cond/branch_1_fun/all_to_all | solution.py:725
  66.7 7.4 %conditional.16 = (f32[8,16,128]{2,1,0:T(8,128)S(1)}) conditional(s32[]{:T(128)} %convert_element_type.2, () %tuple.80, f32[8,16,128]{2,1,0:T(8,128)S(1)} %get-tuple-element.140), branch_computations={%region_10.0_spmd, %region_11.0_spmd} | conditional | bytes 131080 | solution.py:723
  66.7 7.4 %all_to_all.54 = f32[8,16,128]{2,1,0:T(8,128)S(1)} all-to-all(f32[8,16,128]{2,1,0:T(8,128)S(1)} %param.11), channel_id=1, replica_groups=mesh['areal'=8,'layer'=4] {'areal'}, dimensions={0} | all-to-all | bytes 131072 | tf_op jit(solution)/shard_map/cond/branch_1_fun/all_to_all | solution.py:725
  77.4 7.2 %conditional.17 = (f32[8,8,128]{2,1,0:T(8,128)S(1)}) conditional(s32[]{:T(128)} %convert_element_type.2, () %tuple.79, f32[8,8,128]{2,1,0:T(8,128)S(1)} %get-tuple-element.145), branch_computations={%region_12.0_spmd, %region_13.0_spmd} | conditional | bytes 65544 | solution.py:723
  77.4 7.2 %all_to_all.55 = f32[8,8,128]{2,1,0:T(8,128)S(1)} all-to-all(f32[8,8,128]{2,1,0:T(8,128)S(1)} %param.13), channel_id=1, replica_groups=mesh['areal'=8,'layer'=4] {'areal'}, dimensions={0} | all-to-all | bytes 65536 | tf_op jit(solution)/shard_map/cond/branch_1_fun/all_to_all | solution.py:725
  88.5 7.2 %conditional.18 = (f32[8,8,128]{2,1,0:T(8,128)S(1)}) conditional(s32[]{:T(128)} %convert_element_type.2, () %tuple.78, f32[8,8,128]{2,1,0:T(8,128)S(1)} %get-tuple-element.150), branch_computations={%region_14.0_spmd, %region_15.0_spmd} | conditional | bytes 65544 | solution.py:723
  88.5 7.2 %all_to_all.56 = f32[8,8,128]{2,1,0:T(8,128)S(1)} all-to-all(f32[8,8,128]{2,1,0:T(8,128)S(1)} %param.15), channel_id=1, replica_groups=mesh['areal'=8,'layer'=4] {'areal'}, dimensions={0} | all-to-all | bytes 65536 | tf_op jit(solution)/shard_map/cond/branch_1_fun/all_to_all | solution.py:725
  98.9 7.2 %conditional.19 = (f32[8,8,128]{2,1,0:T(8,128)S(1)}) conditional(s32[]{:T(128)} %convert_element_type.2, () %tuple.77, f32[8,8,128]{2,1,0:T(8,128)S(1)} %get-tuple-element.154), branch_computations={%region_16.0_spmd, %region_17.0_spmd} | conditional | bytes 65544 | solution.py:723
  98.9 7.2 %all_to_all.57 = f32[8,8,128]{2,1,0:T(8,128)S(1)} all-to-all(f32[8,8,128]{2,1,0:T(8,128)S(1)} %param.17), channel_id=1, replica_groups=mesh['areal'=8,'layer'=4] {'areal'}, dimensions={0} | all-to-all | bytes 65536 | tf_op jit(solution)/shard_map/cond/branch_1_fun/all_to_all | solution.py:725
  109.9 7.2 %conditional.20 = (f32[8,8,128]{2,1,0:T(8,128)S(1)}) conditional(s32[]{:T(128)} %convert_element_type.2, () %tuple.76, f32[8,8,128]{2,1,0:T(8,128)S(1)} %get-tuple-element.158), branch_computations={%region_18.0_spmd, %region_19.0_spmd} | conditional | bytes 65544 | solution.py:723
  109.9 7.2 %all_to_all.58 = f32[8,8,128]{2,1,0:T(8,128)S(1)} all-to-all(f32[8,8,128]{2,1,0:T(8,128)S(1)} %param.19), channel_id=1, replica_groups=mesh['areal'=8,'layer'=4] {'areal'}, dimensions={0} | all-to-all | bytes 65536 | tf_op jit(solution)/shard_map/cond/branch_1_fun/all_to_all | solution.py:725
  120.5 7.4 %conditional.21 = (f32[8,16,128]{2,1,0:T(8,128)S(1)}) conditional(s32[]{:T(128)} %convert_element_type.2, () %tuple.75, f32[8,16,128]{2,1,0:T(8,128)S(1)} %get-tuple-element.163), branch_computations={%region_20.0_spmd, %region_21.0_spmd} | conditional | bytes 131080 | solution.py:723
  120.5 7.4 %all_to_all.59 = f32[8,16,128]{2,1,0:T(8,128)S(1)} all-to-all(f32[8,16,128]{2,1,0:T(8,128)S(1)} %param.21), channel_id=1, replica_groups=mesh['areal'=8,'layer'=4] {'areal'}, dimensions={0} | all-to-all | bytes 131072 | tf_op jit(solution)/shard_map/cond/branch_1_fun/all_to_all | solution.py:725
  128.3 10.1 %all_to_all.60.sums_ref = f32[32,1,128]{2,1,0:T(1,128)S(1)} all-to-all(f32[32,1,128]{2,1,0:T(1,128)S(1)} %shard_map.142), channel_id=1, replica_groups=mesh['areal'=8,'layer'=4] {'areal','layer'}, dimensions={0} | all-to-all | bytes 32768 | tf_op jit(solution)/shard_map/all_to_all | solution.py:833
  (64 shorter events, 42.1 us)
Async XLA Ops:
  3.2 12.9 %collective-permute-start = (f32[5,16,128]{2,1,0:T(8,128)}, f32[5,16,128]{2,1,0:T(8,128)S(1)}, u32[]{:S(2)}, u32[]{:S(2)}) collective-permute-start(f32[5,16,128]{2,1,0:T(8,128)} %get-tuple-element.110), channel_id=1, source_target_pairs={{0,1},{1,0},{2,3},{3,2},{4,5},{5,4},{6,7},{7,6},{8,9},{9,8},{10,11... | collective-permute-start | bytes 122888 | tf_op jit(solution)/shard_map/ppermute | solution.py:718
  6.3 9.8 %collective-permute-start.1 = (f32[5,16,128]{2,1,0:T(8,128)}, f32[5,16,128]{2,1,0:T(8,128)S(1)}, u32[]{:S(2)}, u32[]{:S(2)}) collective-permute-start(f32[5,16,128]{2,1,0:T(8,128)} %get-tuple-element.111), channel_id=1, source_target_pairs={{1,2},{2,1},{5,6},{6,5},{9,10},{10,9},{13,14},{14,13},{17,18},{18,... | collective-permute-start | bytes 122888 | tf_op jit(solution)/shard_map/ppermute | solution.py:718
  7.0 9.1 %copy-start = (bf16[128,512]{1,0:T(8,128)(2,1)S(1)}, bf16[128,512]{1,0:T(8,128)(2,1)}, u32[]{:S(2)}) copy-start(bf16[128,512]{1,0:T(8,128)(2,1)} %get-tuple-element.114.col_ref) | copy-start | bytes 393220
  7.0 9.1 %copy-start.1 = (f32[64,512]{1,0:T(8,128)S(1)}, f32[64,512]{1,0:T(8,128)}, u32[]{:S(2)}) copy-start(f32[64,512]{1,0:T(8,128)} %get-tuple-element.115.row_ref) | copy-start | bytes 393220
  18.5 12.3 %collective-permute-start.2 = (f32[1,16,128]{2,1,0:T(8,128)S(1)}, f32[1,16,128]{2,1,0:T(8,128)S(1)}, u32[]{:S(2)}, u32[]{:S(2)}) collective-permute-start(f32[1,16,128]{2,1,0:T(8,128)S(1)} %get-tuple-element.118), channel_id=1, source_target_pairs={{0,1},{1,0},{2,3},{3,2},{4,5},{5,4},{6,7},{7,6},{8,9},{9,8},{10,11... | collective-permute-start | bytes 24584 | tf_op jit(solution)/shard_map/ppermute | solution.py:718
  23.0 7.9 %collective-permute-start.3 = (f32[1,16,128]{2,1,0:T(8,128)S(1)}, f32[1,16,128]{2,1,0:T(8,128)S(1)}, u32[]{:S(2)}, u32[]{:S(2)}) collective-permute-start(f32[1,16,128]{2,1,0:T(8,128)S(1)} %get-tuple-element.119), channel_id=1, source_target_pairs={{1,2},{2,1},{5,6},{6,5},{9,10},{10,9},{13,14},{14,13},{17,18},{18,... | collective-permute-start | bytes 24584 | tf_op jit(solution)/shard_map/ppermute | solution.py:718
  31.4 9.2 %collective-permute-start.4 = (f32[1,16,128]{2,1,0:T(8,128)S(1)}, f32[1,16,128]{2,1,0:T(8,128)S(1)}, u32[]{:S(2)}, u32[]{:S(2)}) collective-permute-start(f32[1,16,128]{2,1,0:T(8,128)S(1)} %get-tuple-element.126), channel_id=1, source_target_pairs={{0,1},{1,0},{2,3},{3,2},{4,5},{5,4},{6,7},{7,6},{8,9},{9,8},{10,11... | collective-permute-start | bytes 24584 | tf_op jit(solution)/shard_map/ppermute | solution.py:718
  32.7 7.9 %collective-permute-start.5 = (f32[1,16,128]{2,1,0:T(8,128)S(1)}, f32[1,16,128]{2,1,0:T(8,128)S(1)}, u32[]{:S(2)}, u32[]{:S(2)}) collective-permute-start(f32[1,16,128]{2,1,0:T(8,128)S(1)} %get-tuple-element.127), channel_id=1, source_target_pairs={{1,2},{2,1},{5,6},{6,5},{9,10},{10,9},{13,14},{14,13},{17,18},{18,... | collective-permute-start | bytes 24584 | tf_op jit(solution)/shard_map/ppermute | solution.py:718
  41.1 11.2 %collective-permute-start.6 = (f32[1,16,128]{2,1,0:T(8,128)S(1)}, f32[1,16,128]{2,1,0:T(8,128)S(1)}, u32[]{:S(2)}, u32[]{:S(2)}) collective-permute-start(f32[1,16,128]{2,1,0:T(8,128)S(1)} %get-tuple-element.130), channel_id=1, source_target_pairs={{0,1},{1,0},{2,3},{3,2},{4,5},{5,4},{6,7},{7,6},{8,9},{9,8},{10,11... | collective-permute-start | bytes 24584 | tf_op jit(solution)/shard_map/ppermute | solution.py:718
  44.4 7.9 %collective-permute-start.7 = (f32[1,16,128]{2,1,0:T(8,128)S(1)}, f32[1,16,128]{2,1,0:T(8,128)S(1)}, u32[]{:S(2)}, u32[]{:S(2)}) collective-permute-start(f32[1,16,128]{2,1,0:T(8,128)S(1)} %get-tuple-element.131), channel_id=1, source_target_pairs={{1,2},{2,1},{5,6},{6,5},{9,10},{10,9},{13,14},{14,13},{17,18},{18,... | collective-permute-start | bytes 24584 | tf_op jit(solution)/shard_map/ppermute | solution.py:718
  52.8 9.9 %collective-permute-start.8 = (f32[1,16,128]{2,1,0:T(8,128)S(1)}, f32[1,16,128]{2,1,0:T(8,128)S(1)}, u32[]{:S(2)}, u32[]{:S(2)}) collective-permute-start(f32[1,16,128]{2,1,0:T(8,128)S(1)} %get-tuple-element.135), channel_id=1, source_target_pairs={{0,1},{1,0},{2,3},{3,2},{4,5},{5,4},{6,7},{7,6},{8,9},{9,8},{10,11... | collective-permute-start | bytes 24584 | tf_op jit(solution)/shard_map/ppermute | solution.py:718
  54.9 7.9 %collective-permute-start.9 = (f32[1,16,128]{2,1,0:T(8,128)S(1)}, f32[1,16,128]{2,1,0:T(8,128)S(1)}, u32[]{:S(2)}, u32[]{:S(2)}) collective-permute-start(f32[1,16,128]{2,1,0:T(8,128)S(1)} %get-tuple-element.136), channel_id=1, source_target_pairs={{1,2},{2,1},{5,6},{6,5},{9,10},{10,9},{13,14},{14,13},{17,18},{18,... | collective-permute-start | bytes 24584 | tf_op jit(solution)/shard_map/ppermute | solution.py:718
  63.4 10.7 %collective-permute-start.10 = (f32[2,16,128]{2,1,0:T(8,128)S(1)}, f32[2,16,128]{2,1,0:T(8,128)S(1)}, u32[]{:S(2)}, u32[]{:S(2)}) collective-permute-start(f32[2,16,128]{2,1,0:T(8,128)S(1)} %get-tuple-element.141), channel_id=1, source_target_pairs={{0,1},{1,0},{2,3},{3,2},{4,5},{5,4},{6,7},{7,6},{8,9},{9,8},{10,11... | collective-permute-start | bytes 49160 | tf_op jit(solution)/shard_map/ppermute | solution.py:718
  66.0 8.1 %collective-permute-start.11 = (f32[2,16,128]{2,1,0:T(8,128)S(1)}, f32[2,16,128]{2,1,0:T(8,128)S(1)}, u32[]{:S(2)}, u32[]{:S(2)}) collective-permute-start(f32[2,16,128]{2,1,0:T(8,128)S(1)} %get-tuple-element.142), channel_id=1, source_target_pairs={{1,2},{2,1},{5,6},{6,5},{9,10},{10,9},{13,14},{14,13},{17,18},{18,... | collective-permute-start | bytes 49160 | tf_op jit(solution)/shard_map/ppermute | solution.py:718
  74.7 10.0 %collective-permute-start.12 = (f32[1,16,128]{2,1,0:T(8,128)S(1)}, f32[1,16,128]{2,1,0:T(8,128)S(1)}, u32[]{:S(2)}, u32[]{:S(2)}) collective-permute-start(f32[1,16,128]{2,1,0:T(8,128)S(1)} %get-tuple-element.146), channel_id=1, source_target_pairs={{0,1},{1,0},{2,3},{3,2},{4,5},{5,4},{6,7},{7,6},{8,9},{9,8},{10,11... | collective-permute-start | bytes 24584 | tf_op jit(solution)/shard_map/ppermute | solution.py:718
  76.8 7.9 %collective-permute-start.13 = (f32[1,16,128]{2,1,0:T(8,128)S(1)}, f32[1,16,128]{2,1,0:T(8,128)S(1)}, u32[]{:S(2)}, u32[]{:S(2)}) collective-permute-start(f32[1,16,128]{2,1,0:T(8,128)S(1)} %get-tuple-element.147), channel_id=1, source_target_pairs={{1,2},{2,1},{5,6},{6,5},{9,10},{10,9},{13,14},{14,13},{17,18},{18,... | collective-permute-start | bytes 24584 | tf_op jit(solution)/shard_map/ppermute | solution.py:718
  85.2 10.5 %collective-permute-start.14 = (f32[1,16,128]{2,1,0:T(8,128)S(1)}, f32[1,16,128]{2,1,0:T(8,128)S(1)}, u32[]{:S(2)}, u32[]{:S(2)}) collective-permute-start(f32[1,16,128]{2,1,0:T(8,128)S(1)} %get-tuple-element.151), channel_id=1, source_target_pairs={{0,1},{1,0},{2,3},{3,2},{4,5},{5,4},{6,7},{7,6},{8,9},{9,8},{10,11... | collective-permute-start | bytes 24584 | tf_op jit(solution)/shard_map/ppermute | solution.py:718
  87.8 7.9 %collective-permute-start.15 = (f32[1,16,128]{2,1,0:T(8,128)S(1)}, f32[1,16,128]{2,1,0:T(8,128)S(1)}, u32[]{:S(2)}, u32[]{:S(2)}) collective-permute-start(f32[1,16,128]{2,1,0:T(8,128)S(1)} %get-tuple-element.152), channel_id=1, source_target_pairs={{1,2},{2,1},{5,6},{6,5},{9,10},{10,9},{13,14},{14,13},{17,18},{18,... | collective-permute-start | bytes 24584 | tf_op jit(solution)/shard_map/ppermute | solution.py:718
  96.2 10.0 %collective-permute-start.16 = (f32[1,16,128]{2,1,0:T(8,128)S(1)}, f32[1,16,128]{2,1,0:T(8,128)S(1)}, u32[]{:S(2)}, u32[]{:S(2)}) collective-permute-start(f32[1,16,128]{2,1,0:T(8,128)S(1)} %get-tuple-element.155), channel_id=1, source_target_pairs={{0,1},{1,0},{2,3},{3,2},{4,5},{5,4},{6,7},{7,6},{8,9},{9,8},{10,11... | collective-permute-start | bytes 24584 | tf_op jit(solution)/shard_map/ppermute | solution.py:718
  98.2 7.9 %collective-permute-start.17 = (f32[1,16,128]{2,1,0:T(8,128)S(1)}, f32[1,16,128]{2,1,0:T(8,128)S(1)}, u32[]{:S(2)}, u32[]{:S(2)}) collective-permute-start(f32[1,16,128]{2,1,0:T(8,128)S(1)} %get-tuple-element.156), channel_id=1, source_target_pairs={{1,2},{2,1},{5,6},{6,5},{9,10},{10,9},{13,14},{14,13},{17,18},{18,... | collective-permute-start | bytes 24584 | tf_op jit(solution)/shard_map/ppermute | solution.py:718
  106.6 10.5 %collective-permute-start.18 = (f32[1,16,128]{2,1,0:T(8,128)S(1)}, f32[1,16,128]{2,1,0:T(8,128)S(1)}, u32[]{:S(2)}, u32[]{:S(2)}) collective-permute-start(f32[1,16,128]{2,1,0:T(8,128)S(1)} %get-tuple-element.159), channel_id=1, source_target_pairs={{0,1},{1,0},{2,3},{3,2},{4,5},{5,4},{6,7},{7,6},{8,9},{9,8},{10,11... | collective-permute-start | bytes 24584 | tf_op jit(solution)/shard_map/ppermute | solution.py:718
  109.3 7.9 %collective-permute-start.19 = (f32[1,16,128]{2,1,0:T(8,128)S(1)}, f32[1,16,128]{2,1,0:T(8,128)S(1)}, u32[]{:S(2)}, u32[]{:S(2)}) collective-permute-start(f32[1,16,128]{2,1,0:T(8,128)S(1)} %get-tuple-element.160), channel_id=1, source_target_pairs={{1,2},{2,1},{5,6},{6,5},{9,10},{10,9},{13,14},{14,13},{17,18},{18,... | collective-permute-start | bytes 24584 | tf_op jit(solution)/shard_map/ppermute | solution.py:718
  117.8 10.1 %collective-permute-start.20 = (f32[2,16,128]{2,1,0:T(8,128)S(1)}, f32[2,16,128]{2,1,0:T(8,128)S(1)}, u32[]{:S(2)}, u32[]{:S(2)}) collective-permute-start(f32[2,16,128]{2,1,0:T(8,128)S(1)} %get-tuple-element.164), channel_id=1, source_target_pairs={{0,1},{1,0},{2,3},{3,2},{4,5},{5,4},{6,7},{7,6},{8,9},{9,8},{10,11... | collective-permute-start | bytes 49160 | tf_op jit(solution)/shard_map/ppermute | solution.py:718
  119.8 8.1 %collective-permute-start.21 = (f32[2,16,128]{2,1,0:T(8,128)S(1)}, f32[2,16,128]{2,1,0:T(8,128)S(1)}, u32[]{:S(2)}, u32[]{:S(2)}) collective-permute-start(f32[2,16,128]{2,1,0:T(8,128)S(1)} %get-tuple-element.165), channel_id=1, source_target_pairs={{1,2},{2,1},{5,6},{6,5},{9,10},{10,9},{13,14},{14,13},{17,18},{18,... | collective-permute-start | bytes 49160 | tf_op jit(solution)/shard_map/ppermute | solution.py:718
  (2 other events, 10.1 us)
